TPU v7x, 32 devices: a whole 2x2x4 slice. The times are simulated.
32 devices in a mesh: fsdp: 16 (over z, y, core), tensor: 2 (over x).
Axes of the slice: x: 2, y: 2, z: 4, core: 2. Of those that a mesh axis runs over, the one named last changes fastest.
Arguments:
- tokens: bfloat16 [32, 1024, 1024], P('fsdp', 'tensor'), may hold values from -6 to 6
- cotangent: bfloat16 [32, 1024, 1024], P('fsdp', 'tensor'), may hold values from -8 to 8
- w_qkv: bfloat16 [1024, 3, 1024], P('fsdp', None, 'tensor'), may hold values from -0.1875 to 0.1875
- wo_t: bfloat16 [1024, 1024], P('fsdp', 'tensor'), may hold values from -1.5 to 1.5
- w_up: bfloat16 [1024, 4096], P('fsdp', 'tensor'), may hold values from -0.1875 to 0.1875
- w_down_t: bfloat16 [1024, 4096], P('fsdp', 'tensor'), may hold values from -0.09375 to 0.09375
- norm_gains: bfloat16 [1024, 2], P('fsdp'), may hold values from 0.5 to 1.5
- norm_shifts: bfloat16 [1024, 2], P('fsdp'), may hold values from -1.796875 to 1.796875
- qk_gains: bfloat16 [2, 64], replicated, may hold values from 0.5 to 1.5
Outputs:
- outputs: bfloat16 [32, 1024, 1024], P('fsdp', 'tensor')
- grad_tokens: float32 [32, 1024, 1024], P('fsdp', 'tensor')
- grad_w_qkv: float32 [1024, 3, 1024], P('fsdp', None, 'tensor')
- grad_wo_t: float32 [1024, 1024], P('fsdp', 'tensor')
- grad_w_up: float32 [1024, 4096], P('fsdp', 'tensor')
- grad_w_down_t: float32 [1024, 4096], P('fsdp', 'tensor')
- grad_norm_gains: float32 [1024, 2], P('fsdp')
- grad_norm_shifts: float32 [1024, 2], P('fsdp')
- grad_qk_gains: float32 [2, 64], replicated
All inputs are finite; a program needn't handle non-finite values.
Results may differ from a plain program's by a relative error of at most 0.015.
Values may be sent and summed in bfloat16 or wider, within the bound.
A program may use at most 256 MiB of HBM per device.

v0:
```python
import jax
import jax.numpy as jnp
from jax import lax
from jax.sharding import PartitionSpec as P

HD = 64


EPSILON = 1e-06


def norm_stats(value):
    center = value - jnp.mean(value, -1, keepdims=True)
    factor = lax.rsqrt(jnp.mean(center * center, -1, keepdims=True) + EPSILON)
    return (center * factor, factor)


def norm_back(grad_hat, normed, factor):
    return factor * (
        grad_hat
        - jnp.mean(grad_hat, -1, keepdims=True)
        - normed * jnp.mean(grad_hat * normed, -1, keepdims=True)
    )


def contract_rows(left, right):
    return lax.dot_general(
        left, right, (((0,), (0,)), ((), ())), preferred_element_type=jnp.float32
    )


def contract_cols(left, right):
    return lax.dot_general(
        left, right, (((1,), (1,)), ((), ())), preferred_element_type=jnp.float32
    )


def per_device(tokens, cotangent, w_qkv, wo_t, w_up, w_down_t, norm_gains, norm_shifts, qk_gains):
    local_rows = tokens.shape[1]
    width = tokens.shape[2]
    head_cols = w_qkv.shape[2]
    local_heads = head_cols // HD
    hidden_cols = w_up.shape[1]
    tensor_count = lax.axis_size("tensor")
    full_len = local_rows * tensor_count
    block = min(512, full_len)
    blocks = full_len // block
    gain_query = qk_gains[0].astype(jnp.float32)
    gain_keys = qk_gains[1].astype(jnp.float32)
    scale_query = HD ** (-0.5)

    def fetch():
        return (
            lax.all_gather(w_qkv, "fsdp", axis=0, tiled=True),
            lax.all_gather(wo_t, "fsdp", axis=0, tiled=True),
            lax.all_gather(w_up, "fsdp", axis=0, tiled=True),
            lax.all_gather(w_down_t, "fsdp", axis=0, tiled=True),
            lax.all_gather(norm_gains, "fsdp", axis=0, tiled=True),
            lax.all_gather(norm_shifts, "fsdp", axis=0, tiled=True),
        )

    def forward(weights, inputs):
        whole_qkv, whole_out, whole_up, whole_down, gains, shifts = weights
        gains = gains.astype(jnp.float32)
        shifts = shifts.astype(jnp.float32)
        flat_qkv = whole_qkv.reshape(width, 3 * head_cols)
        residual = inputs.astype(jnp.float32)
        first_hat, first_factor = norm_stats(residual)
        first = (first_hat * gains[:, 0] + shifts[:, 0]).astype(jnp.bfloat16)
        piece = lax.all_gather(first, "tensor", axis=0, tiled=True)
        first_full = piece
        joined = jnp.dot(piece, flat_qkv, preferred_element_type=jnp.float32)
        joined = joined.reshape(full_len, 3, local_heads, HD)
        query_hat, query_factor = norm_stats(joined[:, 0])
        keys_hat, keys_factor = norm_stats(joined[:, 1])
        query_n = (query_hat * gain_query * scale_query).astype(jnp.bfloat16)
        keys_n = (keys_hat * gain_keys).astype(jnp.bfloat16)
        values = joined[:, 2].astype(jnp.bfloat16)

        def attend(query_block):
            scores = jnp.einsum(
                "qhd,khd->hqk", query_block, keys_n, preferred_element_type=jnp.float32
            )
            largest = jnp.max(scores, -1, keepdims=True)
            exponent = jnp.exp(scores - largest)
            total_sum = jnp.sum(exponent, -1, keepdims=True)
            probs_low = (exponent / total_sum).astype(jnp.bfloat16)
            mixed_block = jnp.einsum(
                "hqk,khd->qhd", probs_low, values, preferred_element_type=jnp.float32
            )
            return (mixed_block.astype(jnp.bfloat16), (largest + jnp.log(total_sum))[..., 0])

        mixed, log_total = lax.map(attend, query_n.reshape(blocks, block, local_heads, HD))
        mixed = mixed.reshape(full_len, head_cols)
        middle = residual + lax.psum_scatter(
            contract_cols(mixed, whole_out), "tensor", scatter_dimension=0, tiled=True
        )
        second_hat, second_factor = norm_stats(middle)
        second = (second_hat * gains[:, 1] + shifts[:, 1]).astype(jnp.bfloat16)
        piece = lax.all_gather(second, "tensor", axis=0, tiled=True)
        hidden = jnp.dot(piece, whole_up, preferred_element_type=jnp.float32)
        active = jax.nn.gelu(hidden, approximate=False).astype(jnp.bfloat16)
        result = (
            middle
            + lax.psum_scatter(
                contract_cols(active, whole_down).astype(jnp.bfloat16),
                "tensor",
                scatter_dimension=0,
                tiled=True,
            ).astype(jnp.float32)
        ).astype(jnp.bfloat16)
        kept = (
            first_hat,
            first_factor,
            first_full,
            query_hat,
            query_factor,
            keys_hat,
            keys_factor,
            query_n,
            keys_n,
            values,
            mixed,
            log_total,
            second_hat,
            second_factor,
            piece,
            hidden,
            active,
        )
        return (kept, result)

    def backward(weights, kept, grad_out):
        whole_qkv, whole_out, whole_up, whole_down, gains, shifts = weights
        gains = gains.astype(jnp.float32)
        flat_qkv = whole_qkv.reshape(width, 3 * head_cols)
        (
            first_hat,
            first_factor,
            first_full,
            query_hat,
            query_factor,
            keys_hat,
            keys_factor,
            query_n,
            keys_n,
            values,
            mixed_keep,
            log_total,
            second_hat,
            second_factor,
            second_full,
            hidden,
            active,
        ) = kept
        piece = lax.all_gather(grad_out, "tensor", axis=0, tiled=True)
        grad_full = piece
        grad_active = jnp.dot(piece, whole_down, preferred_element_type=jnp.float32)
        grad_down = contract_rows(grad_full, active)
        unused_value, gelu_pull = jax.vjp(
            lambda value: jax.nn.gelu(value, approximate=False), hidden
        )
        grad_hidden = gelu_pull(grad_active)[0].astype(jnp.bfloat16)
        grad_up = contract_rows(second_full, grad_hidden)
        grad_second = lax.psum_scatter(
            contract_cols(grad_hidden, whole_up), "tensor", scatter_dimension=0, tiled=True
        )
        grad_middle = grad_out.astype(jnp.float32) + norm_back(
            grad_second * gains[:, 1], second_hat, second_factor
        )
        grad_branch = grad_middle.astype(jnp.bfloat16)
        piece = lax.all_gather(grad_branch, "tensor", axis=0, tiled=True)
        grad_mixed = jnp.dot(piece, whole_out, preferred_element_type=jnp.float32)
        grad_out_w = contract_rows(piece, mixed_keep)
        grad_mixed = grad_mixed.astype(jnp.bfloat16)
        grad_mixed = grad_mixed.reshape(blocks, block, local_heads, HD)

        def attend_back(carry, item):
            grad_keys_sum, grad_values_sum = carry
            query_block, grad_block, log_block = item
            scores = jnp.einsum(
                "qhd,khd->hqk", query_block, keys_n, preferred_element_type=jnp.float32
            )
            probs = jnp.exp(scores - log_block[..., None])
            grad_probs = jnp.einsum(
                "qhd,khd->hqk", grad_block, values, preferred_element_type=jnp.float32
            )
            delta = jnp.sum(probs * grad_probs, -1, keepdims=True)
            grad_scores = (probs * (grad_probs - delta)).astype(jnp.bfloat16)
            grad_query_block = jnp.einsum(
                "hqk,khd->qhd", grad_scores, keys_n, preferred_element_type=jnp.float32
            )
            grad_keys_sum = grad_keys_sum + jnp.einsum(
                "hqk,qhd->khd", grad_scores, query_block, preferred_element_type=jnp.float32
            )
            grad_values_sum = grad_values_sum + jnp.einsum(
                "hqk,qhd->khd",
                probs.astype(jnp.bfloat16),
                grad_block,
                preferred_element_type=jnp.float32,
            )
            return ((grad_keys_sum, grad_values_sum), grad_query_block)

        empty_heads = jnp.zeros((full_len, local_heads, HD), jnp.float32)
        (grad_keys_n, grad_values), grad_query_n = lax.scan(
            attend_back,
            (empty_heads, empty_heads),
            (query_n.reshape(blocks, block, local_heads, HD), grad_mixed, log_total),
        )
        grad_query_n = grad_query_n.reshape(full_len, local_heads, HD)
        grad_query = norm_back(grad_query_n * gain_query * scale_query, query_hat, query_factor)
        grad_keys = norm_back(grad_keys_n * gain_keys, keys_hat, keys_factor)
        qk_grad = jnp.stack(
            [
                jnp.sum(grad_query_n * query_hat * scale_query, (0, 1)),
                jnp.sum(grad_keys_n * keys_hat, (0, 1)),
            ]
        )
        grad_joined = jnp.stack([grad_query, grad_keys, grad_values], 1).astype(jnp.bfloat16)
        grad_joined = grad_joined.reshape(full_len, 3 * head_cols)
        grad_qkv = contract_rows(first_full, grad_joined).reshape(width, 3, head_cols)
        grad_first = lax.psum_scatter(
            contract_cols(grad_joined, flat_qkv).astype(jnp.bfloat16),
            "tensor",
            scatter_dimension=0,
            tiled=True,
        ).astype(jnp.float32)
        grad_input = grad_middle + norm_back(grad_first * gains[:, 0], first_hat, first_factor)
        gain_grad = jnp.stack(
            [jnp.sum(grad_first * first_hat, 0), jnp.sum(grad_second * second_hat, 0)], 1
        )
        shift_grad = jnp.stack([jnp.sum(grad_first, 0), jnp.sum(grad_second, 0)], 1)
        return (
            (grad_qkv, grad_out_w, grad_up, grad_down, gain_grad, shift_grad, qk_grad),
            grad_input,
        )

    def micro_step(totals, item):
        inputs, grad_out = item
        forward_weights = fetch()
        kept, result = forward(forward_weights, inputs)
        backward_weights = fetch()
        grads, grad_input = backward(backward_weights, kept, grad_out)
        totals = tuple((total + part for total, part in zip(totals, grads)))
        return (totals, (result, grad_input))

    out_cols_count = wo_t.shape[1]
    start_sums = (
        jnp.zeros((width, 3, head_cols), jnp.float32),
        jnp.zeros((width, out_cols_count), jnp.float32),
        jnp.zeros((width, hidden_cols), jnp.float32),
        jnp.zeros((width, hidden_cols), jnp.float32),
        jnp.zeros((width, 2), jnp.float32),
        jnp.zeros((width, 2), jnp.float32),
        jnp.zeros((2, HD), jnp.float32),
    )
    totals, (outputs, grad_tokens) = lax.scan(micro_step, start_sums, (tokens, cotangent))
    out_total = totals[1]
    grad_qkv, grad_out_w, grad_up, grad_down = (
        lax.psum_scatter(
            totals[0].astype(jnp.bfloat16), "fsdp", scatter_dimension=0, tiled=True
        ).astype(jnp.float32),
        lax.psum_scatter(
            out_total.astype(jnp.bfloat16), "fsdp", scatter_dimension=0, tiled=True
        ).astype(jnp.float32),
        lax.psum_scatter(
            totals[2].astype(jnp.bfloat16), "fsdp", scatter_dimension=0, tiled=True
        ).astype(jnp.float32),
        lax.psum_scatter(
            totals[3].astype(jnp.bfloat16), "fsdp", scatter_dimension=0, tiled=True
        ).astype(jnp.float32),
    )
    gain_total, shift_total, qk_total = lax.psum(
        (totals[4], totals[5], totals[6]), ("fsdp", "tensor")
    )
    own_rows = width // lax.axis_size("fsdp")
    offset = lax.axis_index("fsdp") * own_rows
    gain_part = lax.dynamic_slice_in_dim(gain_total, offset, own_rows, 0)
    shift_part = lax.dynamic_slice_in_dim(shift_total, offset, own_rows, 0)
    return (
        outputs,
        grad_tokens,
        grad_qkv,
        grad_out_w,
        grad_up,
        grad_down,
        gain_part,
        shift_part,
        qk_total,
    )


def solution(mesh):
    in_specs = (
        P("fsdp", "tensor", None),
        P("fsdp", "tensor", None),
        P("fsdp", None, "tensor"),
        P("fsdp", "tensor"),
        P("fsdp", "tensor"),
        P("fsdp", "tensor"),
        P("fsdp", None),
        P("fsdp", None),
        P(),
    )
    out_specs = (
        P("fsdp", "tensor", None),
        P("fsdp", "tensor", None),
        P("fsdp", None, "tensor"),
        P("fsdp", "tensor"),
        P("fsdp", "tensor"),
        P("fsdp", "tensor"),
        P("fsdp", None),
        P("fsdp", None),
        P(),
    )
    return jax.shard_map(
        per_device, mesh=mesh, in_specs=in_specs, out_specs=out_specs, check_vma=False
    )
```

profile of v0, /device:TPU:0, one launch (start us, length us, event | category | flops | bytes accessed | tf_op | source)
XLA Modules:
  0.0 1565.1 jit_solution(4395496500692842202)
XLA Ops:
  8.8 1264.8 %while.58 = (s32[]{:T(128)}, f32[1024,3,512]{2,0,1:T(8,128)}, f32[1024,512]{1,0:T(8,128)}, f32[1024,2048]{1,0:T(8,128)}, f32[1024,2048]{1,0:T(8,128)}, /*index=5...) while((s32[]{:T(128)}, f32[1024,3,512]{2,0,1:T(8,128)}, ...), condition=%wide.region_34.35_spmd.clone, body=%wide.region_0.34_spmd.clone.sunk | while | flops 42723983360 | bytes 958744064 | solution.py:257
  9.6 23.2 %all-gather.10 = bf16[16,64,2]{1,2,0:T(2,128)(2,1)S(1)} all-gather(bf16[1,64,2]{1,2,0:T(2,128)(2,1)} %bitcast.385), channel_id=1, replica_groups=mesh['fsdp'=16,'tensor'=2] {'fsdp'}, dimensions={0}, use_global_device_ids=true | all-gather | bytes 4352 | tf_op jit(solution)/shard_map/while/body/eval_jaxpr/all_gather | solution.py:58
  32.9 17.5 %all-gather.9 = bf16[16,64,2]{1,2,0:T(2,128)(2,1)S(1)} all-gather(bf16[1,64,2]{1,2,0:T(2,128)(2,1)} %bitcast.386), channel_id=1, replica_groups=mesh['fsdp'=16,'tensor'=2] {'fsdp'}, dimensions={0}, use_global_device_ids=true | all-gather | bytes 4352 | tf_op jit(solution)/shard_map/while/body/eval_jaxpr/all_gather | solution.py:59
  63.3 30.4 %all-gather.23.cloned.1.call-done = bf16[1024,1024]{1,0:T(8,128)(2,1)} async-done(((bf16[512,1024]{1,0:T(8,128)(2,1)}), bf16[1024,1024]{1,0:T(8,128)(2,1)}) %all-gather.23.cloned.1.call-update) | async-done | bytes 2097168 | tf_op jit(solution)/shard_map/while/body/eval_jaxpr/all_gather | solution.py:70
  110.8 22.3 %while.59 = (s32[]{:T(128)}, bf16[2,512,8,64]{1,3,2,0:T(8,128)(2,1)}, f32[2,8,512]{2,1,0:T(8,128)S(1)}, bf16[2,512,8,64]{1,3,2,0:T(8,128)(2,1)S(1)}, bf16[1024,8...) while((s32[]{:T(128)}, bf16[2,512,8,64]{1,3,2,0:T(8,128)(2,1)}, ...), condition=%wide.region_10.10_spmd, body=%wide.region_7.9_spmd.sunk | while | flops 1099165696 | bytes 66191540 | solution.py:93
  142.1 53.8 %reduce-scatter.17.cloned.1.call-done = f32[512,1024]{1,0:T(8,128)} async-done(((f32[1024,1024]{1,0:T(8,128)}), f32[512,1024]{1,0:T(8,128)}) %reduce-scatter.17.cloned.1.call-update) | async-done | bytes 2097168 | tf_op jit(solution)/shard_map/while/body/eval_jaxpr/reduce_scatter | solution.py:95
  204.0 44.6 %all-gather.29.cloned.1.call-done = bf16[1024,2048]{1,0:T(8,128)(2,1)} async-done(((bf16[64,2048]{1,0:T(8,128)(2,1)}), bf16[1024,2048]{1,0:T(8,128)(2,1)}) %all-gather.29.cloned.1.call-update) | async-done | bytes 4194320 | tf_op jit(solution)/shard_map/while/body/eval_jaxpr/all_gather | solution.py:56
  248.5 33.0 %all-gather.27.cloned.1.call-done = bf16[1024,1024]{1,0:T(8,128)(2,1)} async-done(((bf16[512,1024]{1,0:T(8,128)(2,1)}), bf16[1024,1024]{1,0:T(8,128)(2,1)}) %all-gather.27.cloned.1.call-update) | async-done | bytes 2097168 | tf_op jit(solution)/shard_map/while/body/eval_jaxpr/all_gather | solution.py:100
  281.6 26.0 %multiply_convert_fusion.10 = (bf16[1024,2048]{1,0:T(8,128)(2,1)}, f32[1024,2048]{1,0:T(8,128)}, f32[1024,2048]{1,0:T(8,128)}) fusion(bf16[1024,1024]{1,0:T(8,128)(2,1)} %all-gather.27.cloned.1.call-done, bf16[1024,2048]{1,0:T(8,128)(2,1)} %all-gather.29.cloned.1.call-done), kind=kOutput, calls=%fused_computation.41.clone.1 | convolution fusion | flops 4431282176 | bytes 27262976 | tf_op jit(solution)/shard_map/while/body/eval_jaxpr/dot_general | solution.py:101
  307.6 8.7 all-gather.33.cloned.1.call-done
  316.3 52.8 %all-gather.31.cloned.1.call-done = bf16[1024,2048]{1,0:T(8,128)(2,1)} async-done(((bf16[64,2048]{1,0:T(8,128)(2,1)}), bf16[1024,2048]{1,0:T(8,128)(2,1)}) %all-gather.31.cloned.1.call-update) | async-done | bytes 4194320 | tf_op jit(solution)/shard_map/while/body/eval_jaxpr/all_gather | solution.py:57
  369.0 12.7 add_convert_fusion.6
  390.0 52.9 %reduce-scatter.19.cloned.1.call-done = f32[512,1024]{1,0:T(8,128)} async-done(((f32[1024,1024]{1,0:T(8,128)}), f32[512,1024]{1,0:T(8,128)}) %reduce-scatter.19.cloned.1.call-update) | async-done | bytes 2097168 | tf_op jit(solution)/shard_map/while/body/eval_jaxpr/reduce_scatter | solution.py:165
  450.8 9.3 convolution_convert_fusion.8
  460.2 23.6 %all-gather.35.cloned.1.call-done = bf16[1024,1024]{1,0:T(8,128)(2,1)} async-done(((bf16[512,1024]{1,0:T(8,128)(2,1)}), bf16[1024,1024]{1,0:T(8,128)(2,1)}) %all-gather.35.cloned.1.call-update) | async-done | bytes 2097168 | tf_op jit(solution)/shard_map/while/body/eval_jaxpr/all_gather | solution.py:172
  495.3 78.1 %while.60 = (s32[]{:T(128)}, f32[1024,8,64]{0,2,1:T(8,128)}, f32[1024,8,64]{0,2,1:T(8,128)}, f32[2,512,8,64]{1,3,2,0:T(8,128)}, bf16[2,512,8,64]{1,3,2,0:T(8,128...) while((s32[]{:T(128)}, f32[1024,8,64]{0,2,1:T(8,128)}, ...), condition=%wide.region_19.19_spmd.clone, body=%wide.region_17.18_spmd.clone.sunk | while | flops 2724196352 | bytes 195150096 | solution.py:205
  501.8 9.4 multiply_reduce_fusion.22
  511.3 7.8 multiply_convert_fusion.11
  540.5 9.4 multiply_reduce_fusion.22
  550.0 7.7 multiply_convert_fusion.11
  602.4 9.3 select_add_fusion.10
  611.6 7.5 select_add_fusion.11
  639.7 21.4 %all-gather.10 = bf16[16,64,2]{1,2,0:T(2,128)(2,1)S(1)} all-gather(bf16[1,64,2]{1,2,0:T(2,128)(2,1)} %bitcast.385), channel_id=1, replica_groups=mesh['fsdp'=16,'tensor'=2] {'fsdp'}, dimensions={0}, use_global_device_ids=true | all-gather | bytes 4352 | tf_op jit(solution)/shard_map/while/body/eval_jaxpr/all_gather | solution.py:58
  661.2 17.5 %all-gather.9 = bf16[16,64,2]{1,2,0:T(2,128)(2,1)S(1)} all-gather(bf16[1,64,2]{1,2,0:T(2,128)(2,1)} %bitcast.386), channel_id=1, replica_groups=mesh['fsdp'=16,'tensor'=2] {'fsdp'}, dimensions={0}, use_global_device_ids=true | all-gather | bytes 4352 | tf_op jit(solution)/shard_map/while/body/eval_jaxpr/all_gather | solution.py:59
  690.6 30.2 %all-gather.23.cloned.1.call-done = bf16[1024,1024]{1,0:T(8,128)(2,1)} async-done(((bf16[512,1024]{1,0:T(8,128)(2,1)}), bf16[1024,1024]{1,0:T(8,128)(2,1)}) %all-gather.23.cloned.1.call-update) | async-done | bytes 2097168 | tf_op jit(solution)/shard_map/while/body/eval_jaxpr/all_gather | solution.py:70
  738.0 22.1 %while.59 = (s32[]{:T(128)}, bf16[2,512,8,64]{1,3,2,0:T(8,128)(2,1)}, f32[2,8,512]{2,1,0:T(8,128)S(1)}, bf16[2,512,8,64]{1,3,2,0:T(8,128)(2,1)S(1)}, bf16[1024,8...) while((s32[]{:T(128)}, bf16[2,512,8,64]{1,3,2,0:T(8,128)(2,1)}, ...), condition=%wide.region_10.10_spmd, body=%wide.region_7.9_spmd.sunk | while | flops 1099165696 | bytes 66191540 | solution.py:93
  769.2 53.8 %reduce-scatter.17.cloned.1.call-done = f32[512,1024]{1,0:T(8,128)} async-done(((f32[1024,1024]{1,0:T(8,128)}), f32[512,1024]{1,0:T(8,128)}) %reduce-scatter.17.cloned.1.call-update) | async-done | bytes 2097168 | tf_op jit(solution)/shard_map/while/body/eval_jaxpr/reduce_scatter | solution.py:95
  830.8 44.7 %all-gather.29.cloned.1.call-done = bf16[1024,2048]{1,0:T(8,128)(2,1)} async-done(((bf16[64,2048]{1,0:T(8,128)(2,1)}), bf16[1024,2048]{1,0:T(8,128)(2,1)}) %all-gather.29.cloned.1.call-update) | async-done | bytes 4194320 | tf_op jit(solution)/shard_map/while/body/eval_jaxpr/all_gather | solution.py:56
  875.6 33.0 %all-gather.27.cloned.1.call-done = bf16[1024,1024]{1,0:T(8,128)(2,1)} async-done(((bf16[512,1024]{1,0:T(8,128)(2,1)}), bf16[1024,1024]{1,0:T(8,128)(2,1)}) %all-gather.27.cloned.1.call-update) | async-done | bytes 2097168 | tf_op jit(solution)/shard_map/while/body/eval_jaxpr/all_gather | solution.py:100
  908.6 26.0 %multiply_convert_fusion.10 = (bf16[1024,2048]{1,0:T(8,128)(2,1)}, f32[1024,2048]{1,0:T(8,128)}, f32[1024,2048]{1,0:T(8,128)}) fusion(bf16[1024,1024]{1,0:T(8,128)(2,1)} %all-gather.27.cloned.1.call-done, bf16[1024,2048]{1,0:T(8,128)(2,1)} %all-gather.29.cloned.1.call-done), kind=kOutput, calls=%fused_computation.41.clone.1 | convolution fusion | flops 4431282176 | bytes 27262976 | tf_op jit(solution)/shard_map/while/body/eval_jaxpr/dot_general | solution.py:101
  934.6 8.7 all-gather.33.cloned.1.call-done
  943.3 52.6 %all-gather.31.cloned.1.call-done = bf16[1024,2048]{1,0:T(8,128)(2,1)} async-done(((bf16[64,2048]{1,0:T(8,128)(2,1)}), bf16[1024,2048]{1,0:T(8,128)(2,1)}) %all-gather.31.cloned.1.call-update) | async-done | bytes 4194320 | tf_op jit(solution)/shard_map/while/body/eval_jaxpr/all_gather | solution.py:57
  995.9 12.8 add_convert_fusion.6
  1016.9 52.9 %reduce-scatter.19.cloned.1.call-done = f32[512,1024]{1,0:T(8,128)} async-done(((f32[1024,1024]{1,0:T(8,128)}), f32[512,1024]{1,0:T(8,128)}) %reduce-scatter.19.cloned.1.call-update) | async-done | bytes 2097168 | tf_op jit(solution)/shard_map/while/body/eval_jaxpr/reduce_scatter | solution.py:165
  1077.6 9.3 convolution_convert_fusion.8
  1087.0 23.6 %all-gather.35.cloned.1.call-done = bf16[1024,1024]{1,0:T(8,128)(2,1)} async-done(((bf16[512,1024]{1,0:T(8,128)(2,1)}), bf16[1024,1024]{1,0:T(8,128)(2,1)}) %all-gather.35.cloned.1.call-update) | async-done | bytes 2097168 | tf_op jit(solution)/shard_map/while/body/eval_jaxpr/all_gather | solution.py:172
  1122.2 78.1 %while.60 = (s32[]{:T(128)}, f32[1024,8,64]{0,2,1:T(8,128)}, f32[1024,8,64]{0,2,1:T(8,128)}, f32[2,512,8,64]{1,3,2,0:T(8,128)}, bf16[2,512,8,64]{1,3,2,0:T(8,128...) while((s32[]{:T(128)}, f32[1024,8,64]{0,2,1:T(8,128)}, ...), condition=%wide.region_19.19_spmd.clone, body=%wide.region_17.18_spmd.clone.sunk | while | flops 2724196352 | bytes 195150096 | solution.py:205
  1128.7 9.4 multiply_reduce_fusion.22
  1138.1 7.8 multiply_convert_fusion.11
  1167.4 9.4 multiply_reduce_fusion.22
  1176.8 7.7 multiply_convert_fusion.11
  1229.2 10.5 select_add_fusion.10
  1239.7 9.8 select_add_fusion.11
  1257.2 7.5 select_add_fusion.8
  1294.4 39.9 %all-reduce = (f32[1024,2]{0,1:T(2,128)S(1)}, f32[1024,2]{0,1:T(2,128)S(1)}, f32[2,64]{1,0:T(2,128)}) all-reduce(f32[1024,2]{0,1:T(2,128)S(1)} %copy-done.47, f32[1024,2]{0,1:T(2,128)S(1)} %copy-done.44, f32[2,64]{1,0:T(2,128)S(1)} %copy-done.54), channel_id=1, replica_groups=mesh['fsdp'=16,'tensor'=2] {'fsdp','tensor'}, use_global_device_ids=true, to_apply=%region_39.40 | all-reduce | flops 4224 | bytes 33792 | tf_op jit(solution)/shard_map/psum | solution.py:273
  1336.9 67.8 %reduce-scatter.9.cloned.1.call-done = bf16[64,3,512]{2,0,1:T(8,128)(2,1)} async-done(((bf16[1024,3,512]{2,0,1:T(8,128)(2,1)}), bf16[64,3,512]{2,0,1:T(8,128)(2,1)}) %reduce-scatter.9.cloned.1.call-update) | async-done | bytes 196624 | tf_op jit(solution)/shard_map/reduce_scatter | solution.py:260
  1406.4 73.9 %reduce-scatter.13.cloned.1.call-done = bf16[64,2048]{1,0:T(8,128)(2,1)} async-done(((bf16[1024,2048]{1,0:T(8,128)(2,1)}), bf16[64,2048]{1,0:T(8,128)(2,1)}) %reduce-scatter.13.cloned.1.call-update) | async-done | bytes 262160 | tf_op jit(solution)/shard_map/reduce_scatter | solution.py:266
  1482.1 73.5 %reduce-scatter.15.cloned.1.call-done = bf16[64,2048]{1,0:T(8,128)(2,1)} async-done(((bf16[1024,2048]{1,0:T(8,128)(2,1)}), bf16[64,2048]{1,0:T(8,128)(2,1)}) %reduce-scatter.15.cloned.1.call-update) | async-done | bytes 262160 | tf_op jit(solution)/shard_map/reduce_scatter | solution.py:269
  (525 shorter events, 399.0 us)
Async XLA Ops:
  8.8 99.2 %copy-start.48 = (f32[64]{0:T(128)}, f32[64]{0:T(128)S(1)}, u32[]{:S(2)}) copy-start(f32[64]{0:T(128)S(1)} %get-tuple-element.968) | copy-start | bytes 772 | tf_op jit(solution)/shard_map/while
  8.8 101.4 %copy-start.50 = (f32[64]{0:T(128)}, f32[64]{0:T(128)S(1)}, u32[]{:S(2)}) copy-start(f32[64]{0:T(128)S(1)} %get-tuple-element.966) | copy-start | bytes 772 | tf_op jit(solution)/shard_map/while
  8.8 46.0 %copy-start.8 = (bf16[2,512,1024]{2,1,0:T(8,128)(2,1)S(1)}, bf16[2,512,1024]{2,1,0:T(8,128)(2,1)}, u32[]{:S(2)}) copy-start(bf16[2,512,1024]{2,1,0:T(8,128)(2,1)} %get-tuple-element.962) | copy-start | bytes 6291460 | tf_op jit(solution)/shard_map/while
  8.8 51.2 %all-gather.21.cloned.1.call-start = ((), (), s32[]{:S(2)}) async-start(), calls=%async_computation.12 | async-start | bytes 3342336 | tf_op jit(solution)/shard_map/while/body/eval_jaxpr/all_gather | solution.py:54
  9.6 84.1 %all-gather.23.cloned.1.call-start = ((), (), s32[]{:S(2)}) async-start(), calls=%async_computation.13 | async-start | bytes 3145728 | tf_op jit(solution)/shard_map/while/body/eval_jaxpr/all_gather | solution.py:70
  56.3 80.4 %all-gather.25.cloned.1.call-start = ((), (), s32[]{:S(2)}) async-start(), calls=%async_computation.14 | async-start | bytes 1114112 | tf_op jit(solution)/shard_map/while/body/eval_jaxpr/all_gather | solution.py:55
  57.0 138.9 %reduce-scatter.17.cloned.1.call-start = ((), (), s32[]{:S(2)}) async-start(), calls=%async_computation.15 | async-start | bytes 6291456 | tf_op jit(solution)/shard_map/while/body/eval_jaxpr/reduce_scatter | solution.py:95
  63.3 35.5 %copy-start.17 = (bf16[1024,3,512]{0,2,1:T(8,128)(2,1)}, bf16[1024,3,512]{0,2,1:T(8,128)(2,1)S(1)}, u32[]{:S(2)}) copy-start(bf16[1024,3,512]{0,2,1:T(8,128)(2,1)S(1)} %copy.88) | copy-start | bytes 9437188 | tf_op jit(solution)/shard_map/while
  141.5 107.1 %all-gather.29.cloned.1.call-start = ((), (), s32[]{:S(2)}) async-start(), calls=%async_computation.17 | async-start | bytes 4456448 | tf_op jit(solution)/shard_map/while/body/eval_jaxpr/all_gather | solution.py:56
  142.1 139.5 %all-gather.27.cloned.1.call-start = ((), (), s32[]{:S(2)}) async-start(), calls=%async_computation.16 | async-start | bytes 3145728 | tf_op jit(solution)/shard_map/while/body/eval_jaxpr/all_gather | solution.py:100
  200.8 115.5 %all-gather.33.cloned.1.call-start = ((), (), s32[]{:S(2)}) async-start(), calls=%async_computation.19 | async-start | bytes 3145728 | tf_op jit(solution)/shard_map/while/body/eval_jaxpr/all_gather | solution.py:156
  203.2 165.9 %all-gather.31.cloned.1.call-start = ((), (), s32[]{:S(2)}) async-start(), calls=%async_computation.18 | async-start | bytes 4456448 | tf_op jit(solution)/shard_map/while/body/eval_jaxpr/all_gather | solution.py:57
  203.9 239.0 %reduce-scatter.19.cloned.1.call-start = ((), (), s32[]{:S(2)}) async-start(), calls=%async_computation.20 | async-start | bytes 6291456 | tf_op jit(solution)/shard_map/while/body/eval_jaxpr/reduce_scatter | solution.py:165
  369.0 14.8 copy-start.55
  390.0 93.8 %all-gather.35.cloned.1.call-start = ((), (), s32[]{:S(2)}) async-start(), calls=%async_computation.21 | async-start | bytes 3145728 | tf_op jit(solution)/shard_map/while/body/eval_jaxpr/all_gather | solution.py:172
  450.5 168.6 %reduce-scatter.23.cloned.1.call-start = ((), (), s32[]{:S(2)}) async-start(), calls=%async_computation.23 | async-start | bytes 3145728 | tf_op jit(solution)/shard_map/while/body/eval_jaxpr/reduce_scatter | solution.py:105
  460.1 172.7 %reduce-scatter.21.cloned.1.call-start = ((), (), s32[]{:S(2)}) async-start(), calls=%async_computation.22 | async-start | bytes 3145728 | tf_op jit(solution)/shard_map/while/body/eval_jaxpr/reduce_scatter | solution.py:222
  578.0 11.0 slice-start
  602.4 9.3 copy-start.58
  602.4 9.3 copy-start.59
  638.9 96.4 %copy-start.48 = (f32[64]{0:T(128)}, f32[64]{0:T(128)S(1)}, u32[]{:S(2)}) copy-start(f32[64]{0:T(128)S(1)} %get-tuple-element.968) | copy-start | bytes 772 | tf_op jit(solution)/shard_map/while
  638.9 98.5 %copy-start.50 = (f32[64]{0:T(128)}, f32[64]{0:T(128)S(1)}, u32[]{:S(2)}) copy-start(f32[64]{0:T(128)S(1)} %get-tuple-element.966) | copy-start | bytes 772 | tf_op jit(solution)/shard_map/while
  638.9 44.2 %copy-start.8 = (bf16[2,512,1024]{2,1,0:T(8,128)(2,1)S(1)}, bf16[2,512,1024]{2,1,0:T(8,128)(2,1)}, u32[]{:S(2)}) copy-start(bf16[2,512,1024]{2,1,0:T(8,128)(2,1)} %get-tuple-element.962) | copy-start | bytes 6291460 | tf_op jit(solution)/shard_map/while
  638.9 48.6 %all-gather.21.cloned.1.call-start = ((), (), s32[]{:S(2)}) async-start(), calls=%async_computation.12 | async-start | bytes 3342336 | tf_op jit(solution)/shard_map/while/body/eval_jaxpr/all_gather | solution.py:54
  639.6 81.2 %all-gather.23.cloned.1.call-start = ((), (), s32[]{:S(2)}) async-start(), calls=%async_computation.13 | async-start | bytes 3145728 | tf_op jit(solution)/shard_map/while/body/eval_jaxpr/all_gather | solution.py:70
  684.5 79.2 %all-gather.25.cloned.1.call-start = ((), (), s32[]{:S(2)}) async-start(), calls=%async_computation.14 | async-start | bytes 1114112 | tf_op jit(solution)/shard_map/while/body/eval_jaxpr/all_gather | solution.py:55
  685.1 137.9 %reduce-scatter.17.cloned.1.call-start = ((), (), s32[]{:S(2)}) async-start(), calls=%async_computation.15 | async-start | bytes 6291456 | tf_op jit(solution)/shard_map/while/body/eval_jaxpr/reduce_scatter | solution.py:95
  690.6 35.4 %copy-start.17 = (bf16[1024,3,512]{0,2,1:T(8,128)(2,1)}, bf16[1024,3,512]{0,2,1:T(8,128)(2,1)S(1)}, u32[]{:S(2)}) copy-start(bf16[1024,3,512]{0,2,1:T(8,128)(2,1)S(1)} %copy.88) | copy-start | bytes 9437188 | tf_op jit(solution)/shard_map/while
  768.5 107.1 %all-gather.29.cloned.1.call-start = ((), (), s32[]{:S(2)}) async-start(), calls=%async_computation.17 | async-start | bytes 4456448 | tf_op jit(solution)/shard_map/while/body/eval_jaxpr/all_gather | solution.py:56
  769.1 139.5 %all-gather.27.cloned.1.call-start = ((), (), s32[]{:S(2)}) async-start(), calls=%async_computation.16 | async-start | bytes 3145728 | tf_op jit(solution)/shard_map/while/body/eval_jaxpr/all_gather | solution.py:100
  827.8 115.5 %all-gather.33.cloned.1.call-start = ((), (), s32[]{:S(2)}) async-start(), calls=%async_computation.19 | async-start | bytes 3145728 | tf_op jit(solution)/shard_map/while/body/eval_jaxpr/all_gather | solution.py:156
  830.2 165.7 %all-gather.31.cloned.1.call-start = ((), (), s32[]{:S(2)}) async-start(), calls=%async_computation.18 | async-start | bytes 4456448 | tf_op jit(solution)/shard_map/while/body/eval_jaxpr/all_gather | solution.py:57
  830.8 239.0 %reduce-scatter.19.cloned.1.call-start = ((), (), s32[]{:S(2)}) async-start(), calls=%async_computation.20 | async-start | bytes 6291456 | tf_op jit(solution)/shard_map/while/body/eval_jaxpr/reduce_scatter | solution.py:165
  995.9 14.8 copy-start.55
  1016.9 93.8 %all-gather.35.cloned.1.call-start = ((), (), s32[]{:S(2)}) async-start(), calls=%async_computation.21 | async-start | bytes 3145728 | tf_op jit(solution)/shard_map/while/body/eval_jaxpr/all_gather | solution.py:172
  1077.4 172.2 %reduce-scatter.23.cloned.1.call-start = ((), (), s32[]{:S(2)}) async-start(), calls=%async_computation.23 | async-start | bytes 3145728 | tf_op jit(solution)/shard_map/while/body/eval_jaxpr/reduce_scatter | solution.py:105
  1087.0 177.8 %reduce-scatter.21.cloned.1.call-start = ((), (), s32[]{:S(2)}) async-start(), calls=%async_computation.22 | async-start | bytes 3145728 | tf_op jit(solution)/shard_map/while/body/eval_jaxpr/reduce_scatter | solution.py:222
  1204.9 11.0 slice-start
  1229.2 10.5 copy-start.58
  1229.2 10.5 copy-start.59
  1239.7 9.8 copy-start.3
  1257.2 7.6 copy-start.34
  1257.2 7.6 copy-start.36
  1257.2 7.6 copy-start.38
  1273.6 61.8 %reduce-scatter.11.cloned.1.call-start = ((), (), s32[]{:S(2)}) async-start(), calls=%async_computation.9 | async-start | bytes 1114112 | tf_op jit(solution)/shard_map/reduce_scatter | solution.py:263
  1276.4 128.3 %reduce-scatter.9.cloned.1.call-start = ((), (), s32[]{:S(2)}) async-start(), calls=%async_computation.8 | async-start | bytes 3342336 | tf_op jit(solution)/shard_map/reduce_scatter | solution.py:260
  1281.3 199.0 %reduce-scatter.13.cloned.1.call-start = ((), (), s32[]{:S(2)}) async-start(), calls=%async_computation.10 | async-start | bytes 4456448 | tf_op jit(solution)/shard_map/reduce_scatter | solution.py:266
  1287.5 268.1 %reduce-scatter.15.cloned.1.call-start = ((), (), s32[]{:S(2)}) async-start(), calls=%async_computation.11 | async-start | bytes 4456448 | tf_op jit(solution)/shard_map/reduce_scatter | solution.py:269
  (117 other events, 357.7 us)
Sparse Core Ops, SparseCore 0:
  12.1 47.9 all-gather.20
  61.7 31.9 all-gather.22
  96.0 37.9 all-gather.24
  141.6 54.3 reduce-scatter.16
  197.9 50.5 all-gather.28
  249.9 31.5 all-gather.26
  283.1 33.1 all-gather.32
  318.4 50.5 all-gather.30
  390.1 52.7 reduce-scatter.18
  450.6 33.1 all-gather.34
  486.1 31.8 reduce-scatter.22
  600.9 31.8 reduce-scatter.20
  642.2 45.2 all-gather.20
  688.9 31.9 all-gather.22
  723.1 37.9 all-gather.24
  768.6 54.2 reduce-scatter.16
  825.0 50.5 all-gather.28
  877.0 31.5 all-gather.26
  910.2 33.1 all-gather.32
  945.3 50.5 all-gather.30
  1017.0 52.7 reduce-scatter.18
  1077.5 33.1 all-gather.34
  1113.0 31.8 reduce-scatter.22
  1227.8 31.8 reduce-scatter.20
Sparse Core Ops, SparseCore 1:
  1277.7 57.6 reduce-scatter.10
  1339.5 65.1 reduce-scatter.8
  1408.9 71.3 reduce-scatter.12
  1484.2 71.3 reduce-scatter.14
where the time goes:
time: 1570 us
  waiting for transfers between devices  826 us (53%)
  matrix products  334 us (21%)
  other arithmetic  158 us (10%)
  blocking collectives  119 us (8%)
  local copies, waits for them, and re-layouts  104 us (7%)
  between operations  16 us (1%)
    reduce_scatter x2, waiting for transfers between devices, forward(): lax.psum_scatter(contract_cols(mixed, whole_out), 'tensor', scatter_dimen...  108 us
    reduce_scatter x2, waiting for transfers between devices, backward(): lax.psum_scatter(contract_cols(grad_hidden, whole_up), 'tensor', scatter_...  106 us
    all_gather x2, waiting for transfers between devices, fetch(): lax.all_gather(w_down_t, 'fsdp', axis=0, tiled=True)  105 us
    all_gather x2, waiting for transfers between devices, fetch(): lax.all_gather(w_up, 'fsdp', axis=0, tiled=True)  89.3 us
    reduce_scatter x1, waiting for transfers between devices, per_device(): lax.psum_scatter(totals[2].astype(jnp.bfloat16), 'fsdp', scatter_dimensio...  73.9 us
    reduce_scatter x1, waiting for transfers between devices, per_device(): lax.psum_scatter(totals[3].astype(jnp.bfloat16), 'fsdp', scatter_dimensio...  73.5 us
    reduce_scatter x1, waiting for transfers between devices, per_device(): lax.psum_scatter(totals[0].astype(jnp.bfloat16), 'fsdp', scatter_dimensio...  67.8 us
    all_gather x2, waiting for transfers between devices, forward(): piece = lax.all_gather(second, 'tensor', axis=0, tiled=True)  66.1 us
  transfers between devices with their start and end apart: 28, of which 23 were waited for; matrix products, arithmetic and copies ran while one was open for 30% of the time, Pallas kernels for 0%

commit v1 on v0

--- a/solution.py
+++ b/solution.py
@@ -290,6 +290,147 @@
     )
 
 
+def whole_images(tokens, cotangent, w_qkv, wo_t, w_up, w_down_t, norm_gains, norm_shifts, qk_gains):
+    tensor_count = lax.axis_size("tensor")
+    local_rows = tokens.shape[1]
+    width = tokens.shape[2]
+    full_len = local_rows * tensor_count
+    own_rows = w_qkv.shape[0]
+    both = ("tensor", "fsdp")
+    scale_query = HD ** (-0.5)
+    gain_query = qk_gains[0].astype(jnp.float32)
+    gain_keys = qk_gains[1].astype(jnp.float32)
+
+    def swap(value):
+        return lax.all_to_all(value, "tensor", split_axis=0, concat_axis=1, tiled=True)
+
+    def swap_back(value):
+        return lax.all_to_all(value, "tensor", split_axis=1, concat_axis=0, tiled=True)
+
+    def gather(shard):
+        return lax.all_gather(shard, both).reshape((tensor_count, width) + shard.shape[1:])
+
+    def scatter(grad):
+        flat = grad.astype(jnp.bfloat16).reshape((tensor_count * width,) + grad.shape[2:])
+        return lax.psum_scatter(flat, both, scatter_dimension=0, tiled=True).astype(jnp.float32)
+
+    image = swap(tokens)[0]
+    grad_out = swap(cotangent)[0]
+    gains = lax.all_gather(norm_gains, "fsdp", axis=0, tiled=True).astype(jnp.float32)
+    shifts = lax.all_gather(norm_shifts, "fsdp", axis=0, tiled=True).astype(jnp.float32)
+    qkv = gather(w_qkv)
+    out_w = gather(wo_t)
+    up = gather(w_up)
+    down = gather(w_down_t)
+    head_cols = qkv.shape[3]
+    heads = head_cols // HD
+
+    residual = image.astype(jnp.float32)
+    first_hat, first_factor = norm_stats(residual)
+    first = (first_hat * gains[:, 0] + shifts[:, 0]).astype(jnp.bfloat16)
+    joined = jnp.einsum("ld,tdpc->tplc", first, qkv, preferred_element_type=jnp.float32)
+    joined = joined.reshape(tensor_count, 3, full_len, heads, HD)
+    query_hat, query_factor = norm_stats(joined[:, 0])
+    keys_hat, keys_factor = norm_stats(joined[:, 1])
+    query_n = (query_hat * gain_query * scale_query).astype(jnp.bfloat16)
+    keys_n = (keys_hat * gain_keys).astype(jnp.bfloat16)
+    values = joined[:, 2].astype(jnp.bfloat16)
+
+    def attend(item):
+        query_one, keys_one, values_one = item
+        scores = jnp.einsum("qhd,khd->hqk", query_one, keys_one, preferred_element_type=jnp.float32)
+        largest = jnp.max(scores, -1, keepdims=True)
+        exponent = jnp.exp(scores - largest)
+        total_sum = jnp.sum(exponent, -1, keepdims=True)
+        probs_low = (exponent / total_sum).astype(jnp.bfloat16)
+        mixed_one = jnp.einsum("hqk,khd->qhd", probs_low, values_one, preferred_element_type=jnp.float32)
+        return mixed_one.astype(jnp.bfloat16), largest + jnp.log(total_sum)
+
+    mixed, log_total = lax.map(attend, (query_n, keys_n, values))
+    mixed = mixed.reshape(tensor_count, full_len, head_cols)
+    middle = residual + jnp.einsum("tlc,tdc->ld", mixed, out_w, preferred_element_type=jnp.float32)
+    second_hat, second_factor = norm_stats(middle)
+    second = (second_hat * gains[:, 1] + shifts[:, 1]).astype(jnp.bfloat16)
+    hidden = jnp.einsum("ld,tdf->tlf", second, up, preferred_element_type=jnp.float32)
+    active, gelu_pull = jax.vjp(lambda value: jax.nn.gelu(value, approximate=False), hidden)
+    active = active.astype(jnp.bfloat16)
+    result = (
+        middle + jnp.einsum("tlf,tdf->ld", active, down, preferred_element_type=jnp.float32)
+    ).astype(jnp.bfloat16)
+
+    grad_active = jnp.einsum("ld,tdf->tlf", grad_out, down, preferred_element_type=jnp.float32)
+    grad_down = jnp.einsum("ld,tlf->tdf", grad_out, active, preferred_element_type=jnp.float32)
+    grad_down = scatter(grad_down)
+    grad_hidden = gelu_pull(grad_active)[0].astype(jnp.bfloat16)
+    grad_up = jnp.einsum("ld,tlf->tdf", second, grad_hidden, preferred_element_type=jnp.float32)
+    grad_up = scatter(grad_up)
+    grad_second = jnp.einsum("tlf,tdf->ld", grad_hidden, up, preferred_element_type=jnp.float32)
+    grad_middle = grad_out.astype(jnp.float32) + norm_back(
+        grad_second * gains[:, 1], second_hat, second_factor
+    )
+    grad_branch = grad_middle.astype(jnp.bfloat16)
+    grad_out_w = jnp.einsum("ld,tlc->tdc", grad_branch, mixed, preferred_element_type=jnp.float32)
+    grad_out_w = scatter(grad_out_w)
+    grad_mixed = jnp.einsum("ld,tdc->tlc", grad_branch, out_w, preferred_element_type=jnp.float32)
+    grad_mixed = grad_mixed.astype(jnp.bfloat16).reshape(tensor_count, full_len, heads, HD)
+
+    def attend_back(item):
+        query_one, keys_one, values_one, grad_one, log_one = item
+        scores = jnp.einsum("qhd,khd->hqk", query_one, keys_one, preferred_element_type=jnp.float32)
+        probs = jnp.exp(scores - log_one)
+        grad_probs = jnp.einsum("qhd,khd->hqk", grad_one, values_one, preferred_element_type=jnp.float32)
+        delta = jnp.sum(probs * grad_probs, -1, keepdims=True)
+        grad_scores = (probs * (grad_probs - delta)).astype(jnp.bfloat16)
+        return (
+            jnp.einsum("hqk,khd->qhd", grad_scores, keys_one, preferred_element_type=jnp.float32),
+            jnp.einsum("hqk,qhd->khd", grad_scores, query_one, preferred_element_type=jnp.float32),
+            jnp.einsum(
+                "hqk,qhd->khd", probs.astype(jnp.bfloat16), grad_one, preferred_element_type=jnp.float32
+            ),
+        )
+
+    grad_query_n, grad_keys_n, grad_values = lax.map(
+        attend_back, (query_n, keys_n, values, grad_mixed, log_total)
+    )
+    grad_query = norm_back(grad_query_n * gain_query * scale_query, query_hat, query_factor)
+    grad_keys = norm_back(grad_keys_n * gain_keys, keys_hat, keys_factor)
+    qk_grad = jnp.stack(
+        [
+            jnp.sum(grad_query_n * query_hat * scale_query, (0, 1, 2)),
+            jnp.sum(grad_keys_n * keys_hat, (0, 1, 2)),
+        ]
+    )
+    grad_joined = jnp.stack([grad_query, grad_keys, grad_values], 1).astype(jnp.bfloat16)
+    grad_joined = grad_joined.reshape(tensor_count, 3, full_len, head_cols)
+    grad_qkv = jnp.einsum("ld,tplc->tdpc", first, grad_joined, preferred_element_type=jnp.float32)
+    grad_qkv = scatter(grad_qkv)
+    grad_first = jnp.einsum("tplc,tdpc->ld", grad_joined, qkv, preferred_element_type=jnp.float32)
+    grad_input = grad_middle + norm_back(grad_first * gains[:, 0], first_hat, first_factor)
+    gain_grad = jnp.stack(
+        [jnp.sum(grad_first * first_hat, 0), jnp.sum(grad_second * second_hat, 0)], 1
+    )
+    shift_grad = jnp.stack([jnp.sum(grad_first, 0), jnp.sum(grad_second, 0)], 1)
+    gain_total, shift_total, qk_total = lax.psum((gain_grad, shift_grad, qk_grad), ("fsdp", "tensor"))
+    offset = lax.axis_index("fsdp") * own_rows
+    return (
+        swap_back(result[None]),
+        swap_back(grad_input[None].astype(jnp.bfloat16)).astype(jnp.float32),
+        grad_qkv,
+        grad_out_w,
+        grad_up,
+        grad_down,
+        lax.dynamic_slice_in_dim(gain_total, offset, own_rows, 0),
+        lax.dynamic_slice_in_dim(shift_total, offset, own_rows, 0),
+        qk_total,
+    )
+
+
+def layer(tokens, *rest):
+    if tokens.shape[0] == lax.axis_size("tensor"):
+        return whole_images(tokens, *rest)
+    return per_device(tokens, *rest)
+
+
 def solution(mesh):
     in_specs = (
         P("fsdp", "tensor", None),
@@ -314,5 +455,5 @@
         P(),
     )
     return jax.shard_map(
-        per_device, mesh=mesh, in_specs=in_specs, out_specs=out_specs, check_vma=False
-    )
+        layer, mesh=mesh, in_specs=in_specs, out_specs=out_specs, check_vma=False
+    )

time: 1570 us -> 1180 us (0.75)
  waiting for transfers between devices: 826 us -> 392 us
  matrix products: 334 us -> 389 us
  starting transfers between devices: 1.53 us -> 17.9 us
    all_gather x16 -> x4, waiting for transfers between devices: 391 us -> 42.2 us  [gather(): lax.all_gather(shard, both).reshape((tensor_count, width) + shard.shape[1:])]
    reduce_scatter x12 -> x4, waiting for transfers between devices: 430 us -> 314 us  [scatter(): lax.psum_scatter(flat, both, scatter_dimension=0, tiled=True)]
    while x276 -> x12, local copies, waits for them, and re-layouts: 64.3 us -> 2.59 us
    dot_general x52 -> x26, matrix products: 334 us -> 389 us  [the longest x1 47.3 us: whole_images(): jnp.einsum('ld,tdf->tlf', second, up, preferred_element_type=jnp.float32)]
    all_gather x4 -> x2, blocking collectives: 79.5 us -> 40 us  [the longest x1 22.6 us: whole_images(): lax.all_gather(norm_gains, 'fsdp', axis=0, tiled=True).astype(jnp.float32)]
    convert_element_type x25 -> x12, other arithmetic: 50.1 us -> 16.1 us  [the longest x4 6.77 us: scatter(): lax.psum_scatter(flat, both, scatter_dimension=0, tiled=True)]
    all_to_all x0 -> x4, waiting for transfers between devices: none -> 33.1 us  [the longest x2 33.1 us: swap(): lax.all_to_all(value, 'tensor', split_axis=0, concat_axis=1, tiled=True)]
    unnamed x6 -> x113, local copies, waits for them, and re-layouts: 0.68 us -> 29.6 us
  transfers between devices with their start and end apart: 28 -> 12, of which waited for: 23 -> 6; matrix products, arithmetic and copies ran while one was open for 30% -> 30% of each run, Pallas kernels for 0% -> 0%
where the time goes in v1:
time: 1180 us; the launch traced here: 1170 us
  waiting for transfers between devices  392 us (33%)
  matrix products  389 us (33%)
  other arithmetic  155 us (13%)
  blocking collectives  105 us (9%)
  local copies, waits for them, and re-layouts  94.4 us (8%)
  starting transfers between devices  17.9 us (2%)
  between operations  15.1 us (1%)
    reduce_scatter x4, waiting for transfers between devices, scatter(): lax.psum_scatter(flat, both, scatter_dimension=0, tiled=True)  314 us
    psum x1, blocking collectives, whole_images(): lax.psum((gain_grad, shift_grad, qk_grad), ('fsdp', 'tensor'))  65.3 us
    convert_element_type x2, other arithmetic, attend_back(): grad_scores = (probs * (grad_probs - delta)).astype(jnp.bfloat16)  56.2 us
    dot_general x1, matrix products, whole_images(): jnp.einsum('ld,tdf->tlf', second, up, preferred_element_type=jnp.float32)  47.3 us
    dot_general x2, matrix products, attend_back(): jnp.einsum('qhd,khd->hqk', grad_one, values_one, preferred_element_type=j...  44.8 us
    all_gather x4, waiting for transfers between devices, gather(): lax.all_gather(shard, both).reshape((tensor_count, width) + shard.shape[1:])  42.2 us
    all_to_all x2, waiting for transfers between devices, swap(): lax.all_to_all(value, 'tensor', split_axis=0, concat_axis=1, tiled=True)  33.1 us
    unnamed x113, local copies, waits for them, and re-layouts  29.6 us
  transfers between devices with their start and end apart: 12, of which 6 were waited for; matrix products, arithmetic and copies ran while one was open for 30% of the time, Pallas kernels for 0%

profile of v1, /device:TPU:0, one launch (start us, length us, event | category | flops | bytes accessed | tf_op | source)
XLA Modules:
  0.0 1169.8 jit_solution(9036196607701467325)
XLA Ops:
  14.3 22.6 %all-gather.4 = bf16[16,64,2]{1,2,0:T(2,128)(2,1)S(1)} all-gather(bf16[1,64,2]{1,2,0:T(2,128)(2,1)S(1)} %bitcast.380), channel_id=1, replica_groups=mesh['fsdp'=16,'tensor'=2] {'fsdp'}, dimensions={0}, use_global_device_ids=true | all-gather | bytes 4352 | tf_op jit(solution)/shard_map/all_gather | solution.py:319
  36.9 17.5 %all-gather.5 = bf16[16,64,2]{1,2,0:T(2,128)(2,1)S(1)} all-gather(bf16[1,64,2]{1,2,0:T(2,128)(2,1)S(1)} %bitcast.381), channel_id=1, replica_groups=mesh['fsdp'=16,'tensor'=2] {'fsdp'}, dimensions={0}, use_global_device_ids=true | all-gather | bytes 4352 | tf_op jit(solution)/shard_map/all_gather | solution.py:320
  62.9 33.1 %all-to-all-done.2 = bf16[2,512,1024]{2,1,0:T(8,128)(2,1)} async-done(((bf16[2,512,1024]{2,1,0:T(8,128)(2,1)}), bf16[2,512,1024]{2,1,0:T(8,128)(2,1)}, u32[]{:S(2)}, u32[]{:S(2)}) %all-to-all-start.2) | async-done | bytes 2097184 | tf_op jit(solution)/shard_map/all_to_all | solution.py:305
  105.1 9.9 fusion.65
  124.1 89.2 %while.26 = (s32[]{:T(128)}, bf16[2,1024,8,64]{1,3,2,0:T(8,128)(2,1)}, f32[2,8,1024,1]{2,1,3,0:T(8,128)S(1)}, bf16[2,1024,8,64]{1,3,2,0:T(8,128)(2,1)}, bf16[2,1...) while((s32[]{:T(128)}, bf16[2,1024,8,64]{1,3,2,0:T(8,128)(2,1)}, ...), condition=%wide.region_9.10_spmd, body=%wide.region_6.9_spmd.sunk | while | flops 2198331392 | bytes 130287792 | solution.py:349
  124.5 14.7 %fusion.142 = (f32[8,1024]{1,0:T(8,128)S(1)}, f32[8,1024,1024]{1,2,0:T(8,128)}) fusion(bf16[2,1024,8,64]{1,3,2,0:T(8,128)(2,1)} %get-tuple-element.304, s32[]{:T(128)S(6)} %copy.259, bf16[2,1024,8,64]{1,3,2,0:T(8,128)(2,1)S(1)} %get-tuple-element.303), kind=kOutput, calls=%fused_computation.173.clone.1 | convolution fusion | flops 1082122240 | bytes 35685376 | tf_op jit(solution)/shard_map/while/body/eval_jaxpr/qhd,khd->hqk/dot_general | solution.py:341
  139.2 14.0 %fusion.143 = f32[8,1024]{1,0:T(8,128)S(1)} fusion(f32[8,1024,1024]{1,2,0:T(8,128)} %get-tuple-element.272, f32[8,1024]{1,0:T(8,128)S(1)} %get-tuple-element.273), kind=kLoop, calls=%fused_computation.2.clone.1 | loop fusion | flops 16769024 | bytes 33619968 | tf_op jit(solution)/shard_map/while/body/eval_jaxpr/reduce_sum | solution.py:344
  153.3 13.8 %fusion.144 = bf16[2,1024,8,64]{1,3,2,0:T(8,128)(2,1)S(1)} fusion(bf16[2,1024,8,64]{1,3,2,0:T(8,128)(2,1)S(1)} %copy-done.52, s32[]{:T(128)S(6)} %copy.259, f32[8,1024,1024]{1,2,0:T(8,128)} %get-tuple-element.272, f32[8,1024]{1,0:T(8,128)S(1)} %fusion.143, f32[8,1024]{1,0:T(8,128)S(1)} %get-tuple-element.273, bf16[2,1024,8,64]{1,3,2,0:T(8,128)(2,1)S(1)} %copy-done.11), kind=kOutput, calls=%fused_computation.6.clone.1 | convolution fusion | flops 1099431936 | bytes 35718144 | tf_op jit(solution)/shard_map/while/body/eval_jaxpr/hqk,khd->qhd/dot_general | solution.py:346
  168.4 14.6 %fusion.142 = (f32[8,1024]{1,0:T(8,128)S(1)}, f32[8,1024,1024]{1,2,0:T(8,128)}) fusion(bf16[2,1024,8,64]{1,3,2,0:T(8,128)(2,1)} %get-tuple-element.304, s32[]{:T(128)S(6)} %copy.259, bf16[2,1024,8,64]{1,3,2,0:T(8,128)(2,1)S(1)} %get-tuple-element.303), kind=kOutput, calls=%fused_computation.173.clone.1 | convolution fusion | flops 1082122240 | bytes 35685376 | tf_op jit(solution)/shard_map/while/body/eval_jaxpr/qhd,khd->hqk/dot_general | solution.py:341
  183.0 13.9 %fusion.143 = f32[8,1024]{1,0:T(8,128)S(1)} fusion(f32[8,1024,1024]{1,2,0:T(8,128)} %get-tuple-element.272, f32[8,1024]{1,0:T(8,128)S(1)} %get-tuple-element.273), kind=kLoop, calls=%fused_computation.2.clone.1 | loop fusion | flops 16769024 | bytes 33619968 | tf_op jit(solution)/shard_map/while/body/eval_jaxpr/reduce_sum | solution.py:344
  197.0 14.9 %fusion.144 = bf16[2,1024,8,64]{1,3,2,0:T(8,128)(2,1)S(1)} fusion(bf16[2,1024,8,64]{1,3,2,0:T(8,128)(2,1)S(1)} %copy-done.52, s32[]{:T(128)S(6)} %copy.259, f32[8,1024,1024]{1,2,0:T(8,128)} %get-tuple-element.272, f32[8,1024]{1,0:T(8,128)S(1)} %fusion.143, f32[8,1024]{1,0:T(8,128)S(1)} %get-tuple-element.273, bf16[2,1024,8,64]{1,3,2,0:T(8,128)(2,1)S(1)} %copy-done.11), kind=kOutput, calls=%fused_computation.6.clone.1 | convolution fusion | flops 1099431936 | bytes 35718144 | tf_op jit(solution)/shard_map/while/body/eval_jaxpr/hqk,khd->qhd/dot_general | solution.py:346
  213.2 6.6 fusion.104
  222.5 10.6 all-gather.15.cloned.1.call-done
  233.0 47.3 %fusion.50 = (bf16[2,1024,2048]{2,1,0:T(8,128)(2,1)}, f32[2,1024,2048]{2,1,0:T(8,128)}, f32[1024,2,2048]{2,0,1:T(8,128)}) fusion(bf16[2,1024,2048]{2,1,0:T(8,128)(2,1)} %bitcast.384, bf16[1024,1024,1]{0,1,2:T(8,128)(2,1)S(1)} %fusion.98.clone.4), kind=kOutput, calls=%fused_computation.65 | convolution fusion | flops 8862564352 | bytes 52428800 | tf_op jit(solution)/shard_map/ld,tdf->tlf/dot_general | solution.py:354
  280.3 31.6 %all-gather.17.cloned.1.call-done = bf16[2048,2048]{1,0:T(8,128)(2,1)} async-done(((bf16[64,2048]{1,0:T(8,128)(2,1)}), bf16[2048,2048]{1,0:T(8,128)(2,1)}) %all-gather.17.cloned.1.call-update) | async-done | bytes 8388624 | tf_op jit(solution)/shard_map/all_gather | solution.py:311
  312.0 25.0 %fusion.47 = bf16[2,1024,2048]{2,1,0:T(8,128)(2,1)} fusion(f32[2,1024,2048]{2,1,0:T(8,128)} %get-tuple-element.160, f32[1024,2,2048]{2,0,1:T(8,128)} %get-tuple-element.179, bf16[1024,1024,1]{1,0,2:T(8,128)(2,1)} %bitcast.47, bf16[2,1024,2048]{2,1,0:T(8,128)(2,1)} %bitcast.382), kind=kOutput, calls=%fused_computation.57 | convolution fusion | flops 8648654848 | bytes 52428800 | tf_op jit(solution)/shard_map/ld,tdf->tlf/dot_general | solution.py:361
  336.9 15.9 %fusion.105 = (f32[1024]{0:T(1024)}, f32[1024,1024]{1,0:T(8,128)}) fusion(bf16[2,1024,2048]{2,1,0:T(8,128)(2,1)} %fusion.47, bf16[2,1024,2048]{2,1,0:T(8,128)(2,1)} %bitcast.385), kind=kOutput, calls=%fused_computation.178 | convolution fusion | flops 8590982144 | bytes 20975616 | tf_op jit(solution)/shard_map/tlf,tdf->ld/dot_general | solution.py:367
  352.8 5.5 copy.169
  377.5 205.1 %while.27 = (s32[]{:T(128)}, f32[2,1024,8,64]{1,3,2,0:T(8,128)}, f32[2,1024,8,64]{1,3,2,0:T(8,128)}, bf16[2,1024,8,64]{1,3,2,0:T(8,128)(2,1)}, bf16[2,1024,8,64]...) while((s32[]{:T(128)}, f32[2,1024,8,64]{1,3,2,0:T(8,128)}, ...), condition=%wide.region_16.17_spmd, body=%wide.region_14.16_spmd.sunk | while | flops 5444198400 | bytes 265524352 | solution.py:392
  377.9 14.4 %fusion.153 = f32[8,1024,1024]{1,2,0:T(8,128)} fusion(bf16[2,1024,8,64]{1,3,2,0:T(8,128)(2,1)S(1)} %get-tuple-element.331, s32[]{:T(128)S(6)} %copy.269, bf16[2,1024,8,64]{1,3,2,0:T(8,128)(2,1)} %get-tuple-element.330), kind=kOutput, calls=%fused_computation.31.clone.1 | convolution fusion | flops 1073741824 | bytes 35652608 | tf_op jit(solution)/shard_map/while/body/eval_jaxpr/qhd,khd->hqk/dot_general | solution.py:379
  392.4 14.6 %bitcast_dynamic-update-slice_fusion.11 = bf16[2,1024,8,64]{1,3,2,0:T(8,128)(2,1)} fusion(bf16[2,1024,8,64]{1,3,2,0:T(8,128)(2,1)} %get-tuple-element.319, s32[]{:T(128)S(6)} %copy.269, f32[8,1024,1024]{1,2,0:T(8,128)} %fusion.153, f32[8,1024]{1,0:T(8,128)S(1)} %dynamic-slice_bitcast_fusion.2, bf16[2,1024,8,64]{1,3,2,0:T(8,128)(2,1)} %get-tuple-element.333), kind=kOutput, calls=%fused_computation.23.clone.1 | convolution fusion | flops 1090519040 | bytes 36733952 | tf_op jit(solution)/shard_map/while/body/eval_jaxpr/hqk,qhd->khd/dot_general | solution.py:387
  406.9 22.4 %multiply_reduce_fusion.17 = (f32[8,1024]{1,0:T(8,128)S(1)}, f32[8,1024,1024]{1,2,0:T(8,128)}) fusion(f32[8,1024,1024]{1,2,0:T(8,128)} %fusion.153, f32[8,1024]{1,0:T(8,128)S(1)} %dynamic-slice_bitcast_fusion.2, bf16[2,1024,8,64]{1,3,2,0:T(8,128)(2,1)} %get-tuple-element.334, s32[]{:T(128)S(6)} %copy.269, ...), kind=kOutput, calls=%fused_computation.18.clone.1 | convolution fusion | flops 1098899456 | bytes 69272576 | tf_op jit(solution)/shard_map/while/body/eval_jaxpr/qhd,khd->hqk/dot_general | solution.py:381
  429.3 28.1 %multiply_convert_fusion.6 = bf16[8,1024,1024]{1,2,0:T(8,128)(2,1)} fusion(f32[8,1024,1024]{1,2,0:T(8,128)} %get-tuple-element.283, f32[8,1024,1024]{1,2,0:T(8,128)} %fusion.153, f32[8,1024]{1,0:T(8,128)S(1)} %get-tuple-element.284, f32[8,1024]{1,0:T(8,128)S(1)} %dynamic-slice_bitcast_fusion.2), kind=kLoop, calls=%fused_computation.17.clone.1 | loop fusion | flops 33554432 | bytes 83951616 | tf_op jit(solution)/shard_map/while/body/eval_jaxpr/convert_element_type | solution.py:383
  457.5 12.3 %bitcast_dynamic-update-slice_fusion.10 = f32[2,1024,8,64]{1,3,2,0:T(8,128)} fusion(f32[2,1024,8,64]{1,3,2,0:T(8,128)} %get-tuple-element.318, s32[]{:T(128)S(6)} %copy.269, bf16[8,1024,1024]{1,2,0:T(8,128)(2,1)} %multiply_convert_fusion.6, bf16[2,1024,8,64]{1,3,2,0:T(8,128)(2,1)S(1)} %get-tuple-element.331), kind=kOutput, calls=%fused_computation.24.clone.1 | convolution fusion | flops 1073741824 | bytes 19923968 | tf_op jit(solution)/shard_map/while/body/eval_jaxpr/hqk,qhd->khd/dot_general | solution.py:386
  469.8 10.4 bitcast_dynamic-update-slice_fusion.9
  480.2 14.4 %fusion.153 = f32[8,1024,1024]{1,2,0:T(8,128)} fusion(bf16[2,1024,8,64]{1,3,2,0:T(8,128)(2,1)S(1)} %get-tuple-element.331, s32[]{:T(128)S(6)} %copy.269, bf16[2,1024,8,64]{1,3,2,0:T(8,128)(2,1)} %get-tuple-element.330), kind=kOutput, calls=%fused_computation.31.clone.1 | convolution fusion | flops 1073741824 | bytes 35652608 | tf_op jit(solution)/shard_map/while/body/eval_jaxpr/qhd,khd->hqk/dot_general | solution.py:379
  494.6 14.6 %bitcast_dynamic-update-slice_fusion.11 = bf16[2,1024,8,64]{1,3,2,0:T(8,128)(2,1)} fusion(bf16[2,1024,8,64]{1,3,2,0:T(8,128)(2,1)} %get-tuple-element.319, s32[]{:T(128)S(6)} %copy.269, f32[8,1024,1024]{1,2,0:T(8,128)} %fusion.153, f32[8,1024]{1,0:T(8,128)S(1)} %dynamic-slice_bitcast_fusion.2, bf16[2,1024,8,64]{1,3,2,0:T(8,128)(2,1)} %get-tuple-element.333), kind=kOutput, calls=%fused_computation.23.clone.1 | convolution fusion | flops 1090519040 | bytes 36733952 | tf_op jit(solution)/shard_map/while/body/eval_jaxpr/hqk,qhd->khd/dot_general | solution.py:387
  509.1 22.4 %multiply_reduce_fusion.17 = (f32[8,1024]{1,0:T(8,128)S(1)}, f32[8,1024,1024]{1,2,0:T(8,128)}) fusion(f32[8,1024,1024]{1,2,0:T(8,128)} %fusion.153, f32[8,1024]{1,0:T(8,128)S(1)} %dynamic-slice_bitcast_fusion.2, bf16[2,1024,8,64]{1,3,2,0:T(8,128)(2,1)} %get-tuple-element.334, s32[]{:T(128)S(6)} %copy.269, ...), kind=kOutput, calls=%fused_computation.18.clone.1 | convolution fusion | flops 1098899456 | bytes 69272576 | tf_op jit(solution)/shard_map/while/body/eval_jaxpr/qhd,khd->hqk/dot_general | solution.py:381
  531.6 28.1 %multiply_convert_fusion.6 = bf16[8,1024,1024]{1,2,0:T(8,128)(2,1)} fusion(f32[8,1024,1024]{1,2,0:T(8,128)} %get-tuple-element.283, f32[8,1024,1024]{1,2,0:T(8,128)} %fusion.153, f32[8,1024]{1,0:T(8,128)S(1)} %get-tuple-element.284, f32[8,1024]{1,0:T(8,128)S(1)} %dynamic-slice_bitcast_fusion.2), kind=kLoop, calls=%fused_computation.17.clone.1 | loop fusion | flops 33554432 | bytes 83951616 | tf_op jit(solution)/shard_map/while/body/eval_jaxpr/convert_element_type | solution.py:383
  559.7 12.3 %bitcast_dynamic-update-slice_fusion.10 = f32[2,1024,8,64]{1,3,2,0:T(8,128)} fusion(f32[2,1024,8,64]{1,3,2,0:T(8,128)} %get-tuple-element.318, s32[]{:T(128)S(6)} %copy.269, bf16[8,1024,1024]{1,2,0:T(8,128)(2,1)} %multiply_convert_fusion.6, bf16[2,1024,8,64]{1,3,2,0:T(8,128)(2,1)S(1)} %get-tuple-element.331), kind=kOutput, calls=%fused_computation.24.clone.1 | convolution fusion | flops 1073741824 | bytes 19923968 | tf_op jit(solution)/shard_map/while/body/eval_jaxpr/hqk,qhd->khd/dot_general | solution.py:386
  571.9 10.5 bitcast_dynamic-update-slice_fusion.9
  592.7 6.0 multiply_reduce_fusion.1
  608.3 13.0 %convert_bitcast_fusion = bf16[2,1024,3,512]{1,3,2,0:T(8,128)(2,1)} fusion(f32[1024,1024]{0,1:T(8,128)} %copy.202, f32[1024]{0:T(1024)S(1)} %bitcast.375, f32[1024]{0:T(1024)S(1)} %bitcast.364, f32[1024]{0:T(1024)S(1)} %bitcast.361, f32[1024]{0:T(1024)S(1)} %bitcast.367, bf16[2,1,1024,512]{3,2,0,1:T(8,128)(2,1)} %copy.174, ...), kind=kOutput, calls=%fused_computation.84 | convolution fusion | flops 6457131008 | bytes 16793600 | tf_op jit(solution)/shard_map/ld,tplc->tdpc/dot_general | solution.py:405
  621.3 8.6 copy.179
  630.6 15.4 %convolution_convert_fusion.1 = bf16[2,2048,1024]{1,2,0:T(8,128)(2,1)} fusion(bf16[2,1024,2048]{2,1,0:T(8,128)(2,1)} %fusion.47, f32[1024,1024]{0,1:T(8,128)} %copy-done.6, f32[1024]{0:T(1024)S(1)} %bitcast.373, f32[1024]{0:T(1024)S(1)} %bitcast.359, f32[1024]{0:T(1024)S(1)} %copy-done.30, f32[1024]{0:T(1024)S(1)} %copy-done.27), kind=kOutput, calls=%fused_computation.86 | convolution fusion | flops 8599371776 | bytes 20987904 | tf_op jit(solution)/shard_map/ld,tlf->tdf/dot_general | solution.py:365
  646.1 15.1 %convolution_convert_fusion = bf16[2,2048,1024]{1,2,0:T(8,128)(2,1)} fusion(bf16[1024,1024,1]{1,0,2:T(8,128)(2,1)} %bitcast.47, bf16[2,1024,2048]{2,1,0:T(8,128)(2,1)} %get-tuple-element.159), kind=kOutput, calls=%fused_computation.85 | convolution fusion | flops 8594128896 | bytes 18874368 | tf_op jit(solution)/shard_map/ld,tlf->tdf/dot_general | solution.py:362
  661.2 14.4 %fusion.91 = bf16[1,1024,1024]{1,2,0:T(8,128)(2,1)S(1)} fusion(f32[1024,1024]{0,1:T(8,128)} %copy-done.6, bf16[2,1024,2048]{2,1,0:T(8,128)(2,1)} %get-tuple-element.159, bf16[2,1024,2048]{2,1,0:T(8,128)(2,1)} %bitcast.383), kind=kOutput, calls=%fused_computation.142 | convolution fusion | flops 8592031744 | bytes 23068672 | tf_op jit(solution)/shard_map/tlf,tdf->ld/dot_general | solution.py:358
  675.6 7.7 copy.164
  683.8 12.8 %reduce.10 = bf16[1024,1024]{1,0:T(8,128)(2,1)S(1)} reduce(bf16[1024,1,1024]{2,1,0:T(2,128)(2,1)} %bitcast.341, bf16[]{:T(256)} %broadcast.241), dimensions={1}, to_apply=%bitcast.265.reduce_sub_computation | reduce | bytes 4194306
  704.0 12.5 %fusion.106 = (f32[1024]{0:T(1024)S(1)}, f32[1024,1024]{1,0:T(8,128)}) fusion(bf16[2,1024,3,512]{3,1,0,2:T(8,128)(2,1)} %bitcast.387, bf16[2,1,1024,512]{3,2,0,1:T(8,128)(2,1)} %copy.174, bf16[2,1,1024,512]{3,2,0,1:T(8,128)(2,1)} %copy.173, bf16[2,1,1024,512]{3,2,0,1:T(8,128)(2,1)} %copy.172), kind=kOutput, calls=%fused_computation.179 | convolution fusion | flops 6449789952 | bytes 16781312 | tf_op jit(solution)/shard_map/tplc,tdpc->ld/dot_general | solution.py:407
  716.4 5.3 copy.175
  731.3 7.5 copy.176
  738.8 12.8 %reduce.11 = bf16[1024,1024]{1,0:T(8,128)(2,1)S(1)} reduce(bf16[1024,1,1024]{2,1,0:T(2,128)(2,1)} %bitcast.342, bf16[]{:T(256)} %broadcast.241), dimensions={1}, to_apply=%bitcast.263.reduce_sub_computation | reduce | bytes 4194306
  758.0 65.3 %all-reduce = (f32[1024,2]{0,1:T(2,128)S(1)}, f32[1024,2]{0,1:T(2,128)S(1)}, f32[2,64]{1,0:T(2,128)}) all-reduce(f32[1024,2]{0,1:T(2,128)S(1)} %pad_maximum_fusion.1, f32[1024,2]{0,1:T(2,128)S(1)} %pad_maximum_fusion.2, f32[2,64]{1,0:T(2,128)S(1)} %pad_maximum_fusion.3), channel_id=1, replica_groups=mesh['fsdp'=16,'tensor'=2] {'fsdp','tensor'}, use_global_device_ids=true, to_apply=%region_29.30 | all-reduce | flops 4224 | bytes 33792 | tf_op jit(solution)/shard_map/psum | solution.py:413
  836.4 5.2 copy.212
  843.1 23.1 %reduce-scatter.5.cloned.1.call-done = bf16[64,3,512]{2,0,1:T(8,128)(2,1)} async-done(((bf16[2048,3,512]{2,0,1:T(8,128)(2,1)}), bf16[64,3,512]{2,0,1:T(8,128)(2,1)}) %reduce-scatter.5.cloned.1.call-update) | async-done | bytes 196624 | tf_op jit(solution)/shard_map/reduce_scatter | solution.py:315
  868.0 145.8 %reduce-scatter.9.cloned.1.call-done = bf16[64,2048]{1,0:T(8,128)(2,1)} async-done(((bf16[2048,2048]{1,0:T(8,128)(2,1)}), bf16[64,2048]{1,0:T(8,128)(2,1)}) %reduce-scatter.9.cloned.1.call-update) | async-done | bytes 262160 | tf_op jit(solution)/shard_map/reduce_scatter | solution.py:315
  1015.6 145.4 %reduce-scatter.11.cloned.1.call-done = bf16[64,2048]{1,0:T(8,128)(2,1)} async-done(((bf16[2048,2048]{1,0:T(8,128)(2,1)}), bf16[64,2048]{1,0:T(8,128)(2,1)}) %reduce-scatter.11.cloned.1.call-update) | async-done | bytes 262160 | tf_op jit(solution)/shard_map/reduce_scatter | solution.py:315
  (218 shorter events, 121.7 us)
Async XLA Ops:
  7.2 7.1 copy-start.49
  7.2 29.7 %copy-start.50 = (bf16[64,2]{0,1:T(2,128)(2,1)S(1)}, bf16[64,2]{0,1:T(2,128)(2,1)}, u32[]{:S(2)}) copy-start(bf16[64,2]{0,1:T(2,128)(2,1)} %param.20) | copy-start | bytes 772
  7.2 97.9 %all-gather.11.cloned.1.call-start = ((), (), s32[]{:S(2)}) async-start(), calls=%async_computation.12 | async-start | bytes 6488064 | tf_op jit(solution)/shard_map/all_gather | solution.py:311
  7.9 205.3 %all-gather.13.cloned.1.call-start = ((), (), s32[]{:S(2)}) async-start(), calls=%async_computation.13 | async-start | bytes 2162688 | tf_op jit(solution)/shard_map/all_gather | solution.py:311
  8.7 224.3 %all-gather.15.cloned.1.call-start = ((), (), s32[]{:S(2)}) async-start(), calls=%async_computation.14 | async-start | bytes 8650752 | tf_op jit(solution)/shard_map/all_gather | solution.py:311
  9.4 51.2 %copy-start.48 = (bf16[2,64]{1,0:T(2,128)(2,1)S(1)}, bf16[2,64]{1,0:T(2,128)(2,1)}, u32[]{:S(2)}) copy-start(bf16[2,64]{1,0:T(2,128)(2,1)} %param.21) | copy-start | bytes 772
  9.4 46.3 %all-to-all-start = ((bf16[2,512,1024]{2,1,0:T(8,128)(2,1)}), bf16[2,512,1024]{2,1,0:T(8,128)(2,1)S(1)}, u32[]{:S(2)}, u32[]{:S(2)}) async-start(bf16[2,512,1024]{2,1,0:T(8,128)(2,1)} %param.13), calls=%async_computation | async-start | bytes 4194304 | tf_op jit(solution)/shard_map/all_to_all | solution.py:305
  13.6 298.3 %all-gather.17.cloned.1.call-start = ((), (), s32[]{:S(2)}) async-start(), calls=%async_computation.15 | async-start | bytes 8650752 | tf_op jit(solution)/shard_map/all_gather | solution.py:311
  55.1 47.8 %copy-start.34 = (f32[1024,1]{0,1:T(1,128)}, f32[1024,1]{0,1:T(1,128)S(1)}, u32[]{:S(2)}) copy-start(f32[1024,1]{0,1:T(1,128)S(1)} %get-tuple-element.168) | copy-start | bytes 12292
  55.7 47.2 %copy-start.41 = (f32[1024,1]{0,1:T(1,128)}, f32[1024,1]{0,1:T(1,128)S(1)}, u32[]{:S(2)}) copy-start(f32[1024,1]{0,1:T(1,128)S(1)} %get-tuple-element.170) | copy-start | bytes 12292
  55.7 40.3 %all-to-all-start.2 = ((bf16[2,512,1024]{2,1,0:T(8,128)(2,1)}), bf16[2,512,1024]{2,1,0:T(8,128)(2,1)}, u32[]{:S(2)}, u32[]{:S(2)}) async-start(bf16[2,512,1024]{2,1,0:T(8,128)(2,1)} %param.14), calls=%async_computation.2 | async-start | bytes 4194304 | tf_op jit(solution)/shard_map/all_to_all | solution.py:305
  60.5 781.1 %reduce-scatter.7.cloned.1.call-start = ((), (), s32[]{:S(2)}) async-start(), calls=%async_computation.9 | async-start | bytes 2162688 | tf_op jit(solution)/shard_map/reduce_scatter | solution.py:315
  60.6 60.3 %copy-start.45 = (f32[64]{0:T(128)}, f32[64]{0:T(128)S(1)}, u32[]{:S(2)}) copy-start(f32[64]{0:T(128)S(1)} %get-tuple-element.176) | copy-start | bytes 772
  60.6 61.2 %copy-start.43 = (f32[64]{0:T(128)}, f32[64]{0:T(128)S(1)}, u32[]{:S(2)}) copy-start(f32[64]{0:T(128)S(1)} %get-tuple-element.175) | copy-start | bytes 772
  139.2 14.0 %copy-start.11 = (bf16[2,1024,8,64]{1,3,2,0:T(8,128)(2,1)S(1)}, bf16[2,1024,8,64]{1,3,2,0:T(8,128)(2,1)}, u32[]{:S(2)}) copy-start(bf16[2,1024,8,64]{1,3,2,0:T(8,128)(2,1)} %get-tuple-element.302) | copy-start | bytes 6291460 | tf_op jit(solution)/shard_map/while
  139.2 14.0 %copy-start.52 = (bf16[2,1024,8,64]{1,3,2,0:T(8,128)(2,1)S(1)}, bf16[2,1024,8,64]{1,3,2,0:T(8,128)(2,1)}, u32[]{:S(2)}) copy-start(bf16[2,1024,8,64]{1,3,2,0:T(8,128)(2,1)} %get-tuple-element.293) | copy-start | bytes 6291460 | tf_op jit(solution)/shard_map/while
  183.0 13.9 %copy-start.11 = (bf16[2,1024,8,64]{1,3,2,0:T(8,128)(2,1)S(1)}, bf16[2,1024,8,64]{1,3,2,0:T(8,128)(2,1)}, u32[]{:S(2)}) copy-start(bf16[2,1024,8,64]{1,3,2,0:T(8,128)(2,1)} %get-tuple-element.302) | copy-start | bytes 6291460 | tf_op jit(solution)/shard_map/while
  183.0 14.0 %copy-start.52 = (bf16[2,1024,8,64]{1,3,2,0:T(8,128)(2,1)S(1)}, bf16[2,1024,8,64]{1,3,2,0:T(8,128)(2,1)}, u32[]{:S(2)}) copy-start(bf16[2,1024,8,64]{1,3,2,0:T(8,128)(2,1)} %get-tuple-element.293) | copy-start | bytes 6291460 | tf_op jit(solution)/shard_map/while
  213.2 6.6 copy-start
  213.2 6.6 copy-start.23
  352.8 5.5 copy-start.26
  352.8 5.5 copy-start.29
  352.8 5.5 copy-start.32
  352.8 10.8 copy-start.14
  358.4 5.2 copy-start.7
  358.4 5.9 copy-start.10
  373.3 4.1 copy-start.1
  373.4 4.1 copy-start.24
  582.6 4.1 copy-start.18
  586.6 279.6 %reduce-scatter.5.cloned.1.call-start = ((), (), s32[]{:S(2)}) async-start(), calls=%async_computation.8 | async-start | bytes 6488064 | tf_op jit(solution)/shard_map/reduce_scatter | solution.py:315
  586.7 4.7 copy-start.3
  586.7 6.0 copy-start.5
  586.7 6.0 copy-start.16
  586.7 6.0 copy-start.20
  586.7 6.0 copy-start.44
  592.7 6.0 copy-start.13
  601.7 6.5 copy-start.35
  601.7 6.5 copy-start.36
  601.7 6.5 copy-start.37
  601.7 6.5 copy-start.42
  629.9 383.9 %reduce-scatter.9.cloned.1.call-start = ((), (), s32[]{:S(2)}) async-start(), calls=%async_computation.10 | async-start | bytes 8650752 | tf_op jit(solution)/shard_map/reduce_scatter | solution.py:315
  646.0 515.0 %reduce-scatter.11.cloned.1.call-start = ((), (), s32[]{:S(2)}) async-start(), calls=%async_computation.11 | async-start | bytes 8650752 | tf_op jit(solution)/shard_map/reduce_scatter | solution.py:315
  699.1 55.1 %all-to-all-start.1 = ((bf16[2,2,262144]{2,1,0:T(2,128)(2,1)}), bf16[2,2,262144]{2,1,0:T(2,128)(2,1)}, u32[]{:S(2)}, u32[]{:S(2)}) async-start(bf16[2,2,262144]{2,1,0:T(2,128)(2,1)} %reshape.307), calls=%async_computation.1 | async-start | bytes 4194304 | tf_op jit(solution)/shard_map/all_to_all | solution.py:308
  721.8 4.8 copy-start.8
  721.8 6.1 copy-start.9
  751.6 6.4 copy-start.47
  751.6 6.4 copy-start.38
  754.2 79.1 %all-to-all-start.3 = ((bf16[2,2,262144]{2,1,0:T(2,128)(2,1)}), bf16[2,2,262144]{2,1,0:T(2,128)(2,1)S(1)}, u32[]{:S(2)}, u32[]{:S(2)}) async-start(bf16[2,2,262144]{2,1,0:T(2,128)(2,1)} %reshape.305), calls=%async_computation.3 | async-start | bytes 4194304 | tf_op jit(solution)/shard_map/all_to_all | solution.py:308
  (22 other events, 48.2 us)
Sparse Core Ops, SparseCore 0:
  11.0 84.6 all-gather.10
  98.6 55.0 all-gather.12
  156.6 76.4 all-gather.14
  235.7 76.1 all-gather.16
  586.7 135.7 reduce-scatter.6
  724.8 141.3 reduce-scatter.4
  868.6 145.1 reduce-scatter.8
  1016.2 144.7 reduce-scatter.10

commit v2 on v0

--- a/solution.py
+++ b/solution.py
@@ -1,6 +1,10 @@
+import functools
+
 import jax
 import jax.numpy as jnp
 from jax import lax
+from jax.experimental import pallas as pl
+from jax.experimental.pallas import tpu as pltpu
 from jax.sharding import PartitionSpec as P
 
 HD = 64
@@ -290,6 +294,848 @@
     )
 
 
+PAIR = 2 * HD
+F32, BF16 = jnp.float32, jnp.bfloat16
+LIMIT = 60 << 20
+
+
+def nn(a, b):
+    return lax.dot_general(a, b, (((1,), (0,)), ((), ())), preferred_element_type=F32)
+
+
+def nt(a, b):
+    return lax.dot_general(a, b, (((1,), (1,)), ((), ())), preferred_element_type=F32)
+
+
+def stats(value):
+    center = value - jnp.mean(value, -1, keepdims=True)
+    factor = lax.rsqrt(jnp.mean(center * center, -1, keepdims=True) + EPSILON)
+    return center * factor, factor
+
+
+def back(grad_hat, normed, factor):
+    return factor * (
+        grad_hat
+        - jnp.mean(grad_hat, -1, keepdims=True)
+        - normed * jnp.mean(grad_hat * normed, -1, keepdims=True)
+    )
+
+
+def head_mean_matrix(width):
+    row = lax.broadcasted_iota(jnp.int32, (width, width), 0) // HD
+    col = lax.broadcasted_iota(jnp.int32, (width, width), 1) // HD
+    return jnp.where(row == col, 1.0 / HD, 0.0).astype(BF16)
+
+
+def head_mean(value, matrix):
+    high = value.astype(BF16)
+    low = (value - high.astype(F32)).astype(BF16)
+    return nn(high, matrix) + nn(low, matrix)
+
+
+def head_stats(value, matrix):
+    center = value - head_mean(value, matrix)
+    factor = lax.rsqrt(head_mean(center * center, matrix) + EPSILON)
+    return center * factor, factor
+
+
+def head_back(grad_hat, normed, factor, matrix):
+    return factor * (
+        grad_hat - head_mean(grad_hat, matrix) - normed * head_mean(grad_hat * normed, matrix)
+    )
+
+
+QKV_TILE = 256
+
+
+def project_body(per_part, image, norms, gains, w, first, qn, kn, v, q_raw, k_raw, held):
+    step = pl.program_id(0)
+
+    @pl.when(step == 0)
+    def _():
+        rows = image.shape[0] // 4
+
+        def norm(i, _):
+            at = pl.ds(i * rows, rows)
+            hat, _f = stats(image[at].astype(F32))
+            value = (hat * norms[0:1] + norms[2:3]).astype(BF16)
+            held[at] = value
+            first[at] = value
+            return 0
+        lax.fori_loop(0, 4, norm, 0)
+
+    joined = nn(held[...], w[0])
+    part = step // per_part
+    matrix = head_mean_matrix(QKV_TILE)
+
+    @pl.when(part == 0)
+    def _():
+        hat, _f = head_stats(joined, matrix)
+        qn[...] = (hat * gains[0:1] * (HD ** -0.5)).astype(BF16)
+        q_raw[...] = joined.astype(BF16)
+
+    @pl.when(part == 1)
+    def _():
+        hat, _f = head_stats(joined, matrix)
+        kn[...] = (hat * gains[1:2]).astype(BF16)
+        k_raw[...] = joined.astype(BF16)
+
+    @pl.when(part == 2)
+    def _():
+        v[...] = joined.astype(BF16)
+
+
+def project(image, norms, gains, w, cols):
+    length, width = image.shape
+    half = cols // 3
+    per_half = half // QKV_TILE
+    per_part = 2 * per_half
+
+    def w_map(s):
+        part, rest = s // per_part, s % per_part
+        return rest // per_half, 0, part * per_half + rest % per_half
+
+    def out_map(part):
+        return lambda s: (0, jnp.clip(s - part * per_part, 0, per_part - 1))
+
+    block = lambda part: pl.BlockSpec((length, QKV_TILE), out_map(part))
+    full = lambda a: pl.BlockSpec(a.shape, lambda s: (0,) * a.ndim)
+    heads = jax.ShapeDtypeStruct((length, 2 * half), BF16)
+    return pl.pallas_call(
+        functools.partial(project_body, per_part),
+        grid=(3 * per_part,),
+        in_specs=[full(image), full(norms), full(gains), pl.BlockSpec((1, width, QKV_TILE), w_map)],
+        out_specs=[pl.BlockSpec((length, width), lambda s: (0, 0)), block(0), block(1), block(2), block(0), block(1)],
+        out_shape=[jax.ShapeDtypeStruct((length, width), BF16)] + [heads] * 5,
+        scratch_shapes=[pltpu.VMEM((length, width), BF16)],
+        compiler_params=pltpu.CompilerParams(vmem_limit_bytes=LIMIT),
+        name="project",
+    )(image, norms, gains, w)
+
+
+Q_TILE = 256
+
+
+def attend_body(qn, kn, v, mixed, inverse):
+    length = qn.shape[0]
+    lane = lax.broadcasted_iota(jnp.int32, (1, PAIR), 1) < HD
+    keys = kn[...]
+    ones = jnp.ones((length, PAIR), BF16)
+    values = jnp.concatenate([v[...], ones], axis=1)
+    zero = jnp.zeros((), BF16)
+    for i in range(length // Q_TILE):
+        at = slice(i * Q_TILE, (i + 1) * Q_TILE)
+        query = qn[at]
+        got = []
+        for mask in (lane, ~lane):
+            scores = nt(jnp.where(mask, query, zero), keys)
+            got.append(nn(jnp.exp(scores).astype(BF16), values))
+        inv = 1.0 / jnp.where(lane, got[0][:, PAIR:], got[1][:, PAIR:])
+        mixed[at] = (jnp.where(lane, got[0][:, :PAIR], got[1][:, :PAIR]) * inv).astype(BF16)
+        inverse[at] = inv
+
+
+def attend(qn, kn, v):
+    length, width = qn.shape
+    block = pl.BlockSpec((length, PAIR), lambda h: (0, h))
+    return pl.pallas_call(
+        attend_body,
+        grid=(width // PAIR,),
+        in_specs=[block] * 3,
+        out_specs=[block] * 2,
+        out_shape=[jax.ShapeDtypeStruct((length, width), BF16), jax.ShapeDtypeStruct((length, width), F32)],
+        compiler_params=pltpu.CompilerParams(vmem_limit_bytes=LIMIT),
+        name="attend",
+    )(qn, kn, v)
+
+
+def attend_back_body(gains, qn, kn, v, q_raw, k_raw, mixed, grad_mixed, inverse, grad_q, grad_k, grad_v, grad_gains):
+    length = qn.shape[0]
+    first = lax.broadcasted_iota(jnp.int32, (1, PAIR), 1) < HD
+    lanes = lax.broadcasted_iota(jnp.int32, (1, PAIR), 1)
+    zero = jnp.zeros((), BF16)
+    go = grad_mixed[...].astype(F32)
+    inv = inverse[...]
+    product = go * mixed[...].astype(F32) * inv
+    go_inv = (go * inv).astype(BF16)
+    query, keys, values = qn[...], kn[...], v[...]
+    heads = []
+    for h, mask in ((0, first), (1, ~first)):
+        delta = -jnp.sum(jnp.where(mask, product, 0.0), -1, keepdims=True)
+        high = delta.astype(BF16)
+        low = (delta - high.astype(F32)).astype(BF16)
+        spare = (1 - h) * HD
+        grad_aug = jnp.where(mask, go_inv, jnp.where(lanes == spare, high, jnp.where(lanes == spare + 1, low, zero)))
+        values_aug = jnp.where(mask, values, jnp.where((lanes == spare) | (lanes == spare + 1), jnp.ones((), BF16), zero))
+        heads.append((jnp.where(mask, query, zero), jnp.where(mask, keys, zero), jnp.where(mask, go_inv, zero), grad_aug, values_aug))
+    dq = []
+    dk = jnp.zeros((length, PAIR), F32)
+    dv = jnp.zeros((length, PAIR), F32)
+    for i in range(length // Q_TILE):
+        at = slice(i * Q_TILE, (i + 1) * Q_TILE)
+        part = jnp.zeros((Q_TILE, PAIR), F32)
+        for qm, km, gm, ga, va in heads:
+            exponent = jnp.exp(nt(km, qm[at]))
+            grad_scores = (exponent * nt(va, ga[at])).astype(BF16)
+            dv = dv + nn(exponent.astype(BF16), gm[at])
+            dk = dk + nn(grad_scores, qm[at])
+            part = part + lax.dot_general(grad_scores, km, (((0,), (0,)), ((), ())), preferred_element_type=F32)
+        dq.append(part)
+    dq = jnp.concatenate(dq, axis=0)
+    grad_v[...] = dv.astype(BF16)
+    matrix = head_mean_matrix(PAIR)
+    hat, factor = head_stats(q_raw[...].astype(F32), matrix)
+    scale = HD ** -0.5
+    sum_q = jnp.sum(dq * hat, 0, keepdims=True) * scale
+    grad_q[...] = head_back(dq * gains[0:1] * scale, hat, factor, matrix).astype(BF16)
+    hat, factor = head_stats(k_raw[...].astype(F32), matrix)
+    sum_k = jnp.sum(dk * hat, 0, keepdims=True)
+    grad_k[...] = head_back(dk * gains[1:2], hat, factor, matrix).astype(BF16)
+
+    @pl.when(pl.program_id(0) == 0)
+    def _():
+        grad_gains[...] = jnp.zeros_like(grad_gains)
+    grad_gains[...] += jnp.concatenate([sum_q, sum_k], axis=0)
+
+
+def attend_back(gains, qn, kn, v, q_raw, k_raw, mixed, grad_mixed, inverse):
+    length, width = qn.shape
+    block = pl.BlockSpec((length, PAIR), lambda h: (0, h))
+    same = pl.BlockSpec((2, PAIR), lambda h: (0, 0))
+    heads = jax.ShapeDtypeStruct((length, width), BF16)
+    return pl.pallas_call(
+        attend_back_body,
+        grid=(width // PAIR,),
+        in_specs=[same] + [block] * 8,
+        out_specs=[block] * 3 + [same],
+        out_shape=[heads] * 3 + [jax.ShapeDtypeStruct((2, PAIR), F32)],
+        compiler_params=pltpu.CompilerParams(vmem_limit_bytes=LIMIT),
+        name="attend_back",
+    )(gains, qn, kn, v, q_raw, k_raw, mixed, grad_mixed, inverse)
+
+
+ROWS = 256
+
+
+def branch_body(image, norms, mixed, w, middle, second):
+    half = w.shape[2]
+    value = image[...].astype(F32) + nt(mixed[:, :half], w[0]) + nt(mixed[:, half:], w[1])
+    middle[...] = value
+    hat, _f = stats(value)
+    second[...] = (hat * norms[1:2] + norms[3:4]).astype(BF16)
+
+
+def branch(image, norms, mixed, w):
+    length, width = image.shape
+    row = pl.BlockSpec((ROWS, width), lambda i: (i, 0))
+    full = lambda a: pl.BlockSpec(a.shape, lambda s: (0,) * a.ndim)
+    return pl.pallas_call(
+        branch_body,
+        grid=(length // ROWS,),
+        in_specs=[row, full(norms), row, full(w)],
+        out_specs=[row, row],
+        out_shape=[jax.ShapeDtypeStruct((length, width), F32), jax.ShapeDtypeStruct((length, width), BF16)],
+        compiler_params=pltpu.CompilerParams(vmem_limit_bytes=LIMIT),
+        name="branch",
+    )(image, norms, mixed, w)
+
+
+FF_TILE = 512
+
+
+def gelu_parts(v):
+    bell = jnp.exp(v * v * -0.5)
+    t = 1.0 / (1.0 + (0.3275911 * 0.7071067811865476) * jnp.abs(v))
+    poly = t * (0.127414796 + t * (-0.142248368 + t * (0.7107068705 + t * (-0.7265760135 + t * 0.5307027145))))
+    tail = poly * bell
+    return jnp.where(v >= 0, 1.0 - tail, tail), bell * 0.3989422804014327
+
+
+def feed_body(second, cot, middle, up, down, result, grad_second, grad_up, grad_down, acc, second_t, cot_t, active, grad_hidden):
+    step = pl.program_id(0)
+    length = second.shape[0]
+
+    @pl.when(step == 0)
+    def _():
+        second_t[...] = second[...].T
+        cot_t[...] = cot[...].T
+        acc[...] = middle[...]
+        grad_second[...] = jnp.zeros_like(grad_second)
+
+    w_up, w_down = up[0], down[0]
+    for i in range(length // ROWS):
+        at = slice(i * ROWS, (i + 1) * ROWS)
+        hidden = nn(second[at], w_up)
+        grad_active = nn(cot[at], w_down)
+        cumulative, density = gelu_parts(hidden)
+        a = (hidden * cumulative).astype(BF16)
+        g = (grad_active * (cumulative + hidden * density)).astype(BF16)
+        active[at] = a
+        grad_hidden[at] = g
+        acc[at] += nt(a, w_down)
+        grad_second[at] += nt(g, w_up)
+    grad_up[0] = nn(second_t[...], grad_hidden[...]).astype(BF16)
+    grad_down[0] = nn(cot_t[...], active[...]).astype(BF16)
+
+    @pl.when(step == pl.num_programs(0) - 1)
+    def _():
+        result[...] = acc[...].astype(BF16)
+
+
+def feed(second, cot, middle, up, down):
+    length, width = second.shape
+    per_half = up.shape[2] // FF_TILE
+    full = lambda a: pl.BlockSpec(a.shape, lambda s: (0,) * a.ndim, pipeline_mode=pl.Buffered(1))
+    tile = pl.BlockSpec((1, width, FF_TILE), lambda s: (s // per_half, 0, s % per_half))
+    out = lambda: pl.BlockSpec((length, width), lambda s: (0, 0), pipeline_mode=pl.Buffered(1))
+    return pl.pallas_call(
+        feed_body,
+        grid=(2 * per_half,),
+        in_specs=[full(second), full(cot), full(middle), tile, tile],
+        out_specs=[out(), out(), tile, tile],
+        out_shape=[
+            jax.ShapeDtypeStruct((length, width), BF16),
+            jax.ShapeDtypeStruct((length, width), F32),
+            jax.ShapeDtypeStruct(up.shape, BF16),
+            jax.ShapeDtypeStruct(down.shape, BF16),
+        ],
+        scratch_shapes=[
+            pltpu.VMEM((length, width), F32),
+            pltpu.VMEM((width, length), BF16),
+            pltpu.VMEM((width, length), BF16),
+            pltpu.VMEM((length, FF_TILE), BF16),
+            pltpu.VMEM((length, FF_TILE), BF16),
+        ],
+        compiler_params=pltpu.CompilerParams(vmem_limit_bytes=LIMIT),
+        name="feed",
+    )(second, cot, middle, up, down)
+
+
+def branch_back_body(norms, cot, grad_second, middle, mixed, w, grad_middle, grad_mixed, grad_w, sums, acc):
+    step = pl.program_id(0)
+    half = w.shape[2]
+
+    @pl.when(step == 0)
+    def _():
+        sums[...] = jnp.zeros_like(sums)
+        acc[...] = jnp.zeros_like(acc)
+    hat, factor = stats(middle[...])
+    gs = grad_second[...]
+    gm = cot[...].astype(F32) + back(gs * norms[1:2], hat, factor)
+    grad_middle[...] = gm
+    branch_grad = gm.astype(BF16)
+    branch_t = branch_grad.T
+    for t in range(2):
+        at = slice(t * half, (t + 1) * half)
+        grad_mixed[:, at] = nn(branch_grad, w[t]).astype(BF16)
+        acc[t] += nn(branch_t, mixed[:, at])
+    sums[0:1] += jnp.sum(gs * hat, 0, keepdims=True)
+    sums[1:2] += jnp.sum(gs, 0, keepdims=True)
+
+    @pl.when(step == pl.num_programs(0) - 1)
+    def _():
+        grad_w[...] = acc[...].astype(BF16)
+
+
+def branch_back(norms, cot, grad_second, middle, mixed, w):
+    length, width = middle.shape
+    row = pl.BlockSpec((ROWS, width), lambda i: (i, 0))
+    full = lambda shape: pl.BlockSpec(shape, lambda s: (0,) * len(shape))
+    return pl.pallas_call(
+        branch_back_body,
+        grid=(length // ROWS,),
+        in_specs=[full(norms.shape), row, row, row, row, full(w.shape)],
+        out_specs=[row, row, full(w.shape), full((2, width))],
+        out_shape=[
+            jax.ShapeDtypeStruct((length, width), F32),
+            jax.ShapeDtypeStruct((length, width), BF16),
+            jax.ShapeDtypeStruct(w.shape, BF16),
+            jax.ShapeDtypeStruct((2, width), F32),
+        ],
+        scratch_shapes=[pltpu.VMEM(w.shape, F32)],
+        compiler_params=pltpu.CompilerParams(vmem_limit_bytes=LIMIT),
+        name="branch_back",
+    )(norms, cot, grad_second, middle, mixed, w)
+
+
+def project_back_body(norms, image, first, grad_middle, gq, gk, gv, w, grad_w, grad_image, sums, acc, first_t):
+    step = pl.program_id(0)
+    length = image.shape[0]
+    half = w.shape[2] // 3
+
+    @pl.when(step == 0)
+    def _():
+        first_t[...] = first[...].T
+        acc[...] = jnp.zeros_like(acc)
+    for part, g in enumerate((gq, gk, gv)):
+        at = slice(part * half, (part + 1) * half)
+        grad_w[0, :, at] = nn(first_t[...], g[...]).astype(BF16)
+        acc[...] += nt(g[...], w[0, :, at])
+
+    @pl.when(step == 1)
+    def _():
+        sum_hat = jnp.zeros((1, image.shape[1]), F32)
+        sum_all = jnp.zeros((1, image.shape[1]), F32)
+        for i in range(length // ROWS):
+            at = slice(i * ROWS, (i + 1) * ROWS)
+            hat, factor = stats(image[at].astype(F32))
+            gf = acc[at]
+            grad_image[at] = (grad_middle[at] + back(gf * norms[0:1], hat, factor)).astype(BF16)
+            sum_hat = sum_hat + jnp.sum(gf * hat, 0, keepdims=True)
+            sum_all = sum_all + jnp.sum(gf, 0, keepdims=True)
+        sums[0:1] = sum_hat
+        sums[1:2] = sum_all
+
+
+def project_back(norms, image, first, grad_middle, gq, gk, gv, w, cols):
+    length, width = image.shape
+    half = cols // 3
+    full = lambda shape: pl.BlockSpec(shape, lambda s: (0,) * len(shape), pipeline_mode=pl.Buffered(1))
+    strip = pl.BlockSpec((length, half), lambda s: (0, s))
+    weight = pl.BlockSpec((1, width, 3 * half), lambda s: (s, 0, 0))
+    return pl.pallas_call(
+        project_back_body,
+        grid=(2,),
+        in_specs=[full(norms.shape), full(image.shape), full(first.shape), full(grad_middle.shape), strip, strip, strip, weight],
+        out_specs=[weight, full(image.shape), full((2, width))],
+        out_shape=[
+            jax.ShapeDtypeStruct((2, width, cols), BF16),
+            jax.ShapeDtypeStruct((length, width), BF16),
+            jax.ShapeDtypeStruct((2, width), F32),
+        ],
+        scratch_shapes=[pltpu.VMEM((length, width), F32), pltpu.VMEM((width, length), BF16)],
+        compiler_params=pltpu.CompilerParams(vmem_limit_bytes=LIMIT),
+        name="project_back",
+    )(norms, image, first, grad_middle, gq, gk, gv, w)
+
+
+MESH = pl.DeviceIdType.MESH
+
+
+class Place:
+    def __init__(self, zs):
+        f = lax.axis_index("fsdp")
+        self.zs = zs
+        self.x = lax.axis_index("tensor")
+        self.c = lax.rem(f, 2)
+        self.y = lax.rem(lax.div(f, 2), 2)
+        self.z = lax.div(f, 4)
+
+    def dev(self, z=None, y=None, c=None, x=None):
+        z = self.z if z is None else z
+        y = self.y if y is None else y
+        c = self.c if c is None else c
+        x = self.x if x is None else x
+        return {"fsdp": (z * 2 + y) * 2 + c, "tensor": x}
+
+    def peers(self):
+        out = [self.dev(z=lax.rem(self.z + k, self.zs)) for k in range(1, self.zs)]
+        return out + [self.dev(y=1 - self.y), self.dev(c=1 - self.c), self.dev(x=1 - self.x)]
+
+
+def meet(place):
+    barrier = pltpu.get_barrier_semaphore()
+    peers = place.peers()
+    for peer in peers:
+        pl.semaphore_signal(barrier, inc=1, device_id=peer, device_id_type=MESH)
+    pl.semaphore_wait(barrier, len(peers))
+
+
+def remote(src, dst, send, recv, peer):
+    return pltpu.make_async_remote_copy(
+        src_ref=src, dst_ref=dst, send_sem=send, recv_sem=recv, device_id=peer, device_id_type=MESH
+    )
+
+
+class Gather:
+    def __init__(self, place, shard, whole, cols, order, send, recv):
+        p = self.p = place
+        self.shard = shard.at[:, cols]
+        self.whole = whole
+        self.cols = cols
+        self.order = order
+        self.send, self.recv = send, recv
+        self.used = 0
+        self.stages = [self.stage(i) for i in range(3)]
+        self.cores = [self.core_parts(i) for i in range(3)]
+        self.own = pltpu.make_async_copy(self.shard, self.at({}), self.send.at[self.used])
+
+    def at(self, index):
+        p = self.p
+        own = {"x": p.x, "y": p.y, "z": p.z}
+        x, y, z = (index.get(d, own[d]) for d in "xyz")
+        return self.whole.at[x, z, y, p.c, :, self.cols]
+
+    def copy(self, src, dst, peer):
+        n = self.used
+        self.used += 1
+        return remote(src, dst, self.send.at[n], self.recv.at[n], peer)
+
+    def others(self, d):
+        p = self.p
+        if d == "z":
+            return [lax.rem(p.z + k, p.zs) for k in range(1, p.zs)]
+        return [1 - getattr(p, d)]
+
+    def stage(self, i):
+        d = self.order[i]
+        held = self.at({e: slice(None) for e in self.order[:i]})
+        src = self.shard if i == 0 else held
+        return [self.copy(src, held, self.p.dev(**{d: to})) for to in self.others(d)]
+
+    def core_parts(self, i):
+        done = {e: slice(None) for e in self.order[:i]}
+        d = self.order[i]
+        peer = self.p.dev(c=1 - self.p.c)
+        if i == 0:
+            refs = [self.at({d: slice(None)})]
+        else:
+            refs = [self.at({**done, d: to}) for to in self.others(d)]
+        return [self.copy(ref, ref, peer) for ref in refs]
+
+    def tick0(self):
+        self.own.start()
+        for copy in self.stages[0]:
+            copy.start()
+
+    def tick(self, i):
+        if i == 1:
+            self.own.wait()
+        for copy in self.stages[i - 1]:
+            copy.wait()
+        if i < 3:
+            for copy in self.stages[i]:
+                copy.start()
+        for copy in self.cores[i - 1]:
+            copy.start()
+
+    def tick1(self):
+        self.tick(1)
+
+    def tick2(self):
+        self.tick(2)
+
+    def tick3(self):
+        self.tick(3)
+
+    def tick4(self):
+        for part in self.cores:
+            for copy in part:
+                copy.wait()
+
+
+def sems_for(zs):
+    return 2 * zs + 8
+
+
+class Swap:
+    def __init__(self, place, value, image, sems):
+        p = self.p = place
+        half = value.shape[1]
+        rows = pl.ds(pl.multiple_of(p.x * half, half), half)
+        self.copy = remote(value.at[1 - p.x], image.at[rows], sems.at[0], sems.at[1], p.dev(x=1 - p.x))
+        self.mine = pltpu.make_async_copy(value.at[p.x], image.at[rows], sems.at[2])
+
+    def start(self):
+        self.copy.start()
+        self.mine.start()
+
+    def wait(self):
+        self.copy.wait()
+        self.mine.wait()
+
+
+def gather_kernel(zs, groups, n_w, n_swap, *refs):
+    shards = refs[:n_w]
+    values = refs[n_w:n_w + n_swap]
+    wholes = refs[n_w + n_swap:2 * n_w + n_swap]
+    images = refs[2 * n_w + n_swap:2 * n_w + 2 * n_swap]
+    send, recv, swap_sem = refs[2 * n_w + 2 * n_swap:]
+    p = Place(zs)
+    meet(p)
+    swaps = [Swap(p, values[i], images[i], swap_sem.at[i]) for i in range(n_swap)]
+    gs = [Gather(p, shards[w], wholes[w], pl.ds(lo, n), order, send.at[i], recv.at[i])
+          for i, (w, lo, n, order) in enumerate(groups)]
+    if swaps:
+        swaps[0].start()
+    n = len(gs)
+    for t in range(n + 4):
+        for k, tick in ((0, "tick0"), (1, "tick1"), (2, "tick2"), (3, "tick3"), (4, "tick4")):
+            if 0 <= t - k < n:
+                getattr(gs[t - k], tick)()
+        if t == 1:
+            for s in swaps[1:]:
+                s.start()
+    for s in swaps:
+        s.wait()
+
+
+def gather_all(shards, values, groups, zs, collective_id):
+    n_w, n_s = len(shards), len(values)
+    out = [jax.ShapeDtypeStruct((2, zs, 2, 2) + s.shape, s.dtype) for s in shards]
+    out += [jax.ShapeDtypeStruct((v.shape[0] * v.shape[1], v.shape[2]), v.dtype) for v in values]
+    got = pl.pallas_call(
+        functools.partial(gather_kernel, zs, groups, n_w, n_s),
+        out_shape=out,
+        in_specs=[pl.BlockSpec(memory_space=pl.ANY)] * (n_w + n_s),
+        out_specs=[pl.BlockSpec(memory_space=pl.ANY)] * (n_w + n_s),
+        scratch_shapes=[
+            pltpu.SemaphoreType.DMA((len(groups), sems_for(zs))),
+            pltpu.SemaphoreType.DMA((len(groups), sems_for(zs))),
+            pltpu.SemaphoreType.DMA((max(n_s, 1), 3)),
+        ],
+        compiler_params=pltpu.CompilerParams(collective_id=collective_id, has_side_effects=True),
+        name="gather_weights",
+    )(*shards, *values)
+    return got[:n_w], got[n_w:]
+
+
+class Scatter:
+    def __init__(self, place, grad, cols, order, a, b, b1, b2, b3, send, recv):
+        self.p = place
+        self.grad, self.cols, self.order = grad, cols, order
+        self.a, self.b, self.b1, self.b2, self.b3 = a, b, b1, b2, b3
+        self.send, self.recv = send, recv
+
+    def load(self):
+        p = self.p
+        return pltpu.make_async_copy(self.grad.at[:, :, :, p.c, :, self.cols], self.a, self.send.at[p.zs + 2])
+
+    def core(self):
+        p = self.p
+        return remote(self.grad.at[:, :, :, 1 - p.c, :, self.cols], self.b, self.send.at[0], self.recv.at[0], p.dev(c=1 - p.c))
+
+    def first(self):
+        p = self.p
+        if self.order == "x":
+            return remote(self.a.at[1 - p.x], self.b1, self.send.at[1], self.recv.at[1], p.dev(x=1 - p.x))
+        return remote(self.a.at[:, :, 1 - p.y], self.b1, self.send.at[1], self.recv.at[1], p.dev(y=1 - p.y))
+
+    def second(self):
+        p = self.p
+        if self.order == "x":
+            return remote(self.a.at[p.x, :, 1 - p.y], self.b2, self.send.at[2], self.recv.at[2], p.dev(y=1 - p.y))
+        return remote(self.a.at[1 - p.x, :, p.y], self.b2, self.send.at[2], self.recv.at[2], p.dev(x=1 - p.x))
+
+    def z_copies(self):
+        p = self.p
+        out = []
+        for k in range(1, p.zs):
+            to = lax.rem(p.z + k, p.zs)
+            out.append(remote(self.a.at[p.x, to, p.y], self.b3.at[k - 1], self.send.at[2 + k], self.recv.at[2 + k], p.dev(z=to)))
+        return out
+
+
+def add_loop(count, body):
+    lax.fori_loop(0, count, lambda i, _: (body(i), 0)[1], 0)
+
+
+class SwapBack:
+    def __init__(self, place, value, out, sems):
+        p = place
+        half = out.shape[1]
+        to = pl.ds(pl.multiple_of((1 - p.x) * half, half), half)
+        rows = pl.ds(pl.multiple_of(p.x * half, half), half)
+        self.copy = remote(value.at[to], out.at[p.x], sems.at[0], sems.at[1], p.dev(x=1 - p.x))
+        self.mine = pltpu.make_async_copy(value.at[rows], out.at[p.x], sems.at[2])
+
+    def start(self):
+        self.copy.start()
+        self.mine.start()
+
+    def wait(self):
+        self.copy.wait()
+        self.mine.wait()
+
+
+class Sum:
+    def __init__(self, place, value, total, got, send, recv):
+        self.p, self.value, self.total, self.got, self.send, self.recv = place, value, total, got, send, recv
+
+    def copies(self, i):
+        p = self.p
+        if i < 3:
+            peers = [(p.dev(c=1 - p.c), p.dev(x=1 - p.x), p.dev(y=1 - p.y))[i]]
+        else:
+            peers = [p.dev(z=lax.rem(p.z + k, p.zs)) for k in range(1, p.zs)]
+        return [remote(self.total, self.got.at[i + k], self.send.at[i + k], self.recv.at[i + k], peer)
+                for k, peer in enumerate(peers)]
+
+    def start(self, i):
+        for copy in self.copies(i):
+            copy.start()
+
+    def finish(self, i):
+        copies = self.copies(i)
+        for copy in copies:
+            copy.wait()
+        total = self.total[...]
+        for k in range(len(copies)):
+            total = total + self.got[i + k]
+        self.total[...] = total
+
+
+def scatter_kernel(zs, groups, n_w, n_s, *refs):
+    grads = refs[:n_w]
+    values = refs[n_w:n_w + n_s]
+    small = refs[n_w + n_s]
+    outs = refs[n_w + n_s + 1:2 * n_w + n_s + 1]
+    backs = refs[2 * n_w + n_s + 1:2 * n_w + 2 * n_s + 1]
+    total = refs[2 * n_w + 2 * n_s + 1]
+    rest = refs[2 * n_w + 2 * n_s + 2:]
+    n = len(groups)
+    bufs = [rest[5 * i:5 * i + 5] for i in range(n)]
+    send, recv, swap_sem, got, sum_send, sum_recv = rest[5 * n:]
+    p = Place(zs)
+    meet(p)
+    gs = [Scatter(p, grads[w], pl.ds(lo, m), order, *bufs[i], send.at[i], recv.at[i])
+          for i, (w, lo, m, order) in enumerate(groups)]
+    swaps = [SwapBack(p, values[i], backs[i], swap_sem.at[i]) for i in range(n_s)]
+    total[...] = small[...]
+    sums = Sum(p, small, total, got, sum_send, sum_recv)
+
+    def t0(i):
+        gs[i].load().start()
+        gs[i].core().start()
+
+    def t1(i):
+        g = gs[i]
+        g.load().wait()
+        g.core().wait()
+
+        def add(j):
+            x, z, y = lax.div(j, 2 * zs), lax.rem(lax.div(j, 2), zs), lax.rem(j, 2)
+            g.a[x, z, y] = g.a[x, z, y] + g.b[x, z, y]
+        add_loop(4 * zs, add)
+        g.first().start()
+
+    def t2(i):
+        g = gs[i]
+        g.first().wait()
+
+        def add(j):
+            if g.order == "x":
+                z, y = lax.div(j, 2), lax.rem(j, 2)
+                g.a[p.x, z, y] = g.a[p.x, z, y] + g.b1[z, y]
+            else:
+                x, z = lax.div(j, zs), lax.rem(j, zs)
+                g.a[x, z, p.y] = g.a[x, z, p.y] + g.b1[x, z]
+        add_loop(2 * zs, add)
+        g.second().start()
+
+    def t3(i):
+        g = gs[i]
+        g.second().wait()
+
+        def add(z):
+            g.a[p.x, z, p.y] = g.a[p.x, z, p.y] + g.b2[z]
+        add_loop(zs, add)
+        for copy in g.z_copies():
+            copy.start()
+
+    def t4(i):
+        g = gs[i]
+        w, lo, m, order = groups[i]
+        for copy in g.z_copies():
+            copy.wait()
+        value = g.a[p.x, p.z, p.y].astype(jnp.float32)
+        for k in range(zs - 1):
+            value = value + g.b3[k].astype(jnp.float32)
+        outs[w][:, lo:lo + m] = value
+
+    for t in range(n + 4):
+        for k, tick in ((0, t0), (4, t4), (3, t3), (2, t2), (1, t1)):
+            if 0 <= t - k < n:
+                tick(t - k)
+        if t < 4:
+            sums.start(t)
+        if t < len(swaps):
+            swaps[t].start()
+        if t < 4:
+            sums.finish(t)
+    for s in swaps:
+        s.wait()
+
+
+def scatter_all(grads, values, small, groups, zs, collective_id):
+    n_w, n_s = len(grads), len(values)
+    rows = grads[0].shape[4]
+    scratch = []
+    for w, lo, m, order in groups:
+        first = (zs, 2, rows, m) if order == "x" else (2, zs, rows, m)
+        for shape in ((2, zs, 2, rows, m), (2, zs, 2, rows, m), first, (zs, rows, m), (zs - 1, rows, m)):
+            scratch.append(pltpu.VMEM(shape, jnp.bfloat16))
+    scratch += [pltpu.SemaphoreType.DMA((len(groups), zs + 3)), pltpu.SemaphoreType.DMA((len(groups), zs + 3))]
+    scratch += [pltpu.SemaphoreType.DMA((n_s, 3)), pltpu.VMEM((zs + 2,) + small.shape, jnp.float32)]
+    scratch += [pltpu.SemaphoreType.DMA((zs + 2,)), pltpu.SemaphoreType.DMA((zs + 2,))]
+    vmem = pl.BlockSpec(memory_space=pltpu.VMEM)
+    hbm = pl.BlockSpec(memory_space=pl.ANY)
+    got = pl.pallas_call(
+        functools.partial(scatter_kernel, zs, groups, n_w, n_s),
+        out_shape=[jax.ShapeDtypeStruct(g.shape[4:], jnp.float32) for g in grads]
+        + [jax.ShapeDtypeStruct((2, v.shape[0] // 2, v.shape[1]), v.dtype) for v in values]
+        + [jax.ShapeDtypeStruct(small.shape, jnp.float32)],
+        in_specs=[hbm] * (n_w + n_s) + [vmem],
+        out_specs=[vmem] * n_w + [hbm] * n_s + [vmem],
+        scratch_shapes=scratch,
+        compiler_params=pltpu.CompilerParams(collective_id=collective_id, has_side_effects=True, vmem_limit_bytes=60 << 20),
+        name="scatter_grads",
+    )(*grads, *values, small)
+    return got[:n_w], got[n_w:n_w + n_s], got[-1]
+
+
+GATHERS = ((0, 0, 768, "zyx"), (0, 768, 896, "zxy"), (1, 0, 512, "zyx"), (2, 0, 1024, "zxy"), (2, 1024, 1024, "zyx"),
+           (3, 0, 1024, "zxy"), (3, 1024, 1024, "zyx"))
+SCATTERS = ((3, 0, 1024, "x"), (3, 1024, 1024, "y"), (2, 0, 1024, "x"), (2, 1024, 1024, "y"), (1, 0, 512, "x"),
+            (0, 0, 768, "y"), (0, 768, 768, "x"))
+
+
+def whole_images(tokens, cotangent, w_qkv, wo_t, w_up, w_down_t, norm_gains, norm_shifts, qk_gains):
+    zs = lax.axis_size("fsdp") // 4
+    rows = w_qkv.shape[0]
+    width = tokens.shape[2]
+    cols = 3 * w_qkv.shape[2]
+    side = jnp.concatenate([norm_gains, norm_shifts, jnp.zeros((rows, 124), BF16)], axis=1)
+    shards = (jnp.concatenate([w_qkv.reshape(rows, cols), side], axis=1), wo_t, w_up, w_down_t)
+    wholes, (image, cot) = gather_all(shards, (tokens, cotangent), GATHERS, zs, 0)
+    qkv, out_w, up, down = (w.reshape(2, width, w.shape[5]) for w in wholes)
+    norms = qkv[0, :, cols:cols + 4].T.astype(F32)
+    gains = qk_gains.astype(F32)
+
+    first, qn, kn, v, q_raw, k_raw = project(image, norms, jnp.tile(gains, (1, QKV_TILE // HD)), qkv, cols)
+    mixed, inverse = attend(qn, kn, v)
+    middle, second = branch(image, norms, mixed, out_w)
+    result, grad_second, grad_up, grad_down = feed(second, cot, middle, up, down)
+    grad_middle, grad_mixed, grad_out_w, sums_second = branch_back(norms, cot, grad_second, middle, mixed, out_w)
+    grad_q, grad_k, grad_v, sums_qk = attend_back(
+        jnp.tile(gains, (1, 2)), qn, kn, v, q_raw, k_raw, mixed, grad_mixed, inverse
+    )
+    grad_qkv, grad_image, sums_first = project_back(norms, image, first, grad_middle, grad_q, grad_k, grad_v, qkv, cols)
+
+    sums_qk = jnp.pad((sums_qk[:, :HD] + sums_qk[:, HD:]).reshape(1, 2 * HD), ((0, 3), (0, width - 2 * HD)))
+    small = jnp.concatenate([sums_first, sums_second, sums_qk], axis=0)
+    grads = [g.reshape((2, zs, 2, 2, rows, g.shape[2])) for g in (grad_qkv, grad_out_w, grad_up, grad_down)]
+    grads, (outputs, grad_tokens), small = scatter_all(grads, (result, grad_image), small, SCATTERS, zs, 1)
+    mine = lax.dynamic_slice_in_dim(small, lax.axis_index("fsdp") * rows, rows, 1)
+    return (
+        outputs,
+        grad_tokens.astype(F32),
+        grads[0].reshape(w_qkv.shape),
+        grads[1],
+        grads[2],
+        grads[3],
+        jnp.stack([mine[0], mine[2]], 1),
+        jnp.stack([mine[1], mine[3]], 1),
+        small[4, :2 * HD].reshape(2, HD),
+    )
+
+
+def layer(tokens, *rest):
+    if tokens.shape[0] == lax.axis_size("tensor") == 2 and lax.axis_size("fsdp") % 4 == 0:
+        return whole_images(tokens, *rest)
+    return per_device(tokens, *rest)
+
+
 def solution(mesh):
     in_specs = (
         P("fsdp", "tensor", None),
@@ -314,5 +1160,5 @@
         P(),
     )
     return jax.shard_map(
-        per_device, mesh=mesh, in_specs=in_specs, out_specs=out_specs, check_vma=False
-    )
+        layer, mesh=mesh, in_specs=in_specs, out_specs=out_specs, check_vma=False
+    )

time: 1570 us -> 661 us (0.42)
  waiting for transfers between devices: 826 us -> 0 us
  Pallas kernels: 0 us -> 641 us
  matrix products: 334 us -> 0 us
  other arithmetic: 158 us -> 7.18 us
  blocking collectives: 119 us -> 0 us
  local copies, waits for them, and re-layouts: 104 us -> 11.9 us
    pallas_call x0 -> x9, Pallas kernels: none -> 641 us  [the longest x1 236 us: scatter_all(): pl.pallas_call(functools.partial(scatter_kernel, zs, groups, n_w, n_s), o...]
    reduce_scatter x12 -> x0, waiting for transfers between devices: 430 us -> none  [the longest x2 108 us: forward(): lax.psum_scatter(contract_cols(mixed, whole_out), 'tensor', scatter_dimen...]
    all_gather x16 -> x0, waiting for transfers between devices: 391 us -> none  [the longest x2 105 us: fetch(): lax.all_gather(w_down_t, 'fsdp', axis=0, tiled=True)]
    dot_general x52 -> x0, matrix products: 334 us -> none  [the longest x8 57.1 us: contract_rows(): lax.dot_general(left, right, (((0,), (0,)), ((), ())), preferred_element_...]
    all_gather x4 -> x0, blocking collectives: 79.5 us -> none  [the longest x2 44.6 us: fetch(): lax.all_gather(norm_gains, 'fsdp', axis=0, tiled=True)]
    convert_element_type x29 -> x2, other arithmetic: 81.2 us -> 5.2 us  [the longest x1 4.22 us: whole_images(): grad_tokens.astype(F32)]
    while x276 -> x0, local copies, waits for them, and re-layouts: 64.3 us -> none
    reduce_sum x24 -> x0, other arithmetic: 57.9 us -> none  [the longest x4 14.1 us: attend(): total_sum = jnp.sum(exponent, -1, keepdims=True)]
  transfers between devices with their start and end apart: 28 -> 0, of which waited for: 23 -> 0; matrix products, arithmetic and copies ran while one was open for 30% -> 0% of each run, Pallas kernels for 0% -> 0%
where the time goes in v2:
time: 661 us
  Pallas kernels  641 us (97%)
  local copies, waits for them, and re-layouts  11.9 us (2%)
  other arithmetic  7.18 us (1%)
    pallas_call x1, Pallas kernels, scatter_all(): pl.pallas_call(functools.partial(scatter_kernel, zs, groups, n_w, n_s), o...  236 us
    pallas_call x1, Pallas kernels, gather_all(): pl.pallas_call(functools.partial(gather_kernel, zs, groups, n_w, n_s), ou...  181 us
    pallas_call x1, Pallas kernels, feed(): pl.pallas_call(feed_body, grid=(2 * per_half,), in_specs=[full(second), f...  69.3 us
    pallas_call x1, Pallas kernels, attend_back(): pl.pallas_call(attend_back_body, grid=(width // PAIR,), in_specs=[same] +...  60.7 us
    pallas_call x1, Pallas kernels, project_back(): pl.pallas_call(project_back_body, grid=(2,), in_specs=[full(norms.shape),...  25.7 us
    pallas_call x1, Pallas kernels, project(): pl.pallas_call(functools.partial(project_body, per_part), grid=(3 * per_p...  24.9 us
    pallas_call x1, Pallas kernels, attend(): pl.pallas_call(attend_body, grid=(width // PAIR,), in_specs=[block] * 3,...  22 us
    pallas_call x1, Pallas kernels, branch_back(): pl.pallas_call(branch_back_body, grid=(length // ROWS,), in_specs=[full(n...  13.5 us

profile of v2, /device:TPU:0, one launch (start us, length us, event | category | flops | bytes accessed | tf_op | source)
XLA Modules:
  0.0 660.7 jit_solution(13761826139849420581)
XLA Ops:
  0.6 0.9 copy.35
  1.6 0.8 copy.27
  2.3 0.8 copy.28
  3.1 0.8 concatenate.6.refs_0_
  3.9 0.0 copy-start.7
  3.9 180.9 %gather_weights.1 = (bf16[2,4,2,2,64,1664]{5,4,3,2,1,0:T(8,128)(2,1)}, bf16[2,4,2,2,64,512]{5,4,3,2,1,0:T(8,128)(2,1)}, bf16[2,4,2,2,64,2048]{5,4,3,2,1,0:T(8,12...) custom-call(bf16[64,1664]{1,0:T(8,128)(2,1)} %concatenate.6.refs_0_, ...), custom_call_target="tpu_custom_call" | custom-call | tf_op jit(solution)/shard_map/gather_weights/pallas_call | solution.py:877
  184.8 1.0 convert_bitcast_fusion
  185.8 0.8 copy.32.norms
  186.6 0.0 copy-done.7
  186.6 0.7 tile.9.gains
  187.3 24.9 %project.1 = (bf16[1024,1024]{1,0:T(8,128)(2,1)}, bf16[1024,1024]{1,0:T(8,128)(2,1)}, bf16[1024,1024]{1,0:T(8,128)(2,1)}, bf16[1024,1024]{1,0:T(8,128)(2,1)}, bf...) custom-call(bf16[1024,1024]{1,0:T(8,128)(2,1)} %get-tuple-element.48.image, f32[4,1024]{1,0:T(4,128)} %copy.32.norms, ...), custom_call_target="tpu_custom_call" | custom-call | tf_op jit(solution)/shard_map/project/pallas_call | solution.py:404
  212.2 22.0 %attend.1 = (bf16[1024,1024]{1,0:T(8,128)(2,1)}, f32[1024,1024]{1,0:T(8,128)}) custom-call(bf16[1024,1024]{1,0:T(8,128)(2,1)} %get-tuple-element.51.qn, bf16[1024,1024]{1,0:T(8,128)(2,1)} %get-tuple-element.52.kn, bf16[1024,1024]{1,0:T(8,128)(2,1)} %get-tuple-element.53.v), custom_call_target="tpu_custom_call" | custom-call | tf_op jit(solution)/shard_map/attend/pallas_call | solution.py:441
  234.2 7.5 %branch.1 = (f32[1024,1024]{1,0:T(8,128)}, bf16[1024,1024]{1,0:T(8,128)(2,1)}) custom-call(bf16[1024,1024]{1,0:T(8,128)(2,1)} %get-tuple-element.48.image, f32[4,1024]{1,0:T(4,128)} %copy.32.norms, bf16[1024,1024]{1,0:T(8,128)(2,1)} %get-tuple-element.54.mixed, bf16[2,1024,512]{2,1,0:T(8,128)(2,1)} %bitcast.34), custom_call_target="tpu_custom_call" | custom-call | tf_op jit(solution)/shard_map/branch/pallas_call | solution.py:532
  241.6 69.3 %feed.1 = (bf16[1024,1024]{1,0:T(8,128)(2,1)}, f32[1024,1024]{1,0:T(8,128)}, bf16[2,1024,2048]{2,1,0:T(8,128)(2,1)}, bf16[2,1024,2048]{2,1,0:T(8,128)(2,1)}) custom-call(bf16[1024,1024]{1,0:T(8,128)(2,1)} %get-tuple-element.56.second, bf16[1024,1024]{1,0:T(8,128)(2,1)} %get-tuple-element.50.cot, f32[1024,1024]{1,0:T(8,128)} %get-tuple-element.57.middle, ...), custom_call_target="tpu_custom_call" | custom-call | tf_op jit(solution)/shard_map/feed/pallas_call | solution.py:591
  311.0 13.5 %branch_back.1 = (f32[1024,1024]{1,0:T(8,128)}, bf16[1024,1024]{1,0:T(8,128)(2,1)}, bf16[2,1024,512]{2,1,0:T(8,128)(2,1)}, f32[2,1024]{1,0:T(2,128)}) custom-call(f32[4,1024]{1,0:T(4,128)} %copy.32.norms, bf16[1024,1024]{1,0:T(8,128)(2,1)} %get-tuple-element.50.cot, f32[1024,1024]{1,0:T(8,128)} %get-tuple-element.60.grad_second, ...), custom_call_target="tpu_custom_call" | custom-call | tf_op jit(solution)/shard_map/branch_back/pallas_call | solution.py:644
  324.5 0.6 tile.21.gains
  325.1 60.7 %attend_back.1 = (bf16[1024,1024]{1,0:T(8,128)(2,1)}, bf16[1024,1024]{1,0:T(8,128)(2,1)}, bf16[1024,1024]{1,0:T(8,128)(2,1)}, f32[2,128]{1,0:T(2,128)}) custom-call(f32[2,128]{1,0:T(2,128)} %tile.21.gains, bf16[1024,1024]{1,0:T(8,128)(2,1)} %get-tuple-element.51.qn, bf16[1024,1024]{1,0:T(8,128)(2,1)} %get-tuple-element.52.kn, ...), custom_call_target="tpu_custom_call" | custom-call | tf_op jit(solution)/shard_map/attend_back/pallas_call | solution.py:506
  385.8 0.0 copy-start.6
  385.8 0.0 copy-start.5
  385.8 25.7 %project_back.1 = (bf16[2,1024,1536]{2,1,0:T(8,128)(2,1)}, bf16[1024,1024]{1,0:T(8,128)(2,1)}, f32[2,1024]{1,0:T(2,128)}) custom-call(f32[4,1024]{1,0:T(4,128)} %copy.32.norms, bf16[1024,1024]{1,0:T(8,128)(2,1)} %get-tuple-element.48.image, bf16[1024,1024]{1,0:T(8,128)(2,1)} %get-tuple-element.49.first, f32[1024,1024]{1,0:T(8,128)} %get-tuple-element.61.grad_middle, ...), custom_call_target="tpu_custom_call" | custom-call | tf_op jit(solution)/shard_map/project_back/pallas_call | solution.py:696
  411.5 0.0 copy-done.6
  411.5 0.1 slice_add_fusion
  411.6 0.1 reshape.69
  411.7 0.0 copy-done.5
  411.7 1.3 select_maximum_fusion.refs_6_
  413.0 236.5 %scatter_grads.1 = (f32[64,1536]{1,0:T(8,128)}, f32[64,512]{1,0:T(8,128)}, f32[64,2048]{1,0:T(8,128)}, f32[64,2048]{1,0:T(8,128)}, bf16[2,512,1024]{2,1,0:T(8,12...) custom-call(bf16[2,4,2,2,64,1536]{5,4,3,2,1,0:T(8,128)(2,1)} %bitcast.38, ...), custom_call_target="tpu_custom_call" | custom-call | tf_op jit(solution)/shard_map/scatter_grads/pallas_call | solution.py:1073
  649.5 0.8 constant_dynamic-slice_fusion
  650.2 0.6 pad_maximum_fusion
  650.8 0.0 copy-start.3
  650.8 0.0 copy-start
  650.8 4.2 convert_element_type.19
  655.0 0.0 copy-done.3
  655.0 0.8 copy.37
  655.8 0.7 slice_reduce_fusion
  656.5 0.6 reshape_squeeze.3
  657.1 0.0 copy-done
  657.1 0.0 copy-start.4
  657.1 0.0 copy-start.2
  657.1 0.0 copy-start.1
  657.2 1.3 copy.42
  658.5 0.0 copy-done.4
  658.5 0.7 copy.43
  659.1 0.0 copy-done.2
  659.1 0.8 copy.44
  659.9 0.0 copy-done.1
  659.9 0.8 copy.45
  (4 shorter events, 0.0 us)
Async XLA Ops:
  3.9 182.7 %copy-start.7 = (bf16[2,64]{1,0:T(2,128)(2,1)S(1)}, bf16[2,64]{1,0:T(2,128)(2,1)}, u32[]{:S(2)}) copy-start(bf16[2,64]{1,0:T(2,128)(2,1)} %param.17) | copy-start | bytes 772
  385.8 25.7 %copy-start.6 = (f32[2,128]{1,0:T(2,128)S(1)}, f32[2,128]{1,0:T(2,128)}, u32[]{:S(2)}) copy-start(f32[2,128]{1,0:T(2,128)} %get-tuple-element.77) | copy-start | bytes 3076
  385.8 25.9 %copy-start.5 = (f32[2,1024]{1,0:T(2,128)S(1)}, f32[2,1024]{1,0:T(2,128)}, u32[]{:S(2)}) copy-start(f32[2,1024]{1,0:T(2,128)} %get-tuple-element.76) | copy-start | bytes 24580
  650.8 4.2 copy-start.3
  650.8 6.3 copy-start
  657.1 1.3 copy-start.4
  657.1 2.0 copy-start.2
  657.1 2.8 copy-start.1

commit v3 on v0

--- a/solution.py
+++ b/solution.py
@@ -1,6 +1,10 @@
+import functools
+
 import jax
 import jax.numpy as jnp
 from jax import lax
+from jax.experimental import pallas as pl
+from jax.experimental.pallas import tpu as pltpu
 from jax.sharding import PartitionSpec as P
 
 HD = 64
@@ -290,6 +294,1143 @@
     )
 
 
+PAIR = 2 * HD
+F32, BF16 = jnp.float32, jnp.bfloat16
+LIMIT = 60 << 20
+
+
+def nn(a, b):
+    return lax.dot_general(a, b, (((1,), (0,)), ((), ())), preferred_element_type=F32)
+
+
+def nt(a, b):
+    return lax.dot_general(a, b, (((1,), (1,)), ((), ())), preferred_element_type=F32)
+
+
+def stats(value):
+    center = value - jnp.mean(value, -1, keepdims=True)
+    factor = lax.rsqrt(jnp.mean(center * center, -1, keepdims=True) + EPSILON)
+    return center * factor, factor
+
+
+def back(grad_hat, normed, factor):
+    return factor * (
+        grad_hat
+        - jnp.mean(grad_hat, -1, keepdims=True)
+        - normed * jnp.mean(grad_hat * normed, -1, keepdims=True)
+    )
+
+
+def head_mean_matrix(width):
+    row = lax.broadcasted_iota(jnp.int32, (width, width), 0) // HD
+    col = lax.broadcasted_iota(jnp.int32, (width, width), 1) // HD
+    return jnp.where(row == col, 1.0 / HD, 0.0).astype(BF16)
+
+
+def head_mean(value, matrix):
+    high = value.astype(BF16)
+    low = (value - high.astype(F32)).astype(BF16)
+    return nn(high, matrix) + nn(low, matrix)
+
+
+def head_stats(value, matrix):
+    center = value - head_mean(value, matrix)
+    factor = lax.rsqrt(head_mean(center * center, matrix) + EPSILON)
+    return center * factor, factor
+
+
+def head_back(grad_hat, normed, factor, matrix):
+    return factor * (
+        grad_hat - head_mean(grad_hat, matrix) - normed * head_mean(grad_hat * normed, matrix)
+    )
+
+
+MESH = pl.DeviceIdType.MESH
+ALL = slice(None)
+
+
+class Place:
+    def __init__(self, zs):
+        f = lax.axis_index("fsdp")
+        self.zs = zs
+        self.x = lax.axis_index("tensor")
+        self.c = lax.rem(f, 2)
+        self.y = lax.rem(lax.div(f, 2), 2)
+        self.z = lax.div(f, 4)
+
+    def dev(self, z=None, y=None, c=None, x=None):
+        z = self.z if z is None else z
+        y = self.y if y is None else y
+        c = self.c if c is None else c
+        x = self.x if x is None else x
+        return {"fsdp": (z * 2 + y) * 2 + c, "tensor": x}
+
+    def along_z(self):
+        return [lax.rem(self.z + k, self.zs) for k in range(1, self.zs)]
+
+    def peers(self):
+        out = [self.dev(z=z) for z in self.along_z()]
+        return out + [self.dev(y=1 - self.y), self.dev(c=1 - self.c), self.dev(x=1 - self.x)]
+
+
+def meet(place):
+    barrier = pltpu.get_barrier_semaphore()
+    peers = place.peers()
+    for peer in peers:
+        pl.semaphore_signal(barrier, inc=1, device_id=peer, device_id_type=MESH)
+    pl.semaphore_wait(barrier, len(peers))
+
+
+def remote(src, dst, send, recv, peer):
+    return pltpu.make_async_remote_copy(
+        src_ref=src, dst_ref=dst, send_sem=send, recv_sem=recv, device_id=peer, device_id_type=MESH
+    )
+
+
+def start(*copies):
+    for copy in copies:
+        copy.start()
+
+
+def wait(*copies):
+    for copy in copies:
+        copy.wait()
+
+
+class Gather:
+    def __init__(self, place, shard, whole, lo, size, order, send, recv):
+        p = self.p = place
+        cols = self.cols = pl.ds(lo, size)
+        self.shard = None if shard is None else shard.at[:, cols]
+        self.whole = whole
+        self.order = order
+        self.send, self.recv = send, recv
+        if shard is not None:
+            self.own = pltpu.make_async_copy(self.shard, self.at({}), self.send.at[2 * p.zs + 7])
+
+    def at(self, index):
+        p = self.p
+        own = {"x": p.x, "y": p.y, "z": p.z}
+        x, y, z = (index.get(d, own[d]) for d in "xyz")
+        return self.whole.at[x, z, y, p.c, :, self.cols]
+
+    def others(self, d):
+        return self.p.along_z() if d == "z" else [1 - getattr(self.p, d)]
+
+    def copies(self, base, i, pairs):
+        base += sum(len(self.others(d)) for d in self.order[:i])
+        return [remote(src, dst, self.send.at[base + k], self.recv.at[base + k], peer) for k, (src, dst, peer) in enumerate(pairs)]
+
+    def stage(self, i):
+        d = self.order[i]
+        held = self.at({e: ALL for e in self.order[:i]})
+        src = self.shard if i == 0 else held
+        return self.copies(0, i, [(src, held, self.p.dev(**{d: to})) for to in self.others(d)])
+
+    def core_parts(self, i):
+        done = {e: ALL for e in self.order[:i]}
+        d = self.order[i]
+        if i == 0:
+            refs = [self.at({d: ALL})]
+        else:
+            refs = [self.at({**done, d: to}) for to in self.others(d)]
+        peer = self.p.dev(c=1 - self.p.c)
+        return self.copies(self.p.zs + 1, i, [(ref, ref, peer) for ref in refs])
+
+    def begin(self):
+        start(self.own, *self.stage(0))
+
+    def begun(self):
+        wait(self.own, *self.stage(0))
+
+    def go(self, i):
+        if i < 3:
+            start(*self.stage(i))
+        start(*self.core_parts(i - 1))
+
+    def came(self, i):
+        wait(*self.stage(i))
+
+    def rest(self, *parts):
+        for i in parts:
+            wait(*self.core_parts(i))
+
+
+def gather_sems(zs):
+    return 2 * zs + 8
+
+
+class Swap:
+    def __init__(self, place, value, image, sems):
+        p = place
+        half = value.shape[1]
+        rows = pl.ds(pl.multiple_of(p.x * half, half), half)
+        self.copy = remote(value.at[1 - p.x], image.at[rows], sems.at[0], sems.at[1], p.dev(x=1 - p.x))
+        self.mine = pltpu.make_async_copy(value.at[p.x], image.at[rows], sems.at[2])
+
+
+class SwapBack:
+    def __init__(self, place, value, out, sems):
+        p = place
+        half = out.shape[1]
+        to = pl.ds(pl.multiple_of((1 - p.x) * half, half), half)
+        rows = pl.ds(pl.multiple_of(p.x * half, half), half)
+        self.copy = remote(value.at[to], out.at[p.x], sems.at[0], sems.at[1], p.dev(x=1 - p.x))
+        self.mine = pltpu.make_async_copy(value.at[rows], out.at[p.x], sems.at[2])
+
+
+class Sum:
+    def __init__(self, place, total, got, send, recv):
+        self.p, self.total, self.got, self.send, self.recv = place, total, got, send, recv
+
+    def copies(self, i):
+        p = self.p
+        if i < 3:
+            peers = [(p.dev(c=1 - p.c), p.dev(x=1 - p.x), p.dev(y=1 - p.y))[i]]
+        else:
+            peers = [p.dev(z=z) for z in p.along_z()]
+        return [remote(self.total, self.got.at[i + k], self.send.at[i + k], self.recv.at[i + k], peer)
+                for k, peer in enumerate(peers)]
+
+    def go(self, i):
+        start(*self.copies(i))
+
+    def add(self, i):
+        copies = self.copies(i)
+        wait(*copies)
+        total = self.total[...]
+        for k in range(len(copies)):
+            total = total + self.got[i + k]
+        self.total[...] = total
+
+
+def add_slabs(count, pair):
+    def body(i, _):
+        into, from_ = pair(i)
+        into[...] = into[...] + from_[...]
+        return 0
+    lax.fori_loop(0, count, body, 0)
+
+
+class Scatter:
+    def __init__(self, place, order, held, away, b, b1, b2, b3, send, recv):
+        self.p, self.order, self.held, self.away = place, order, held, away
+        self.b, self.b1, self.b2, self.b3 = b, b1, b2, b3
+        self.send, self.recv = send, recv
+
+    def copy(self, n, src, dst, peer):
+        return remote(src, dst, self.send.at[n], self.recv.at[n], peer)
+
+    def core(self):
+        return self.copy(0, self.away, self.b, self.p.dev(c=1 - self.p.c))
+
+    def core_add(self):
+        zs = self.p.zs
+        wait(self.core())
+
+        def pair(j):
+            x, z, y = lax.div(j, 2 * zs), lax.rem(lax.div(j, 2), zs), lax.rem(j, 2)
+            return self.held(x, z, y), self.b.at[x, z, y]
+        add_slabs(4 * zs, pair)
+
+    def first(self):
+        p = self.p
+        if self.order == "x":
+            return self.copy(1, self.held(1 - p.x, ALL, ALL), self.b1, p.dev(x=1 - p.x))
+        return self.copy(1, self.held(ALL, ALL, 1 - p.y), self.b1, p.dev(y=1 - p.y))
+
+    def first_add(self):
+        p, zs = self.p, self.p.zs
+        wait(self.first())
+
+        def pair(j):
+            if self.order == "x":
+                z, y = lax.div(j, 2), lax.rem(j, 2)
+                return self.held(p.x, z, y), self.b1.at[z, y]
+            x, z = lax.div(j, zs), lax.rem(j, zs)
+            return self.held(x, z, p.y), self.b1.at[x, z]
+        add_slabs(2 * zs, pair)
+
+    def state(self):
+        p = self.p
+        return self.held(p.x, ALL, ALL) if self.order == "x" else self.held(ALL, ALL, p.y)
+
+    def second(self):
+        p = self.p
+        if self.order == "x":
+            return self.copy(2, self.held(p.x, ALL, 1 - p.y), self.b2, p.dev(y=1 - p.y))
+        return self.copy(2, self.held(1 - p.x, ALL, p.y), self.b2, p.dev(x=1 - p.x))
+
+    def second_add(self):
+        p = self.p
+        wait(self.second())
+        add_slabs(p.zs, lambda z: (self.held(p.x, z, p.y), self.b2.at[z]))
+
+    def last(self):
+        p = self.p
+        return [self.copy(3 + k, self.held(p.x, to, p.y), self.b3.at[k], p.dev(z=to)) for k, to in enumerate(p.along_z())]
+
+    def finish(self, out):
+        p = self.p
+        wait(*self.last())
+        value = self.held(p.x, p.z, p.y)[...].astype(F32)
+        for k in range(p.zs - 1):
+            value = value + self.b3[k].astype(F32)
+        out[...] = value
+
+
+def scatter_sems(zs):
+    return zs + 2
+
+
+def landing(zs, rows, m, order, stages="0123"):
+    shapes = [(2, zs, 2, rows, m), (zs, 2, rows, m) if order == "x" else (2, zs, rows, m), (zs, rows, m), (zs - 1, rows, m)]
+    return [pltpu.VMEM(shapes[int(i)], BF16) for i in stages]
+
+
+def state_shape(zs, rows, m, order):
+    return (zs, 2, rows, m) if order == "x" else (2, zs, rows, m)
+
+
+def on(step, hooks):
+    for at, hook in hooks.items():
+        pl.when(step == at)(hook)
+
+
+HBM = pl.BlockSpec(memory_space=pl.ANY)
+WHOLE_VMEM = pl.BlockSpec(memory_space=pltpu.VMEM)
+DMA = pltpu.SemaphoreType.DMA
+
+
+def params(collective_id):
+    return pltpu.CompilerParams(collective_id=collective_id, has_side_effects=True, vmem_limit_bytes=LIMIT)
+
+
+Q_GROUPS = ((0, 384, "zyx"), (384, 384, "zxy"), (768, 512, "zxy"), (1280, 384, "zxy"))
+FF_GROUP = 512
+
+
+def opening_body(zs, q, o, u, d, tokens, whole_q, whole_o, whole_u, whole_d, image, send, recv, swap_sem):
+    p = Place(zs)
+    meet(p)
+    swap = Swap(p, tokens, image, swap_sem)
+    a, b, c, e = (Gather(p, q, whole_q, lo, n, order, send.at[i], recv.at[i]) for i, (lo, n, order) in enumerate(Q_GROUPS))
+    others = [(o, whole_o, 0), (u, whole_u, 0), (d, whole_d, 0), (u, whole_u, 1), (d, whole_d, 1)]
+    later = [Gather(p, s, w, j * FF_GROUP, FF_GROUP, "zxy", send.at[4 + i], recv.at[4 + i]) for i, (s, w, j) in enumerate(others)]
+    start(swap.copy, swap.mine)
+    a.begin()
+    b.begin()
+    a.begun()
+    a.go(1)
+    c.begin()
+    b.begun()
+    b.go(1)
+    e.begin()
+    a.came(1)
+    a.go(2)
+    b.came(1)
+    b.go(2)
+    c.begun()
+    c.go(1)
+    for g in later[:3]:
+        g.begin()
+    e.begun()
+    e.go(1)
+    for g in later[3:]:
+        g.begin()
+    c.came(1)
+    c.go(2)
+    e.came(1)
+    e.go(2)
+    for g in (a, b, c, e):
+        g.came(2)
+        g.go(3)
+    for g in later:
+        g.begun()
+    wait(swap.copy, swap.mine)
+    for g in (a, b, c, e):
+        g.rest(0, 1, 2)
+
+
+def opening(q, o, u, d, tokens, zs):
+    whole = lambda s: jax.ShapeDtypeStruct((2, zs, 2, 2) + s.shape, s.dtype)
+    return pl.pallas_call(
+        functools.partial(opening_body, zs),
+        out_shape=[whole(q), whole(o), whole(u), whole(d), jax.ShapeDtypeStruct((2 * tokens.shape[1], tokens.shape[2]), BF16)],
+        in_specs=[HBM] * 5,
+        out_specs=[HBM] * 5,
+        scratch_shapes=[DMA((9, gather_sems(zs))), DMA((9, gather_sems(zs))), DMA((3,))],
+        compiler_params=params(0),
+        name="opening",
+    )(q, o, u, d, tokens)
+
+
+QKV_TILE = 256
+Q_TILE = 256
+ROWS = 256
+
+
+def full(shape):
+    return pl.BlockSpec(shape, lambda s: (0,) * len(shape), pipeline_mode=pl.Buffered(1))
+
+
+def clipped(shape, axis, first, count):
+    def at(s):
+        i = jnp.clip(s - first, 0, count - 1)
+        return (i, 0) if axis == 0 else (0, i)
+    return pl.BlockSpec(shape, at)
+
+
+def project_step(step, per_part, joined, gains, kept, blocks):
+    part = lax.div(step, per_part)
+    tile = lax.rem(step, per_part)
+    matrix = head_mean_matrix(QKV_TILE)
+    cols = pl.ds(pl.multiple_of(tile * QKV_TILE, QKV_TILE), QKV_TILE)
+    qn_s, kn_s, v_s = kept
+    qn, kn, v, q_raw, k_raw = blocks
+
+    @pl.when(part == 0)
+    def _():
+        hat, _f = head_stats(joined, matrix)
+        value = (hat * gains[0:1] * (HD ** -0.5)).astype(BF16)
+        qn[...] = value
+        qn_s[:, cols] = value
+        q_raw[...] = joined.astype(BF16)
+
+    @pl.when(part == 1)
+    def _():
+        hat, _f = head_stats(joined, matrix)
+        value = (hat * gains[1:2]).astype(BF16)
+        kn[...] = value
+        kn_s[:, cols] = value
+        k_raw[...] = joined.astype(BF16)
+
+    @pl.when(part == 2)
+    def _():
+        value = joined.astype(BF16)
+        v[...] = value
+        v_s[:, cols] = value
+
+
+def attend_step(query_all, keys, values, mixed_s, cols, mixed, inverse):
+    length = keys.shape[0]
+    lane = lax.broadcasted_iota(jnp.int32, (1, PAIR), 1) < HD
+    values = jnp.concatenate([values, jnp.ones((length, PAIR), BF16)], axis=1)
+    zero = jnp.zeros((), BF16)
+    for i in range(length // Q_TILE):
+        at = slice(i * Q_TILE, (i + 1) * Q_TILE)
+        query = query_all[at]
+        got = []
+        for mask in (lane, ~lane):
+            scores = nt(jnp.where(mask, query, zero), keys)
+            got.append(nn(jnp.exp(scores).astype(BF16), values))
+        inv = 1.0 / jnp.where(lane, got[0][:, PAIR:], got[1][:, PAIR:])
+        value = (jnp.where(lane, got[0][:, :PAIR], got[1][:, :PAIR]) * inv).astype(BF16)
+        mixed[at] = value
+        mixed_s[at, cols] = value
+        inverse[at] = inv
+
+
+def attention_body(
+    zs, per_part, pairs, image, norms, gains, w, cot_in, u, d, _o, _u, _d,
+    first, qn, kn, v, q_raw, k_raw, mixed, inverse, middle, second, cot, whole_o, whole_u, whole_d,
+    held, qn_s, kn_s, v_s, mixed_s, out_w, send, recv, swap_sem,
+):
+    step = pl.program_id(0)
+    p = Place(zs)
+    length = image.shape[0]
+    head0, row0 = 3 * per_part, 3 * per_part + pairs
+    n = FF_GROUP
+    swap = Swap(p, cot_in, cot, swap_sem)
+    o = Gather(p, None, whole_o, 0, whole_o.shape[5], "zxy", send.at[0], recv.at[0])
+    u0 = Gather(p, None, whole_u, 0, n, "zxy", send.at[1], recv.at[1])
+    d0 = Gather(p, None, whole_d, 0, n, "zyx", send.at[2], recv.at[2])
+    u1 = Gather(p, None, whole_u, n, n, "zxy", send.at[3], recv.at[3])
+    d1 = Gather(p, None, whole_d, n, n, "zxy", send.at[4], recv.at[4])
+    nexts = [Gather(p, s, t, j * n, n, "zxy", send.at[5 + i], recv.at[5 + i])
+             for i, (s, t, j) in enumerate(((u, whole_u, 2), (d, whole_d, 2), (u, whole_u, 3), (d, whole_d, 3)))]
+    load = pltpu.make_async_copy(whole_o, out_w, swap_sem.at[3])
+
+    def h0():
+        meet(p)
+        o.go(1)
+        d0.go(1)
+        nexts[0].begin()
+        nexts[1].begin()
+
+    def h3():
+        o.came(1)
+        o.go(2)
+        d0.came(1)
+        u0.go(1)
+
+    def h6():
+        u0.came(1)
+        u0.go(2)
+        u1.go(1)
+        d0.go(2)
+
+    def h9():
+        u1.came(1)
+        u1.go(2)
+        d1.go(1)
+        nexts[2].begin()
+        nexts[3].begin()
+
+    def h12():
+        d1.came(1)
+        d1.go(2)
+        start(swap.copy, swap.mine)
+
+    def h15():
+        o.came(2)
+        o.go(3)
+
+    def h18():
+        u0.came(2)
+        u0.go(3)
+        o.rest(0, 1, 2)
+        load.start()
+
+    def h19():
+        d0.came(2)
+        d0.go(3)
+
+    def h20():
+        load.wait()
+
+    def h22():
+        u1.came(2)
+        u1.go(3)
+
+    on(step, {0: h0, 3: h3, 6: h6, 9: h9, 12: h12, 15: h15, 18: h18, 19: h19, 20: h20, 22: h22})
+
+    @pl.when(step == 0)
+    def _():
+        rows = length // 4
+
+        def norm(i, _):
+            at = pl.ds(i * rows, rows)
+            hat, _f = stats(image[at].astype(F32))
+            value = (hat * norms[0:1] + norms[2:3]).astype(BF16)
+            held[at] = value
+            first[at] = value
+            return 0
+        lax.fori_loop(0, 4, norm, 0)
+
+    @pl.when(step < head0)
+    def _():
+        project_step(step, per_part, nn(held[...], w[0]), gains, (qn_s, kn_s, v_s), (qn, kn, v, q_raw, k_raw))
+
+    @pl.when((step >= head0) & (step < row0))
+    def _():
+        cols = pl.ds(pl.multiple_of((step - head0) * PAIR, PAIR), PAIR)
+        attend_step(qn_s[:, cols], kn_s[:, cols], v_s[:, cols], mixed_s, cols, mixed, inverse)
+
+    @pl.when(step >= row0)
+    def _():
+        at = pl.ds(pl.multiple_of((step - row0) * ROWS, ROWS), ROWS)
+        half = out_w.shape[5]
+        w0, w1 = (out_w[t].reshape(-1, half) for t in range(2))
+        value = image[at].astype(F32) + nt(mixed_s[at, :half], w0) + nt(mixed_s[at, half:], w1)
+        middle[...] = value
+        hat, _f = stats(value)
+        second[...] = (hat * norms[1:2] + norms[3:4]).astype(BF16)
+
+    @pl.when(step == pl.num_programs(0) - 1)
+    def _():
+        d1.came(2)
+        d1.go(3)
+        for g in nexts:
+            g.begun()
+        wait(swap.copy, swap.mine)
+        for g in (u0, d0, u1, d1):
+            g.rest(0, 1, 2)
+
+
+def attention(image, norms, gains, w, cols, cot, u, d, whole_o, whole_u, whole_d, zs):
+    length, width = image.shape
+    half = cols // 3
+    per_half = half // QKV_TILE
+    per_part = 2 * per_half
+    pairs = 2 * half // PAIR
+    head0, row0 = 3 * per_part, 3 * per_part + pairs
+    steps = row0 + length // ROWS
+
+    def w_map(s):
+        s = jnp.minimum(s, head0 - 1)
+        part, rest = s // per_part, s % per_part
+        return rest // per_half, 0, part * per_half + rest % per_half
+
+    tiles = lambda part: clipped((length, QKV_TILE), 1, part * per_part, per_part)
+    heads = clipped((length, PAIR), 1, head0, pairs)
+    rows = clipped((ROWS, width), 0, row0, length // ROWS)
+    bf = jax.ShapeDtypeStruct((length, 2 * half), BF16)
+    same = lambda a: jax.ShapeDtypeStruct(a.shape, a.dtype)
+    store = pltpu.VMEM((length, 2 * half), BF16)
+    return pl.pallas_call(
+        functools.partial(attention_body, zs, per_part, pairs),
+        grid=(steps,),
+        in_specs=[full(image.shape), full(norms.shape), full(gains.shape), pl.BlockSpec((1, width, QKV_TILE), w_map)] + [HBM] * 6,
+        out_specs=[full((length, width)), tiles(0), tiles(1), tiles(2), tiles(0), tiles(1), heads, heads, rows, rows] + [HBM] * 4,
+        out_shape=[same(image), bf, bf, bf, bf, bf, bf, jax.ShapeDtypeStruct((length, 2 * half), F32),
+                   jax.ShapeDtypeStruct((length, width), F32), same(image), same(image), same(whole_o), same(whole_u), same(whole_d)],
+        scratch_shapes=[pltpu.VMEM((length, width), BF16), store, store, store, store, pltpu.VMEM(whole_o.shape, BF16),
+                        DMA((9, gather_sems(zs))), DMA((9, gather_sems(zs))), DMA((4,))],
+        input_output_aliases={7: 11, 8: 12, 9: 13},
+        compiler_params=params(1),
+        name="attention",
+    )(image, norms, gains, w, cot, u, d, whole_o, whole_u, whole_d)
+
+
+def gelu_parts(v):
+    bell = jnp.exp(v * v * -0.5)
+    t = 1.0 / (1.0 + (0.3275911 * 0.7071067811865476) * jnp.abs(v))
+    poly = t * (0.127414796 + t * (-0.142248368 + t * (0.7107068705 + t * (-0.7265760135 + t * 0.5307027145))))
+    tail = poly * bell
+    return jnp.where(v >= 0, 1.0 - tail, tail), bell * 0.3989422804014327
+
+
+FEED_ORDERS = ("y", "x")
+
+
+def feed_body(
+    zs, second, cot, middle, _u, _d,
+    result, grad_second, grad_u, grad_d, state_u, state_d, whole_u, whole_d,
+    acc, second_t, cot_t, active, grad_hidden, tiles, g, tile_sem, misc_sem, send, recv, *landings,
+):
+    step = pl.program_id(0)
+    p = Place(zs)
+    length = second.shape[0]
+    n = FF_GROUP
+    u2 = Gather(p, None, whole_u, 2 * n, n, "zxy", send.at[0], recv.at[0])
+    d2 = Gather(p, None, whole_d, 2 * n, n, "zyx", send.at[1], recv.at[1])
+    u3 = Gather(p, None, whole_u, 3 * n, n, "zxy", send.at[2], recv.at[2])
+    d3 = Gather(p, None, whole_d, 3 * n, n, "zyx", send.at[3], recv.at[3])
+    groups = []
+    for j in range(2):
+        for k in range(2):
+            i = 2 * j + k
+            held = lambda x, z, y, j=j, k=k: g.at[k, j, x, z, y, p.c]
+            groups.append(Scatter(p, FEED_ORDERS[k], held, g.at[k, j, :, :, :, 1 - p.c], *landings[2 * i:2 * i + 2], None, None,
+                                  send.at[4 + i], recv.at[4 + i]))
+    su0, sd0, su1, sd1 = groups
+    init = pltpu.make_async_copy(middle, acc, misc_sem.at[0])
+    states = [pltpu.make_async_copy(s.state(), (state_u, state_d)[k].at[j], misc_sem.at[1 + 2 * j + k])
+              for j in range(2) for k, s in ((0, groups[2 * j]), (1, groups[2 * j + 1]))]
+    outs = [pltpu.make_async_copy(g.at[k, j], (grad_u, grad_d)[k].at[j - 2], misc_sem.at[5 + 2 * (j - 2) + k])
+            for j in (2, 3) for k in range(2)]
+
+    def loads(s):
+        j, t = (s // 2, s % 2) if isinstance(s, int) else (lax.div(s, 2), lax.rem(s, 2))
+        slot = t
+        cols = pl.ds(j * n if isinstance(s, int) else pl.multiple_of(j * n, n), n)
+        return [pltpu.make_async_copy(w.at[t, :, :, :, :, cols], tiles.at[k, slot], tile_sem.at[k, slot])
+                for k, w in ((0, whole_u), (1, whole_d))]
+
+    @pl.when(step == 0)
+    def _():
+        meet(p)
+        start(*loads(0))
+        start(*loads(1))
+        init.start()
+        for w in (u2, d2, u3, d3):
+            w.go(1)
+        second_t[...] = second[...].T
+        cot_t[...] = cot[...].T
+        grad_second[...] = jnp.zeros_like(grad_second)
+
+    def h1():
+        start(*loads(2))
+        for w in (u2, d2):
+            w.came(1)
+            w.go(2)
+
+    def h2():
+        start(*loads(3))
+        start(su0.core(), sd0.core())
+        for w in (u3, d3):
+            w.came(1)
+            w.go(2)
+
+    def h3():
+        su0.core_add()
+        sd0.core_add()
+        start(su0.first(), sd0.first())
+        for w in (u2, d2):
+            w.came(2)
+            w.go(3)
+
+    def h4():
+        for w in (u2, d2):
+            w.rest(0, 1, 2)
+        start(*loads(4))
+        start(*loads(5))
+        start(su1.core(), sd1.core())
+        for w in (u3, d3):
+            w.came(2)
+            w.go(3)
+
+    def h5():
+        for w in (u3, d3):
+            w.rest(0, 1, 2)
+        start(*loads(6))
+        su1.core_add()
+        sd1.core_add()
+        start(su1.first(), sd1.first())
+
+    def h6():
+        start(*loads(7))
+        su0.first_add()
+        sd0.first_add()
+        start(*states[:2])
+        start(*outs[:2])
+
+    on(step, {1: h1, 2: h2, 3: h3, 4: h4, 5: h5, 6: h6})
+    wait(*loads(step))
+
+    @pl.when(step == 0)
+    def _():
+        init.wait()
+    slot = lax.rem(step, 2)
+    w_up = tiles[0, slot].reshape(-1, n)
+    w_down = tiles[1, slot].reshape(-1, n)
+    for i in range(length // ROWS):
+        at = slice(i * ROWS, (i + 1) * ROWS)
+        hidden = nn(second[at], w_up)
+        grad_active = nn(cot[at], w_down)
+        cumulative, density = gelu_parts(hidden)
+        a = (hidden * cumulative).astype(BF16)
+        b = (grad_active * (cumulative + hidden * density)).astype(BF16)
+        active[at] = a
+        grad_hidden[at] = b
+        acc[at] += nt(a, w_down)
+        grad_second[at] += nt(b, w_up)
+    j, t = lax.div(step, 2), lax.rem(step, 2)
+    shape = g.shape[3:]
+    g[0, j, t] = nn(second_t[...], grad_hidden[...]).astype(BF16).reshape(shape)
+    g[1, j, t] = nn(cot_t[...], active[...]).astype(BF16).reshape(shape)
+
+    @pl.when(step == pl.num_programs(0) - 1)
+    def _():
+        start(*outs[2:])
+        result[...] = acc[...].astype(BF16)
+        su1.first_add()
+        sd1.first_add()
+        start(*states[2:])
+        wait(*states)
+        wait(*outs)
+
+
+def feed(second, cot, middle, whole_u, whole_d, zs):
+    length, width = second.shape
+    rows, n = whole_u.shape[4], FF_GROUP
+    same = lambda a: jax.ShapeDtypeStruct(a.shape, a.dtype)
+    tile = (2, zs, 2, 2, rows, n)
+    grads = jax.ShapeDtypeStruct((2,) + tile, BF16)
+    square = pltpu.VMEM((length, width), BF16)
+    strip = pltpu.VMEM((length, n), BF16)
+    scratch = [pltpu.VMEM((length, width), F32), square, square, strip, strip, pltpu.VMEM((2, 2) + tile[1:], BF16),
+               pltpu.VMEM((2, 4) + tile, BF16), DMA((2, 2)), DMA((9,)), DMA((8, gather_sems(zs))), DMA((8, gather_sems(zs)))]
+    for i in range(4):
+        scratch += landing(zs, rows, n, FEED_ORDERS[i % 2], "01")
+    return pl.pallas_call(
+        functools.partial(feed_body, zs),
+        grid=(8,),
+        in_specs=[full(second.shape), full(cot.shape), HBM, HBM, HBM],
+        out_specs=[full(second.shape), full(second.shape)] + [HBM] * 6,
+        out_shape=[same(second), jax.ShapeDtypeStruct((length, width), F32), grads, grads]
+        + [jax.ShapeDtypeStruct((2,) + state_shape(zs, rows, n, o), BF16) for o in FEED_ORDERS]
+        + [same(whole_u), same(whole_d)],
+        scratch_shapes=scratch,
+        input_output_aliases={3: 6, 4: 7},
+        compiler_params=params(2),
+        name="feed",
+    )(second, cot, middle, whole_u, whole_d)
+
+
+LATE_ORDERS = ("x", "y", "y", "y")
+
+
+def attend_back_step(gains, go, inv, query, keys, values, q_raw, k_raw, mixed, grad_q, grad_k, grad_v, grad_gains):
+    length = query.shape[0]
+    lanes = lax.broadcasted_iota(jnp.int32, (1, PAIR), 1)
+    first = lanes < HD
+    zero = jnp.zeros((), BF16)
+    go = go.astype(F32)
+    product = go * mixed.astype(F32) * inv
+    go_inv = (go * inv).astype(BF16)
+    heads = []
+    for h, mask in ((0, first), (1, ~first)):
+        delta = -jnp.sum(jnp.where(mask, product, 0.0), -1, keepdims=True)
+        high = delta.astype(BF16)
+        low = (delta - high.astype(F32)).astype(BF16)
+        spare = (1 - h) * HD
+        grad_aug = jnp.where(mask, go_inv, jnp.where(lanes == spare, high, jnp.where(lanes == spare + 1, low, zero)))
+        values_aug = jnp.where(mask, values, jnp.where((lanes == spare) | (lanes == spare + 1), jnp.ones((), BF16), zero))
+        heads.append((jnp.where(mask, query, zero), jnp.where(mask, keys, zero), jnp.where(mask, go_inv, zero), grad_aug, values_aug))
+    dq = []
+    dk = jnp.zeros((length, PAIR), F32)
+    dv = jnp.zeros((length, PAIR), F32)
+    for i in range(length // Q_TILE):
+        at = slice(i * Q_TILE, (i + 1) * Q_TILE)
+        part = jnp.zeros((Q_TILE, PAIR), F32)
+        for qm, km, gm, ga, va in heads:
+            exponent = jnp.exp(nt(km, qm[at]))
+            grad_scores = (exponent * nt(va, ga[at])).astype(BF16)
+            dv = dv + nn(exponent.astype(BF16), gm[at])
+            dk = dk + nn(grad_scores, qm[at])
+            part = part + lax.dot_general(grad_scores, km, (((0,), (0,)), ((), ())), preferred_element_type=F32)
+        dq.append(part)
+    dq = jnp.concatenate(dq, axis=0)
+    grad_v[...] = dv.astype(BF16)
+    matrix = head_mean_matrix(PAIR)
+    hat, factor = head_stats(q_raw.astype(F32), matrix)
+    scale = HD ** -0.5
+    sum_q = jnp.sum(dq * hat, 0, keepdims=True) * scale
+    grad_q[...] = head_back(dq * gains[0:1] * scale, hat, factor, matrix).astype(BF16)
+    hat, factor = head_stats(k_raw.astype(F32), matrix)
+    sum_k = jnp.sum(dk * hat, 0, keepdims=True)
+    grad_k[...] = head_back(dk * gains[1:2], hat, factor, matrix).astype(BF16)
+    grad_gains[...] += jnp.concatenate([sum_q, sum_k], axis=0)
+
+
+def backward_body(
+    zs, rows_steps, norms, gains, cot, grad_second, middle, mixed_rows, w, qn, kn, v, q_raw, k_raw, mixed, inverse,
+    grads_u, grads_d, state_u, state_d, result,
+    grad_middle, grad_q, grad_k, grad_v, grad_gains, sums, shard_u, shard_d, shard_o, outputs,
+    grad_mixed, acc, g_o, own_early, own_late, load_sem, swap_sem, send, recv, *landings,
+):
+    step = pl.program_id(0)
+    p = Place(zs)
+    n = FF_GROUP
+    half = w.shape[2]
+    at = iter(landings)
+    take = lambda count: [next(at) for _ in range(count)]
+    early, late, loads = [], [], []
+    for i in range(4):
+        j, k = divmod(i, 2)
+        order = FEED_ORDERS[k]
+        state = (state_u, state_d)[k].at[j]
+        if order == "x":
+            far, near = state.at[:, 1 - p.y], state.at[:, p.y]
+        else:
+            far, near = state.at[1 - p.x], state.at[p.x]
+        b2, b3 = take(2)
+        s = Scatter(p, order, lambda x, z, y, i=i: own_early.at[i, z], None, None, None, b2, b3, send.at[i], recv.at[i])
+        s.second = lambda s=s, far=far, order=order: s.copy(2, far, s.b2, p.dev(y=1 - p.y) if order == "x" else p.dev(x=1 - p.x))
+        early.append(s)
+        loads.append(pltpu.make_async_copy(near, own_early.at[i], load_sem.at[i]))
+    for i in range(4):
+        j, k = divmod(i, 2)
+        grad = (grads_u, grads_d)[k].at[j]
+        s = Scatter(p, LATE_ORDERS[i], lambda x, z, y, i=i: own_late.at[i, x, z, y], grad.at[:, :, :, 1 - p.c],
+                    *take(4), send.at[4 + i], recv.at[4 + i])
+        late.append(s)
+        loads.append(pltpu.make_async_copy(grad.at[:, :, :, p.c], own_late.at[i], load_sem.at[4 + i]))
+    so = Scatter(p, "y", lambda x, z, y: g_o.at[x, z, y, p.c], g_o.at[:, :, :, 1 - p.c], *take(4), send.at[8], recv.at[8])
+    swap = SwapBack(p, result, outputs, swap_sem)
+
+    def out(k, j):
+        return (shard_u, shard_d)[k].at[:, pl.ds(j * n, n)]
+
+    def h0():
+        meet(p)
+        start(*loads)
+        start(*[s.second() for s in early])
+        start(*[s.core() for s in late[:2]])
+
+    def h2():
+        wait(*loads)
+        for s in late[:2]:
+            s.core_add()
+            s.first().start()
+        start(*[s.core() for s in late[2:]])
+
+    def h4():
+        so.core().start()
+        for s in early:
+            s.second_add()
+            start(*s.last())
+        for s in late[2:]:
+            s.core_add()
+            s.first().start()
+
+    def h5():
+        so.core_add()
+        so.first().start()
+
+    def h6():
+        for s in late[:2]:
+            s.first_add()
+            s.second().start()
+        start(swap.copy, swap.mine)
+
+    def h9():
+        for s in late[2:]:
+            s.first_add()
+            s.second().start()
+        for s in late[:2]:
+            s.second_add()
+            start(*s.last())
+
+    def h10():
+        so.first_add()
+        so.second().start()
+        for i, s in enumerate(early):
+            s.finish(out(i % 2, i // 2))
+
+    def h11():
+        for s in late[2:]:
+            s.second_add()
+            start(*s.last())
+
+    on(step, {0: h0, 2: h2, 4: h4, 5: h5, 6: h6, 9: h9, 10: h10, 11: h11})
+
+    @pl.when(step == 0)
+    def _():
+        sums[...] = jnp.zeros_like(sums)
+        acc[...] = jnp.zeros_like(acc)
+        grad_gains[...] = jnp.zeros_like(grad_gains)
+
+    @pl.when(step < rows_steps)
+    def _():
+        hat, factor = stats(middle[...])
+        gs = grad_second[...]
+        gm = cot[...].astype(F32) + back(gs * norms[1:2], hat, factor)
+        grad_middle[...] = gm
+        branch_grad = gm.astype(BF16)
+        branch_t = branch_grad.T
+        here = pl.ds(pl.multiple_of(step * ROWS, ROWS), ROWS)
+        for t in range(2):
+            cols = slice(t * half, (t + 1) * half)
+            grad_mixed[here, cols] = nn(branch_grad, w[t]).astype(BF16)
+            acc[t] += nn(branch_t, mixed_rows[:, cols])
+        sums[0:1] += jnp.sum(gs * hat, 0, keepdims=True)
+        sums[1:2] += jnp.sum(gs, 0, keepdims=True)
+
+    @pl.when(step == rows_steps - 1)
+    def _():
+        g_o[...] = acc[...].astype(BF16).reshape(g_o.shape)
+
+    @pl.when(step >= rows_steps)
+    def _():
+        cols = pl.ds(pl.multiple_of((step - rows_steps) * PAIR, PAIR), PAIR)
+        attend_back_step(gains, grad_mixed[:, cols], inverse[...], qn[...], kn[...], v[...], q_raw[...], k_raw[...], mixed[...],
+                         grad_q, grad_k, grad_v, grad_gains)
+
+    @pl.when(step == pl.num_programs(0) - 1)
+    def _():
+        so.second_add()
+        start(*so.last())
+        for i, s in enumerate(late):
+            s.finish(out(i % 2, 2 + i // 2))
+        so.finish(shard_o)
+        wait(swap.copy, swap.mine)
+
+
+def backward(norms, gains, cot, grad_second, middle, mixed, w, kept, inverse, grads_u, grads_d, state_u, state_d, result, zs):
+    length, width = middle.shape
+    half = w.shape[2]
+    rows, n = grads_u.shape[5], FF_GROUP
+    row_steps, pairs = length // ROWS, 2 * half // PAIR
+    row = clipped((ROWS, width), 0, 0, row_steps)
+    head = clipped((length, PAIR), 1, row_steps, pairs)
+    heads = jax.ShapeDtypeStruct((length, 2 * half), BF16)
+    f32 = lambda *shape: jax.ShapeDtypeStruct(shape, F32)
+    scratch = [
+        pltpu.VMEM((length, 2 * half), BF16), pltpu.VMEM(w.shape, F32), pltpu.VMEM((2, zs, 2, 2, rows, half), BF16),
+        pltpu.VMEM((4, zs, rows, n), BF16), pltpu.VMEM((4, 2, zs, 2, rows, n), BF16), DMA((8,)), DMA((3,)),
+        DMA((9, scatter_sems(zs))), DMA((9, scatter_sems(zs))),
+    ]
+    for i in range(4):
+        scratch += landing(zs, rows, n, FEED_ORDERS[i % 2], "23")
+    for i in range(4):
+        scratch += landing(zs, rows, n, LATE_ORDERS[i])
+    scratch += landing(zs, rows, half, "y")
+    return pl.pallas_call(
+        functools.partial(backward_body, zs, row_steps),
+        grid=(row_steps + pairs,),
+        in_specs=[full(norms.shape), full(gains.shape), row, row, row, row, full(w.shape)] + [head] * 7 + [HBM] * 5,
+        out_specs=[row, head, head, head, full((2, PAIR)), full((2, width)), full((rows, 4 * n)), full((rows, 4 * n)),
+                   full((rows, half)), HBM],
+        out_shape=[f32(length, width), heads, heads, heads, f32(2, PAIR), f32(2, width), f32(rows, 4 * n), f32(rows, 4 * n),
+                   f32(rows, half), jax.ShapeDtypeStruct((2, length // 2, width), BF16)],
+        scratch_shapes=scratch,
+        compiler_params=params(3),
+        name="backward",
+    )(norms, gains, cot, grad_second, middle, mixed, w, *kept, mixed, inverse, grads_u, grads_d, state_u, state_d, result)
+
+
+PART_GROUP = 256
+CLOSING = ((0, 0, 768, "y"), (1, 0, 384, "y"), (1, 384, 384, "x"))
+
+
+def closing_body(
+    zs, norms, sums_second, sums_qk, image_in, first_in, grad_middle_in, gq_in, gk_in, gv_in, w_in,
+    shard_q, total, grad_tokens,
+    image, first, grad_middle, grads, w, first_t, acc, grad_image, g, load_sem, swap_sem, got, sum_send, sum_recv, send, recv, *landings,
+):
+    p = Place(zs)
+    meet(p)
+    length, width = image.shape
+    half = grads.shape[2] // 2
+    load_grads = [pltpu.make_async_copy(a, grads.at[i], load_sem.at[i]) for i, a in enumerate((gq_in, gk_in, gv_in))]
+    load_first = pltpu.make_async_copy(first_in, first, load_sem.at[3])
+    load_w = pltpu.make_async_copy(w_in, w, load_sem.at[4])
+    load_image = pltpu.make_async_copy(image_in, image, load_sem.at[5])
+    load_middle = pltpu.make_async_copy(grad_middle_in, grad_middle, load_sem.at[6])
+    start(load_first, *load_grads, load_w, load_image, load_middle)
+    groups = []
+    for i, (k, lo, m, order) in enumerate(CLOSING):
+        at = pl.ds(lo, m)
+        held = lambda x, z, y, k=k, at=at: g.at[k, x, z, y, p.c, :, at]
+        groups.append(Scatter(p, order, held, g.at[k, :, :, :, 1 - p.c, :, at], *landings[4 * i:4 * i + 4], send.at[i], recv.at[i]))
+    a, b, c = groups
+    swap = SwapBack(p, grad_image, grad_tokens, swap_sem)
+    small = Sum(p, total, got, sum_send, sum_recv)
+
+    load_first.wait()
+    first_t[...] = first[...].T
+    wait(*load_grads)
+
+    def weight_grad(k):
+        def one(i, _):
+            t, part = lax.div(i, 3), lax.rem(i, 3)
+            cols = pl.ds(pl.multiple_of(t * half + k * PART_GROUP, PART_GROUP), PART_GROUP)
+            value = nn(first_t[...], grads[part, :, cols]).astype(BF16)
+            g[k, t, :, :, :, :, pl.ds(pl.multiple_of(part * PART_GROUP, PART_GROUP), PART_GROUP)] = value.reshape(
+                g.shape[2:6] + (PART_GROUP,))
+            return 0
+        lax.fori_loop(0, 6, one, 0)
+
+    weight_grad(0)
+    a.core().start()
+    weight_grad(1)
+    start(b.core(), c.core())
+    a.core_add()
+    a.first().start()
+    b.core_add()
+    b.first().start()
+    c.core_add()
+    c.first().start()
+    load_w.wait()
+    acc[...] = jnp.zeros_like(acc)
+
+    def to_first(i, _):
+        t, part = lax.div(i, 3), lax.rem(i, 3)
+        cols = pl.ds(pl.multiple_of(t * half, half), half)
+        acc[...] += nt(grads[part, :, cols], w[t, :, pl.ds(pl.multiple_of(part * half, half), half)])
+        return 0
+    lax.fori_loop(0, 6, to_first, 0)
+    wait(load_image, load_middle)
+
+    def norm_back(i, carry):
+        at = pl.ds(pl.multiple_of(i * ROWS, ROWS), ROWS)
+        hat, factor = stats(image[at].astype(F32))
+        gf = acc[at]
+        grad_image[at] = (grad_middle[at] + back(gf * norms[0:1], hat, factor)).astype(BF16)
+        return carry[0] + jnp.sum(gf * hat, 0, keepdims=True), carry[1] + jnp.sum(gf, 0, keepdims=True)
+    zero = jnp.zeros((1, width), F32)
+    sum_hat, sum_all = lax.fori_loop(0, length // ROWS, norm_back, (zero, zero))
+    start(swap.copy, swap.mine)
+    total[...] = jnp.zeros_like(total)
+    total[0:1] = sum_hat
+    total[1:2] = sum_all
+    total[2:4] = sums_second[...]
+    total[4:6, 0:PAIR] = sums_qk[...]
+    small.go(0)
+    a.first_add()
+    a.second().start()
+    small.add(0)
+    small.go(1)
+    c.first_add()
+    c.second().start()
+    small.add(1)
+    small.go(2)
+    b.first_add()
+    b.second().start()
+    small.add(2)
+    small.go(3)
+    a.second_add()
+    start(*a.last())
+    small.add(3)
+    c.second_add()
+    start(*c.last())
+    b.second_add()
+    start(*b.last())
+    for s, (k, lo, m, order) in zip(groups, CLOSING):
+        s.finish(shard_q.at[k, :, pl.ds(lo, m)])
+    wait(swap.copy, swap.mine)
+
+
+def closing(norms, sums_second, sums_qk, image, first, grad_middle, gq, gk, gv, w, zs):
+    length, width = image.shape
+    rows = width // (4 * zs)
+    wide = 3 * PART_GROUP
+    square = pltpu.VMEM((length, width), BF16)
+    scratch = [
+        square, square, pltpu.VMEM((length, width), F32), pltpu.VMEM((3,) + gq.shape, BF16), pltpu.VMEM(w.shape, BF16), square,
+        pltpu.VMEM((length, width), F32), square, pltpu.VMEM((2, 2, zs, 2, 2, rows, wide), BF16), DMA((7,)), DMA((3,)),
+        pltpu.VMEM((zs + 2, 8, width), F32), DMA((zs + 2,)), DMA((zs + 2,)),
+        DMA((3, scatter_sems(zs))), DMA((3, scatter_sems(zs))),
+    ]
+    for k, lo, m, order in CLOSING:
+        scratch += landing(zs, rows, m, order)
+    return pl.pallas_call(
+        functools.partial(closing_body, zs),
+        in_specs=[WHOLE_VMEM] * 3 + [HBM] * 7,
+        out_specs=[WHOLE_VMEM, WHOLE_VMEM, HBM],
+        out_shape=[jax.ShapeDtypeStruct((2, rows, wide), F32), jax.ShapeDtypeStruct((8, width), F32),
+                   jax.ShapeDtypeStruct((2, length // 2, width), BF16)],
+        scratch_shapes=scratch,
+        compiler_params=params(4),
+        name="closing",
+    )(norms, sums_second, sums_qk, image, first, grad_middle, gq, gk, gv, w)
+
+
+def whole_images(tokens, cotangent, w_qkv, wo_t, w_up, w_down_t, norm_gains, norm_shifts, qk_gains):
+    zs = lax.axis_size("fsdp") // 4
+    rows = w_qkv.shape[0]
+    width = tokens.shape[2]
+    half = w_qkv.shape[2]
+    cols = 3 * half
+    side = jnp.concatenate([norm_gains, norm_shifts, jnp.zeros((rows, 124), BF16)], axis=1)
+    shard_q = jnp.concatenate([w_qkv.reshape(rows, cols), side], axis=1)
+    whole_q, whole_o, whole_u, whole_d, image = opening(shard_q, wo_t, w_up, w_down_t, tokens, zs)
+    qkv = whole_q.reshape(2, width, cols + 128)
+    norms = qkv[0, :, cols:cols + 4].T.astype(F32)
+    gains = qk_gains.astype(F32)
+    first, qn, kn, v, q_raw, k_raw, mixed, inverse, middle, second, cot, whole_o, whole_u, whole_d = attention(
+        image, norms, jnp.tile(gains, (1, QKV_TILE // HD)), qkv, cols, cotangent, w_up, w_down_t, whole_o, whole_u, whole_d, zs
+    )
+    result, grad_second, grads_u, grads_d, state_u, state_d, whole_u, whole_d = feed(second, cot, middle, whole_u, whole_d, zs)
+    grad_middle, gq, gk, gv, sums_qk, sums_second, shard_u, shard_d, shard_o, outputs = backward(
+        norms, jnp.tile(gains, (1, 2)), cot, grad_second, middle, mixed, whole_o.reshape(2, width, half),
+        (qn, kn, v, q_raw, k_raw), inverse, grads_u, grads_d, state_u, state_d, result, zs
+    )
+    grad_q, small, grad_tokens = closing(norms, sums_second, sums_qk, image, first, grad_middle, gq, gk, gv, qkv, zs)
+    grad_q = grad_q.reshape(2, rows, 3, PART_GROUP).transpose(1, 2, 0, 3).reshape(w_qkv.shape)
+    mine = lax.dynamic_slice_in_dim(small, lax.axis_index("fsdp") * rows, rows, 1)
+    return (
+        outputs,
+        grad_tokens.astype(F32),
+        grad_q,
+        shard_o,
+        shard_u,
+        shard_d,
+        jnp.stack([mine[0], mine[2]], 1),
+        jnp.stack([mine[1], mine[3]], 1),
+        small[4:6, :HD] + small[4:6, HD:2 * HD],
+    )
+
+
+def layer(tokens, *rest):
+    if tokens.shape[0] == lax.axis_size("tensor") == 2 and lax.axis_size("fsdp") % 4 == 0:
+        return whole_images(tokens, *rest)
+    return per_device(tokens, *rest)
+
+
 def solution(mesh):
     in_specs = (
         P("fsdp", "tensor", None),
@@ -314,5 +1455,5 @@
         P(),
     )
     return jax.shard_map(
-        per_device, mesh=mesh, in_specs=in_specs, out_specs=out_specs, check_vma=False
-    )
+        layer, mesh=mesh, in_specs=in_specs, out_specs=out_specs, check_vma=False
+    )

time: 1570 us -> 459 us (0.29)
  waiting for transfers between devices: 826 us -> 0 us
  Pallas kernels: 0 us -> 439 us
  matrix products: 334 us -> 0 us
  other arithmetic: 158 us -> 7.06 us
  blocking collectives: 119 us -> 0 us
  local copies, waits for them, and re-layouts: 104 us -> 11.3 us
    pallas_call x0 -> x5, Pallas kernels: none -> 439 us  [the longest x1 101 us: backward(): pl.pallas_call(functools.partial(backward_body, zs, row_steps), grid=(row...]
    reduce_scatter x12 -> x0, waiting for transfers between devices: 430 us -> none  [the longest x2 108 us: forward(): lax.psum_scatter(contract_cols(mixed, whole_out), 'tensor', scatter_dimen...]
    all_gather x16 -> x0, waiting for transfers between devices: 391 us -> none  [the longest x2 105 us: fetch(): lax.all_gather(w_down_t, 'fsdp', axis=0, tiled=True)]
    dot_general x52 -> x0, matrix products: 334 us -> none  [the longest x8 57.1 us: contract_rows(): lax.dot_general(left, right, (((0,), (0,)), ((), ())), preferred_element_...]
    all_gather x4 -> x0, blocking collectives: 79.5 us -> none  [the longest x2 44.6 us: fetch(): lax.all_gather(norm_gains, 'fsdp', axis=0, tiled=True)]
    convert_element_type x29 -> x2, other arithmetic: 81.2 us -> 5.1 us  [the longest x1 4.12 us: whole_images(): grad_tokens.astype(F32)]
    while x276 -> x0, local copies, waits for them, and re-layouts: 64.3 us -> none
    reduce_sum x24 -> x0, other arithmetic: 57.9 us -> none  [the longest x4 14.1 us: attend(): total_sum = jnp.sum(exponent, -1, keepdims=True)]
  transfers between devices with their start and end apart: 28 -> 0, of which waited for: 23 -> 0; matrix products, arithmetic and copies ran while one was open for 30% -> 0% of each run, Pallas kernels for 0% -> 0%
where the time goes in v3:
time: 459 us
  Pallas kernels  439 us (96%)
  local copies, waits for them, and re-layouts  11.3 us (2%)
  other arithmetic  7.06 us (2%)
    pallas_call x1, Pallas kernels, backward(): pl.pallas_call(functools.partial(backward_body, zs, row_steps), grid=(row...  101 us
    pallas_call x1, Pallas kernels, closing(): pl.pallas_call(functools.partial(closing_body, zs), in_specs=[WHOLE_VMEM]...  89.9 us
    pallas_call x1, Pallas kernels, opening(): pl.pallas_call(functools.partial(opening_body, zs), out_shape=[whole(q),...  87.2 us
    pallas_call x1, Pallas kernels, attention(): pl.pallas_call(functools.partial(attention_body, zs, per_part, pairs), gr...  81.4 us
    pallas_call x1, Pallas kernels, feed(): pl.pallas_call(functools.partial(feed_body, zs), grid=(8,), in_specs=[ful...  79.8 us

profile of v3, /device:TPU:0, one launch (start us, length us, event | category | flops | bytes accessed | tf_op | source)
XLA Modules:
  0.0 458.5 jit_solution(18003278076054946713)
XLA Ops:
  0.6 0.9 copy.43
  1.6 0.8 copy.37
  2.4 0.8 copy.38
  3.1 0.8 concatenate.3.q
  3.9 0.0 copy-start.5
  3.9 87.2 %opening.1 = (bf16[2,4,2,2,64,1664]{5,4,3,2,1,0:T(8,128)(2,1)}, bf16[2,4,2,2,64,512]{5,4,3,2,1,0:T(8,128)(2,1)}, bf16[2,4,2,2,64,2048]{5,4,3,2,1,0:T(8,128)(2,1)...) custom-call(bf16[64,1664]{1,0:T(8,128)(2,1)} %concatenate.3.q, bf16[64,512]{1,0:T(8,128)(2,1)} %o.1, ...), custom_call_target="tpu_custom_call" | custom-call | tf_op jit(solution)/shard_map/opening/pallas_call | solution.py:657
  91.1 1.0 convert_bitcast_fusion
  92.1 0.8 copy.40.norms
  92.9 0.0 copy-done.5
  92.9 0.7 tile.21.gains
  93.5 81.4 %attention.1 = (bf16[1024,1024]{1,0:T(8,128)(2,1)}, bf16[1024,1024]{1,0:T(8,128)(2,1)}, bf16[1024,1024]{1,0:T(8,128)(2,1)}, bf16[1024,1024]{1,0:T(8,128)(2,1)}, ...) custom-call(bf16[1024,1024]{1,0:T(8,128)(2,1)} %get-tuple-element.48, ...), custom_call_target="tpu_custom_call", output_to_operand_aliasing={{11}: (7, {}), {12}: (8, {}), {13}: (9, {})} | custom-call | tf_op jit(solution)/shard_map/attention/pallas_call | solution.py:871
  174.9 79.8 %feed.1 = (bf16[1024,1024]{1,0:T(8,128)(2,1)}, f32[1024,1024]{1,0:T(8,128)}, bf16[2,2,4,2,2,64,512]{6,5,4,3,2,1,0:T(8,128)(2,1)}, bf16[2,2,4,2,2,64,512]{6,5,4,3...) custom-call(bf16[1024,1024]{1,0:T(8,128)(2,1)} %get-tuple-element.53, ...), custom_call_target="tpu_custom_call", output_to_operand_aliasing={{6}: (3, {}), {7}: (4, {})} | custom-call | tf_op jit(solution)/shard_map/feed/pallas_call | solution.py:1037
  254.7 0.6 tile.9.gains
  255.4 101.3 %backward.1 = (f32[1024,1024]{1,0:T(8,128)}, bf16[1024,1024]{1,0:T(8,128)(2,1)}, bf16[1024,1024]{1,0:T(8,128)(2,1)}, bf16[1024,1024]{1,0:T(8,128)(2,1)}, f32[2,1...) custom-call(f32[4,1024]{1,0:T(4,128)} %copy.40.norms, ...), custom_call_target="tpu_custom_call" | custom-call | tf_op jit(solution)/shard_map/backward/pallas_call | solution.py:1251
  356.6 89.9 %closing.1 = (f32[2,64,768]{2,1,0:T(8,128)}, f32[8,1024]{1,0:T(8,128)}, bf16[2,512,1024]{2,1,0:T(8,128)(2,1)}) custom-call(f32[4,1024]{1,0:T(4,128)} %copy.40.norms, f32[2,1024]{1,0:T(2,128)} %get-tuple-element.72.sums_second, f32[2,128]{1,0:T(2,128)} %get-tuple-element.73.sums_qk, bf16[1024,1024]{1,0:T(8,128)(2,1)} %get-tuple-element.48.image.image_in, ...), custom_call_target="tpu_custom_call" | custom-call | tf_op jit(solution)/shard_map/closing/pallas_call | solution.py:1380
  446.5 0.7 constant_dynamic-slice_fusion
  447.3 0.6 pad_maximum_fusion
  447.9 0.0 copy-start.3
  447.9 4.1 convert_element_type.17
  452.0 0.0 copy-start
  452.0 0.0 copy-done.3
  452.0 0.2 reshape.45
  452.2 0.3 copy.42
  452.5 1.1 reshape.46
  453.6 1.4 slice_add_fusion
  455.0 0.0 copy-done
  455.0 0.0 copy-start.4
  455.0 0.0 copy-start.2
  455.0 0.0 copy-start.1
  455.0 1.3 copy.53
  456.3 0.0 copy-done.4
  456.3 0.7 copy.54
  456.9 0.0 copy-done.2
  457.0 0.8 copy.55
  457.7 0.0 copy-done.1
  457.7 0.8 copy.56
  (4 shorter events, 0.0 us)
Async XLA Ops:
  3.9 89.0 %copy-start.5 = (bf16[2,64]{1,0:T(2,128)(2,1)S(1)}, bf16[2,64]{1,0:T(2,128)(2,1)}, u32[]{:S(2)}) copy-start(bf16[2,64]{1,0:T(2,128)(2,1)} %param.17) | copy-start | bytes 772
  447.9 4.1 copy-start.3
  452.0 3.0 copy-start
  455.0 1.3 copy-start.4
  455.0 2.0 copy-start.2
  455.0 2.8 copy-start.1

commit v4 on v3

--- a/solution.py
+++ b/solution.py
@@ -398,12 +398,12 @@
 
 
 class Gather:
-    def __init__(self, place, shard, whole, lo, size, order, send, recv):
+    def __init__(self, place, shard, whole, lo, size, order, send, recv, since=0):
         p = self.p = place
         cols = self.cols = pl.ds(lo, size)
         self.shard = None if shard is None else shard.at[:, cols]
         self.whole = whole
-        self.order = order
+        self.order, self.since = order, since
         self.send, self.recv = send, recv
         if shard is not None:
             self.own = pltpu.make_async_copy(self.shard, self.at({}), self.send.at[2 * p.zs + 7])
@@ -437,22 +437,24 @@
         peer = self.p.dev(c=1 - self.p.c)
         return self.copies(self.p.zs + 1, i, [(ref, ref, peer) for ref in refs])
 
-    def begin(self):
-        start(self.own, *self.stage(0))
-
-    def begun(self):
-        wait(self.own, *self.stage(0))
-
-    def go(self, i):
+    def start(self, i):
+        if i == 0:
+            self.own.start()
         if i < 3:
             start(*self.stage(i))
-        start(*self.core_parts(i - 1))
-
-    def came(self, i):
-        wait(*self.stage(i))
-
-    def rest(self, *parts):
-        for i in parts:
+        if i > 0:
+            start(*self.core_parts(i - 1))
+
+    def done(self, i):
+        if i == 0:
+            self.own.wait()
+        if i < 3:
+            wait(*self.stage(i))
+        else:
+            self.rest(self.since - 1 if self.since else 0, 3)
+
+    def rest(self, lo, hi):
+        for i in range(lo, hi):
             wait(*self.core_parts(i))
 
 
@@ -460,23 +462,24 @@
     return 2 * zs + 8
 
 
+CHUNKS = 4
+
+
 class Swap:
-    def __init__(self, place, value, image, sems):
-        p = place
-        half = value.shape[1]
-        rows = pl.ds(pl.multiple_of(p.x * half, half), half)
-        self.copy = remote(value.at[1 - p.x], image.at[rows], sems.at[0], sems.at[1], p.dev(x=1 - p.x))
-        self.mine = pltpu.make_async_copy(value.at[p.x], image.at[rows], sems.at[2])
-
-
-class SwapBack:
-    def __init__(self, place, value, out, sems):
-        p = place
-        half = out.shape[1]
-        to = pl.ds(pl.multiple_of((1 - p.x) * half, half), half)
-        rows = pl.ds(pl.multiple_of(p.x * half, half), half)
-        self.copy = remote(value.at[to], out.at[p.x], sems.at[0], sems.at[1], p.dev(x=1 - p.x))
-        self.mine = pltpu.make_async_copy(value.at[rows], out.at[p.x], sems.at[2])
+    def __init__(self, place, src, dst, sems):
+        rows = src.shape[0] // CHUNKS
+        part = lambda ref, i: ref.at[pl.ds(i * rows, rows)]
+        self.copies = [remote(part(src, i), part(dst, i), sems.at[0, i], sems.at[1, i], place.dev(x=1 - place.x)) for i in range(CHUNKS)]
+
+    def start(self, i):
+        self.copies[i].start()
+
+    def done(self, i):
+        self.copies[i].wait()
+
+
+def half_rows(ref, which, rows):
+    return ref.at[pl.ds(pl.multiple_of(which * rows, rows), rows)]
 
 
 class Sum:
@@ -492,10 +495,10 @@
         return [remote(self.total, self.got.at[i + k], self.send.at[i + k], self.recv.at[i + k], peer)
                 for k, peer in enumerate(peers)]
 
-    def go(self, i):
+    def start(self, i):
         start(*self.copies(i))
 
-    def add(self, i):
+    def done(self, i):
         copies = self.copies(i)
         wait(*copies)
         total = self.total[...]
@@ -513,83 +516,105 @@
 
 
 class Scatter:
-    def __init__(self, place, order, held, away, b, b1, b2, b3, send, recv):
+    def __init__(self, place, order, held, away, landings, send, recv, out=None):
         self.p, self.order, self.held, self.away = place, order, held, away
-        self.b, self.b1, self.b2, self.b3 = b, b1, b2, b3
-        self.send, self.recv = send, recv
-
-    def copy(self, n, src, dst, peer):
-        return remote(src, dst, self.send.at[n], self.recv.at[n], peer)
-
-    def core(self):
-        return self.copy(0, self.away, self.b, self.p.dev(c=1 - self.p.c))
-
-    def core_add(self):
-        zs = self.p.zs
-        wait(self.core())
-
-        def pair(j):
-            x, z, y = lax.div(j, 2 * zs), lax.rem(lax.div(j, 2), zs), lax.rem(j, 2)
-            return self.held(x, z, y), self.b.at[x, z, y]
-        add_slabs(4 * zs, pair)
-
-    def first(self):
+        self.landings, self.send, self.recv, self.out = landings, send, recv, out
+
+    def size(self, d):
+        return self.p.zs if d == "z" else 2
+
+    def others(self, d):
+        return self.p.along_z() if d == "z" else [1 - getattr(self.p, d)]
+
+    def part(self, i, value, rest=None):
+        at = {e: ALL for e in "xzy"}
+        at.update(rest or {})
+        at.update({e: getattr(self.p, e) for e in self.order[:i]})
+        at[self.order[i]] = value
+        return self.held(at["x"], at["z"], at["y"])
+
+    def copies(self, i):
         p = self.p
-        if self.order == "x":
-            return self.copy(1, self.held(1 - p.x, ALL, ALL), self.b1, p.dev(x=1 - p.x))
-        return self.copy(1, self.held(ALL, ALL, 1 - p.y), self.b1, p.dev(y=1 - p.y))
-
-    def first_add(self):
-        p, zs = self.p, self.p.zs
-        wait(self.first())
-
-        def pair(j):
-            if self.order == "x":
-                z, y = lax.div(j, 2), lax.rem(j, 2)
-                return self.held(p.x, z, y), self.b1.at[z, y]
-            x, z = lax.div(j, zs), lax.rem(j, zs)
-            return self.held(x, z, p.y), self.b1.at[x, z]
-        add_slabs(2 * zs, pair)
+        if i == 0:
+            return [remote(self.away, self.landings[0], self.send.at[0], self.recv.at[0], p.dev(c=1 - p.c))]
+        d = self.order[i - 1]
+        base = 1 + sum(len(self.others(e)) for e in self.order[:i - 1])
+        return [remote(self.part(i - 1, to), self.landings[i].at[k], self.send.at[base + k], self.recv.at[base + k], p.dev(**{d: to}))
+                for k, to in enumerate(self.others(d))]
+
+    def start(self, i):
+        start(*self.copies(i))
+
+    def done(self, i):
+        p = self.p
+        wait(*self.copies(i))
+        if i == 3:
+            value = self.part(2, getattr(p, self.order[2]))[...].astype(F32)
+            for k in range(len(self.others(self.order[2]))):
+                value = value + self.landings[3][k].astype(F32)
+            self.out[...] = value
+            return
+        dims = [e for e in "xzy" if e not in self.order[:i]]
+        count = 1
+        for e in dims:
+            count *= self.size(e)
+
+        def body(j, _):
+            at, left = {}, j
+            for e in reversed(dims):
+                at[e] = lax.rem(left, self.size(e))
+                left = lax.div(left, self.size(e))
+            index = tuple(at[e] for e in dims)
+            if i == 0:
+                into, froms = self.held(at["x"], at["z"], at["y"]), [self.landings[0].at[index]]
+            else:
+                d = self.order[i - 1]
+                into = self.part(i - 1, getattr(p, d), at)
+                froms = [self.landings[i].at[(k,) + index] for k in range(len(self.others(d)))]
+            value = into[...]
+            if len(froms) == 1:
+                value = value + froms[0][...]
+            else:
+                value = value.astype(F32)
+                for from_ in froms:
+                    value = value + from_[...].astype(F32)
+                value = value.astype(BF16)
+            into[...] = value
+            return 0
+        lax.fori_loop(0, count, body, 0)
 
     def state(self):
-        p = self.p
-        return self.held(p.x, ALL, ALL) if self.order == "x" else self.held(ALL, ALL, p.y)
-
-    def second(self):
-        p = self.p
-        if self.order == "x":
-            return self.copy(2, self.held(p.x, ALL, 1 - p.y), self.b2, p.dev(y=1 - p.y))
-        return self.copy(2, self.held(1 - p.x, ALL, p.y), self.b2, p.dev(x=1 - p.x))
-
-    def second_add(self):
-        p = self.p
-        wait(self.second())
-        add_slabs(p.zs, lambda z: (self.held(p.x, z, p.y), self.b2.at[z]))
-
-    def last(self):
-        p = self.p
-        return [self.copy(3 + k, self.held(p.x, to, p.y), self.b3.at[k], p.dev(z=to)) for k, to in enumerate(p.along_z())]
-
-    def finish(self, out):
-        p = self.p
-        wait(*self.last())
-        value = self.held(p.x, p.z, p.y)[...].astype(F32)
-        for k in range(p.zs - 1):
-            value = value + self.b3[k].astype(F32)
-        out[...] = value
+        return self.part(0, getattr(self.p, self.order[0]))
 
 
 def scatter_sems(zs):
     return zs + 2
 
 
-def landing(zs, rows, m, order, stages="0123"):
-    shapes = [(2, zs, 2, rows, m), (zs, 2, rows, m) if order == "x" else (2, zs, rows, m), (zs, rows, m), (zs - 1, rows, m)]
-    return [pltpu.VMEM(shapes[int(i)], BF16) for i in stages]
-
-
-def state_shape(zs, rows, m, order):
-    return (zs, 2, rows, m) if order == "x" else (2, zs, rows, m)
+def rest_shape(zs, rows, m, gone):
+    size = {"x": 2, "z": zs, "y": 2}
+    return tuple(size[e] for e in "xzy" if e not in gone) + (rows, m)
+
+
+def landing(zs, rows, m, order, since=0):
+    shapes = [rest_shape(zs, rows, m, "")]
+    for i, d in enumerate(order):
+        shapes.append((zs - 1 if d == "z" else 1,) + rest_shape(zs, rows, m, order[:i + 1]))
+    return [pltpu.VMEM(shape, BF16) for shape in shapes[since:]]
+
+
+def follow(chains, plan):
+    for name, i in plan:
+        if i < 0:
+            chains[name].start(-1 - i)
+        else:
+            chains[name].done(i)
+
+
+def at_steps(step, chains, plans):
+    for at, plan in enumerate(plans):
+        if plan:
+            pl.when(step == at)(functools.partial(follow, chains, plan))
 
 
 def on(step, hooks):
@@ -606,68 +631,98 @@
     return pltpu.CompilerParams(collective_id=collective_id, has_side_effects=True, vmem_limit_bytes=LIMIT)
 
 
-Q_GROUPS = ((0, 384, "zyx"), (384, 384, "zxy"), (768, 512, "zxy"), (1280, 384, "zxy"))
-FF_GROUP = 512
-
-
-def opening_body(zs, q, o, u, d, tokens, whole_q, whole_o, whole_u, whole_d, image, send, recv, swap_sem):
-    p = Place(zs)
-    meet(p)
-    swap = Swap(p, tokens, image, swap_sem)
-    a, b, c, e = (Gather(p, q, whole_q, lo, n, order, send.at[i], recv.at[i]) for i, (lo, n, order) in enumerate(Q_GROUPS))
-    others = [(o, whole_o, 0), (u, whole_u, 0), (d, whole_d, 0), (u, whole_u, 1), (d, whole_d, 1)]
-    later = [Gather(p, s, w, j * FF_GROUP, FF_GROUP, "zxy", send.at[4 + i], recv.at[4 + i]) for i, (s, w, j) in enumerate(others)]
-    start(swap.copy, swap.mine)
-    a.begin()
-    b.begin()
-    a.begun()
-    a.go(1)
-    c.begin()
-    b.begun()
-    b.go(1)
-    e.begin()
-    a.came(1)
-    a.go(2)
-    b.came(1)
-    b.go(2)
-    c.begun()
-    c.go(1)
-    for g in later[:3]:
-        g.begin()
-    e.begun()
-    e.go(1)
-    for g in later[3:]:
-        g.begin()
-    c.came(1)
-    c.go(2)
-    e.came(1)
-    e.go(2)
-    for g in (a, b, c, e):
-        g.came(2)
-        g.go(3)
-    for g in later:
-        g.begun()
-    wait(swap.copy, swap.mine)
-    for g in (a, b, c, e):
-        g.rest(0, 1, 2)
-
-
-def opening(q, o, u, d, tokens, zs):
-    whole = lambda s: jax.ShapeDtypeStruct((2, zs, 2, 2) + s.shape, s.dtype)
-    return pl.pallas_call(
-        functools.partial(opening_body, zs),
-        out_shape=[whole(q), whole(o), whole(u), whole(d), jax.ShapeDtypeStruct((2 * tokens.shape[1], tokens.shape[2]), BF16)],
-        in_specs=[HBM] * 5,
-        out_specs=[HBM] * 5,
-        scratch_shapes=[DMA((9, gather_sems(zs))), DMA((9, gather_sems(zs))), DMA((3,))],
-        compiler_params=params(0),
-        name="opening",
-    )(q, o, u, d, tokens)
-
-
-QKV_TILE = 256
+Q_ORDERS = ('zxy', 'xyz', 'zxy', 'yzx', 'zyx', 'yzx')
+O_ORDER = 'xzy'
+U_ORDERS = ('xzy', 'zxy', 'xzy', 'yzx')
+D_ORDERS = ('yzx', 'yzx', 'zyx', 'xyz')
+FEED_SINCE = (2, 1, 1)
+FEED_ORDERS = ('xyz', 'xzy', 'yxz', 'xyz')
+LATE_ORDERS = ('yxz', 'yxz', 'xzy', 'xyz')
+O_BACK_ORDER = 'yxz'
+CLOSING = ((0, 0, 384, 'yxz'), (0, 384, 384, 'xyz'), (1, 0, 384, 'yzx'), (1, 384, 384, 'zxy'))
+ATTENTION_LEAVES = (('U1', 2), ('D1', 2), ('U2', 1), ('D2', 1), ('U3', 1), ('D3', 1))
+OPENING_PLAN = (('T', -1), (0, -1), (1, -1), (2, -1), (3, -1), (5, -1), (1, 0), ('O', -1), (3, 0), (1, -2), (5, 0), ('D0', -1), (2, 0), (3, -2), (1, 1), ('D1', -1), ('O', 0), (2, -2), ('D0', 0), ('U3', -1), (0, 0), (1, -3), ('T', 0), ('T', -2), ('D1', 0), ('U3', 0), (2, 1), (0, -2), (2, -3), (3, 1), (4, -1), ('T', 1), ('T', -3), (2, 2), (2, -4), (0, 1), (0, -3), (3, -3), (2, 3), (4, 0), (4, -2), (5, -2), (1, 2), (1, -4), ('O', -2), ('T', 2), ('T', -4), (1, 3), (3, 2), (3, -4), ('U0', -1), (4, 1), (0, 2), (0, -4), (3, 3), (5, 1), ('D0', -2), ('U0', 0), (4, -3), (0, 3), ('T', 3), (5, -3),)
+ATTENTION_PLANS = (
+    (),
+    (),
+    (),
+    (),
+    (),
+    ((4, 2), (4, -4), ('C', -1),),
+    (('O', 1), ('O', -3), ('U0', -2), (5, 2), (5, -4), ('U2', -1),),
+    ((4, 3),),
+    ((5, 3), ('D0', 1), ('U1', -1), ('U2', 0), ('D0', -3),),
+    (('C', 0), ('C', -2),),
+    (),
+    (),
+    (('O', 2), ('O', -4),),
+    (),
+    (('U1', 0), ('D1', -2), ('O', 3), ('U0', 1), ('U0', -3), ('D2', -1),),
+    (('C', 1), ('C', -3),),
+    (('D0', 2), ('D0', -4), ('U1', -2),),
+    (),
+    (('D0', 3),),
+    (('U0', 2), ('U0', -4), ('D2', 0), ('C', 2), ('C', -4),),
+    (),
+    (('U1', 1), ('D3', -1), ('U0', 3),),
+    (('D1', 1),),
+    (),
+)
+ATTENTION_END = (('D3', 0), ('C', 3),)
+FEED_PLANS = (
+    (('U1', -3), ('D1', -3), ('U2', -2), ('D2', -2), ('U3', -2),),
+    (),
+    (),
+    (('D1', 2), ('D1', -4), ('D2', 1), ('D2', -3), ('D3', -2),),
+    (('u0', -1), ('d0', -1), ('U1', 2), ('U1', -4), ('D1', 3), ('D3', 1), ('U2', 1), ('U2', -3), ('D3', -3), ('U3', 1), ('U3', -3), ('U1', 3),),
+    (('u0', 0), ('d0', 0),),
+    (('D2', 2), ('D2', -4), ('u0', -2),),
+    (('U2', 2), ('U2', -4), ('D2', 3),),
+    (('u1', -1), ('d1', -1), ('U3', 2), ('d0', -2), ('U3', -4), ('U2', 3),),
+    (('D3', 2), ('D3', -4),),
+    (('U3', 3),),
+    (('u1', 0), ('u1', -2), ('d1', 0), ('D3', 3), ('u0', 1), ('d1', -2),),
+    (),
+    (('d0', 1),),
+    (),
+    (('u1', 1), ('d1', 1),),
+)
+FEED_END = ()
+BACKWARD_PLANS = (
+    (('u0', -3), ('d0', -3), ('u1', -3), ('d1', -3), ('u2', -1), ('d2', -1), ('u3', -1), ('d3', -1), ('R', -1),),
+    (),
+    (),
+    (),
+    (),
+    (('u0', 2), ('u0', -4), ('d0', 2), ('d0', -4), ('u1', 2), ('u1', -4), ('d1', 2), ('d1', -4), ('R', 0), ('R', -2), ('u2', 0), ('o', -1), ('u2', -2), ('d2', 0), ('u3', 0), ('u3', -2), ('d3', 0),),
+    (('d0', 3), ('d2', -2),),
+    (('o', 0),),
+    (('R', 1), ('d3', -2),),
+    (),
+    (('u0', 3), ('u1', 3), ('d1', 3), ('u2', 1), ('o', -2),),
+    (('u3', 1), ('u2', -3), ('u3', -3),),
+    (('d2', 1),),
+    (('d3', 1), ('d2', -3), ('d3', -3),),
+    (('u2', 2), ('u2', -4), ('R', -3),),
+    (('o', 1), ('u3', 2), ('u3', -4),),
+    (('d3', 2), ('d3', -4), ('d2', 2), ('o', -3), ('d2', -4), ('u3', 3), ('u2', 3),),
+    (('R', 2), ('R', -4),),
+    (),
+    (('o', 2), ('o', -4),),
+)
+BACKWARD_END = (('d3', 3), ('d2', 3), ('R', 3), ('o', 3),)
+CLOSING_PLANS = (
+    ((0, -1), (1, -1),),
+    ((2, -1), (3, -1),),
+    ((0, 0), (0, -2), (1, 0), (1, -2),),
+    ((2, 0), (2, -2), (3, 0), (3, -2),),
+)
+CLOSING_END = (('S', -1), ('G', -1), (1, 1), ('S', 0), ('S', -2), (0, 1), (1, -3), ('S', 1), (0, -3), ('G', 0), ('G', -2), (2, 1), ('S', -3), (2, -3), (1, 2), (0, 2), (3, 1), (0, -4), (3, -3), ('S', 2), ('G', 1), ('G', -3), (3, 2), (3, -4), (3, 3), (0, 3), ('S', -4), ('G', 2), ('G', -4), (2, 2), (1, -4), (2, -4), (2, 3), ('S', 3), (1, 3), ('G', 3),)
+
+
 Q_TILE = 256
 ROWS = 256
+FF_GROUP = 512
 
 
 def full(shape):
@@ -681,35 +736,42 @@
     return pl.BlockSpec(shape, at)
 
 
-def project_step(step, per_part, joined, gains, kept, blocks):
-    part = lax.div(step, per_part)
-    tile = lax.rem(step, per_part)
-    matrix = head_mean_matrix(QKV_TILE)
-    cols = pl.ds(pl.multiple_of(tile * QKV_TILE, QKV_TILE), QKV_TILE)
+def tile_of(part, s):
+    i = jnp.clip(s - 4 * part, 0, 3)
+    column = lax.div(i, 2)
+    return lax.rem(i, 2) * 2 + (1 - column if part == 0 else column)
+
+
+def project_step(step, joined, gains, kept, blocks):
+    tile = joined.shape[1]
     qn_s, kn_s, v_s = kept
     qn, kn, v, q_raw, k_raw = blocks
-
-    @pl.when(part == 0)
+    matrix = head_mean_matrix(tile)
+
+    def cols(part):
+        return pl.ds(pl.multiple_of(tile_of(part, step) * tile, tile), tile)
+
+    @pl.when(step < 4)
+    def _():
+        value = joined.astype(BF16)
+        v[...] = value
+        v_s[:, cols(0)] = value
+
+    @pl.when((step >= 4) & (step < 8))
+    def _():
+        hat, _f = head_stats(joined, matrix)
+        value = (hat * gains[1:2]).astype(BF16)
+        kn[...] = value
+        kn_s[:, cols(1)] = value
+        k_raw[...] = joined.astype(BF16)
+
+    @pl.when(step >= 8)
     def _():
         hat, _f = head_stats(joined, matrix)
         value = (hat * gains[0:1] * (HD ** -0.5)).astype(BF16)
         qn[...] = value
-        qn_s[:, cols] = value
+        qn_s[:, cols(2)] = value
         q_raw[...] = joined.astype(BF16)
-
-    @pl.when(part == 1)
-    def _():
-        hat, _f = head_stats(joined, matrix)
-        value = (hat * gains[1:2]).astype(BF16)
-        kn[...] = value
-        kn_s[:, cols] = value
-        k_raw[...] = joined.astype(BF16)
-
-    @pl.when(part == 2)
-    def _():
-        value = joined.astype(BF16)
-        v[...] = value
-        v_s[:, cols] = value
 
 
 def attend_step(query_all, keys, values, mixed_s, cols, mixed, inverse):
@@ -731,96 +793,86 @@
         inverse[at] = inv
 
 
+PROJECT_STEPS = 12
+
+
+def first_after(plans, name):
+    return max([at for at, plan in enumerate(plans) if (name, 3) in plan], default=0)
+
+
 def attention_body(
-    zs, per_part, pairs, image, norms, gains, w, cot_in, u, d, _o, _u, _d,
-    first, qn, kn, v, q_raw, k_raw, mixed, inverse, middle, second, cot, whole_o, whole_u, whole_d,
-    held, qn_s, kn_s, v_s, mixed_s, out_w, send, recv, swap_sem,
+    zs, pairs, qk_gains, q_in, o_in, u_in, d_in, tokens, cot_in,
+    first, qn, kn, v, q_raw, k_raw, mixed, inverse, middle, second, norms, image, cot, whole_q, whole_o, whole_u, whole_d,
+    image_v, qn_s, kn_s, v_s, mixed_s, out_w, tiles, q_v, o_v, u_v, d_v, cot_v, side_v, local_sem, send, recv, swap_sem,
 ):
     step = pl.program_id(0)
     p = Place(zs)
-    length = image.shape[0]
-    head0, row0 = 3 * per_part, 3 * per_part + pairs
+    length = image_v.shape[0]
+    half = whole_o.shape[5]
+    tile = half // 2
+    head0, row0 = PROJECT_STEPS, PROJECT_STEPS + pairs
     n = FF_GROUP
-    swap = Swap(p, cot_in, cot, swap_sem)
-    o = Gather(p, None, whole_o, 0, whole_o.shape[5], "zxy", send.at[0], recv.at[0])
-    u0 = Gather(p, None, whole_u, 0, n, "zxy", send.at[1], recv.at[1])
-    d0 = Gather(p, None, whole_d, 0, n, "zyx", send.at[2], recv.at[2])
-    u1 = Gather(p, None, whole_u, n, n, "zxy", send.at[3], recv.at[3])
-    d1 = Gather(p, None, whole_d, n, n, "zxy", send.at[4], recv.at[4])
-    nexts = [Gather(p, s, t, j * n, n, "zxy", send.at[5 + i], recv.at[5 + i])
-             for i, (s, t, j) in enumerate(((u, whole_u, 2), (d, whole_d, 2), (u, whole_u, 3), (d, whole_d, 3)))]
-    load = pltpu.make_async_copy(whole_o, out_w, swap_sem.at[3])
-
-    def h0():
+    mine = pl.ds(pl.multiple_of(p.x * (length // 2), length // 2), length // 2)
+    chains = {
+        "T": Swap(p, tokens.at[1 - p.x], half_rows(image_v, p.x, length // 2), swap_sem.at[0]),
+        "C": Swap(p, cot_in.at[1 - p.x], half_rows(cot, p.x, length // 2), swap_sem.at[1]),
+    }
+    local = lambda i, src, dst: pltpu.make_async_copy(src, dst, local_sem.at[i])
+    own_shards = [local(i, a, b) for i, (a, b) in enumerate(((q_in, q_v), (o_in, o_v), (u_in, u_v), (d_in, d_v)))]
+    own_tokens = local(4, tokens.at[p.x], image_v.at[mine])
+    own_cot = [local(5, cot_in.at[p.x], cot_v), local(6, cot_v, cot.at[mine])]
+    keep_image = local(7, image_v, image)
+    side = local(8, whole_q.at[0, :, :, :, :, pl.ds(3 * half, PAIR)], side_v)
+    load_out = local(9, whole_o, out_w)
+    starts = (2 * half + tile, 2 * half, half, half + tile, 0, tile)
+    for i, lo in enumerate(starts):
+        chains[i] = Gather(p, q_v, whole_q, lo, tile + PAIR if i == 0 else tile, Q_ORDERS[i], send.at[i], recv.at[i])
+
+    def load_tile(i):
+        return local(10 + i % 2, whole_q.at[:, :, :, :, :, pl.ds(starts[i], tile)], tiles.at[i % 2])
+
+    chains["O"] = Gather(p, o_v, whole_o, 0, half, O_ORDER, send.at[6], recv.at[6])
+    for j in range(4):
+        chains[f"U{j}"] = Gather(p, u_v, whole_u, j * n, n, U_ORDERS[j], send.at[7 + j], recv.at[7 + j])
+        chains[f"D{j}"] = Gather(p, d_v, whole_d, j * n, n, D_ORDERS[j], send.at[11 + j], recv.at[11 + j])
+
+    @pl.when(step == 0)
+    def _():
+        start(*own_shards, own_tokens, own_cot[0])
         meet(p)
-        o.go(1)
-        d0.go(1)
-        nexts[0].begin()
-        nexts[1].begin()
-
-    def h3():
-        o.came(1)
-        o.go(2)
-        d0.came(1)
-        u0.go(1)
-
-    def h6():
-        u0.came(1)
-        u0.go(2)
-        u1.go(1)
-        d0.go(2)
-
-    def h9():
-        u1.came(1)
-        u1.go(2)
-        d1.go(1)
-        nexts[2].begin()
-        nexts[3].begin()
-
-    def h12():
-        d1.came(1)
-        d1.go(2)
-        start(swap.copy, swap.mine)
-
-    def h15():
-        o.came(2)
-        o.go(3)
-
-    def h18():
-        u0.came(2)
-        u0.go(3)
-        o.rest(0, 1, 2)
-        load.start()
-
-    def h19():
-        d0.came(2)
-        d0.go(3)
-
-    def h20():
-        load.wait()
-
-    def h22():
-        u1.came(2)
-        u1.go(3)
-
-    on(step, {0: h0, 3: h3, 6: h6, 9: h9, 12: h12, 15: h15, 18: h18, 19: h19, 20: h20, 22: h22})
-
-    @pl.when(step == 0)
-    def _():
-        rows = length // 4
+        wait(*own_shards)
+        follow(chains, OPENING_PLAN)
+        load_tile(0).start()
+        side.start()
+        own_cot[0].wait()
+        own_cot[1].start()
+        side.wait()
+        norms[...] = side_v[...].reshape(-1, PAIR).astype(F32).T[:8]
+        own_tokens.wait()
+        keep_image.start()
 
         def norm(i, _):
-            at = pl.ds(i * rows, rows)
-            hat, _f = stats(image[at].astype(F32))
-            value = (hat * norms[0:1] + norms[2:3]).astype(BF16)
-            held[at] = value
-            first[at] = value
+            at = pl.ds(pl.multiple_of(i * ROWS, ROWS), ROWS)
+            hat, _f = stats(image_v[at].astype(F32))
+            first[at] = (hat * norms[0:1] + norms[2:3]).astype(BF16)
             return 0
-        lax.fori_loop(0, 4, norm, 0)
+        lax.fori_loop(0, length // ROWS, norm, 0)
+
+    at_steps(step, chains, ATTENTION_PLANS)
+
+    on(step, {0: lambda: load_tile(0).wait()})
+    for i in range(1, 6):
+        on(step, {max(2 * i - 2, first_after(ATTENTION_PLANS, i)): lambda i=i: load_tile(i).start()})
+        on(step, {2 * i: lambda i=i: load_tile(i).wait()})
+    on(step, {max(1, first_after(ATTENTION_PLANS, "O")): lambda: load_out.start()})
+    on(step, {row0: lambda: load_out.wait()})
 
     @pl.when(step < head0)
     def _():
-        project_step(step, per_part, nn(held[...], w[0]), gains, (qn_s, kn_s, v_s), (qn, kn, v, q_raw, k_raw))
+        gains = qk_gains[...].astype(F32)
+        gains = jnp.concatenate([gains] * (tile // HD), axis=1)
+        w = tiles[lax.rem(lax.div(step, 2), 2), lax.rem(step, 2)].reshape(-1, tile)
+        project_step(step, nn(first[...], w), gains, (qn_s, kn_s, v_s), (qn, kn, v, q_raw, k_raw))
 
     @pl.when((step >= head0) & (step < row0))
     def _():
@@ -830,57 +882,51 @@
     @pl.when(step >= row0)
     def _():
         at = pl.ds(pl.multiple_of((step - row0) * ROWS, ROWS), ROWS)
-        half = out_w.shape[5]
         w0, w1 = (out_w[t].reshape(-1, half) for t in range(2))
-        value = image[at].astype(F32) + nt(mixed_s[at, :half], w0) + nt(mixed_s[at, half:], w1)
+        value = image_v[at].astype(F32) + nt(mixed_s[at, :half], w0) + nt(mixed_s[at, half:], w1)
         middle[...] = value
         hat, _f = stats(value)
         second[...] = (hat * norms[1:2] + norms[3:4]).astype(BF16)
 
     @pl.when(step == pl.num_programs(0) - 1)
     def _():
-        d1.came(2)
-        d1.go(3)
-        for g in nexts:
-            g.begun()
-        wait(swap.copy, swap.mine)
-        for g in (u0, d0, u1, d1):
-            g.rest(0, 1, 2)
-
-
-def attention(image, norms, gains, w, cols, cot, u, d, whole_o, whole_u, whole_d, zs):
-    length, width = image.shape
-    half = cols // 3
-    per_half = half // QKV_TILE
-    per_part = 2 * per_half
+        follow(chains, ATTENTION_END)
+        for name, stages in ATTENTION_LEAVES:
+            chains[name].rest(0, stages - 1)
+        wait(own_cot[1], keep_image)
+
+
+def attention(qk_gains, q, o, u, d, tokens, cot, zs):
+    rows = q.shape[0]
+    length, width = 2 * tokens.shape[1], tokens.shape[2]
+    half = o.shape[1]
     pairs = 2 * half // PAIR
-    head0, row0 = 3 * per_part, 3 * per_part + pairs
-    steps = row0 + length // ROWS
-
-    def w_map(s):
-        s = jnp.minimum(s, head0 - 1)
-        part, rest = s // per_part, s % per_part
-        return rest // per_half, 0, part * per_half + rest % per_half
-
-    tiles = lambda part: clipped((length, QKV_TILE), 1, part * per_part, per_part)
+    head0, row0 = PROJECT_STEPS, PROJECT_STEPS + pairs
+    tile = half // 2
+    tiles = lambda part: pl.BlockSpec((length, tile), lambda s: (0, tile_of(part, s)))
     heads = clipped((length, PAIR), 1, head0, pairs)
-    rows = clipped((ROWS, width), 0, row0, length // ROWS)
+    by_rows = clipped((ROWS, width), 0, row0, length // ROWS)
     bf = jax.ShapeDtypeStruct((length, 2 * half), BF16)
-    same = lambda a: jax.ShapeDtypeStruct(a.shape, a.dtype)
+    square = jax.ShapeDtypeStruct((length, width), BF16)
+    f32 = lambda *shape: jax.ShapeDtypeStruct(shape, F32)
+    whole = lambda s: jax.ShapeDtypeStruct((2, zs, 2, 2) + s.shape, BF16)
     store = pltpu.VMEM((length, 2 * half), BF16)
+    same = lambda s: pltpu.VMEM(s.shape, BF16)
     return pl.pallas_call(
-        functools.partial(attention_body, zs, per_part, pairs),
-        grid=(steps,),
-        in_specs=[full(image.shape), full(norms.shape), full(gains.shape), pl.BlockSpec((1, width, QKV_TILE), w_map)] + [HBM] * 6,
-        out_specs=[full((length, width)), tiles(0), tiles(1), tiles(2), tiles(0), tiles(1), heads, heads, rows, rows] + [HBM] * 4,
-        out_shape=[same(image), bf, bf, bf, bf, bf, bf, jax.ShapeDtypeStruct((length, 2 * half), F32),
-                   jax.ShapeDtypeStruct((length, width), F32), same(image), same(image), same(whole_o), same(whole_u), same(whole_d)],
-        scratch_shapes=[pltpu.VMEM((length, width), BF16), store, store, store, store, pltpu.VMEM(whole_o.shape, BF16),
-                        DMA((9, gather_sems(zs))), DMA((9, gather_sems(zs))), DMA((4,))],
-        input_output_aliases={7: 11, 8: 12, 9: 13},
-        compiler_params=params(1),
+        functools.partial(attention_body, zs, pairs),
+        grid=(row0 + length // ROWS,),
+        in_specs=[full(qk_gains.shape)] + [HBM] * 6,
+        out_specs=[full((length, width)), tiles(2), tiles(1), tiles(0), tiles(2), tiles(1), heads, heads, by_rows, by_rows,
+                   full((8, width))] + [HBM] * 6,
+        out_shape=[square, bf, bf, bf, bf, bf, bf, f32(length, 2 * half), f32(length, width), square, f32(8, width),
+                   square, square, whole(q), whole(o), whole(u), whole(d)],
+        scratch_shapes=[pltpu.VMEM((length, width), BF16), store, store, store, store, pltpu.VMEM((2, zs, 2, 2, rows, half), BF16),
+                        pltpu.VMEM((2, 2, zs, 2, 2, rows, tile), BF16), same(q), same(o), same(u), same(d),
+                        pltpu.VMEM((length // 2, width), BF16), pltpu.VMEM((zs, 2, 2, rows, PAIR), BF16),
+                        DMA((12,)), DMA((15, gather_sems(zs))), DMA((15, gather_sems(zs))), DMA((2, 2, CHUNKS))],
+        compiler_params=params(0),
         name="attention",
-    )(image, norms, gains, w, cot, u, d, whole_o, whole_u, whole_d)
+    )(qk_gains, q, o, u, d, tokens, cot)
 
 
 def gelu_parts(v):
@@ -891,33 +937,32 @@
     return jnp.where(v >= 0, 1.0 - tail, tail), bell * 0.3989422804014327
 
 
-FEED_ORDERS = ("y", "x")
-
-
 def feed_body(
     zs, second, cot, middle, _u, _d,
-    result, grad_second, grad_u, grad_d, state_u, state_d, whole_u, whole_d,
+    result, grad_second, grad_u, grad_d, state_0, state_1, state_2, state_3, outputs, whole_u, whole_d,
     acc, second_t, cot_t, active, grad_hidden, tiles, g, tile_sem, misc_sem, send, recv, *landings,
 ):
     step = pl.program_id(0)
     p = Place(zs)
     length = second.shape[0]
     n = FF_GROUP
-    u2 = Gather(p, None, whole_u, 2 * n, n, "zxy", send.at[0], recv.at[0])
-    d2 = Gather(p, None, whole_d, 2 * n, n, "zyx", send.at[1], recv.at[1])
-    u3 = Gather(p, None, whole_u, 3 * n, n, "zxy", send.at[2], recv.at[2])
-    d3 = Gather(p, None, whole_d, 3 * n, n, "zyx", send.at[3], recv.at[3])
-    groups = []
+    state_refs = (state_0, state_1, state_2, state_3)
+    chains = {}
+    for j in (1, 2, 3):
+        for i, (name, w, orders) in enumerate((("U", whole_u, U_ORDERS), ("D", whole_d, D_ORDERS))):
+            k = 2 * j - 2 + i
+            chains[f"{name}{j}"] = Gather(p, None, w, j * n, n, orders[j], send.at[k], recv.at[k], FEED_SINCE[j - 1])
+    at, states = iter(landings), []
     for j in range(2):
         for k in range(2):
             i = 2 * j + k
             held = lambda x, z, y, j=j, k=k: g.at[k, j, x, z, y, p.c]
-            groups.append(Scatter(p, FEED_ORDERS[k], held, g.at[k, j, :, :, :, 1 - p.c], *landings[2 * i:2 * i + 2], None, None,
-                                  send.at[4 + i], recv.at[4 + i]))
-    su0, sd0, su1, sd1 = groups
+            s = Scatter(p, FEED_ORDERS[i], held, g.at[k, j, :, :, :, 1 - p.c], [next(at), next(at)], send.at[6 + i], recv.at[6 + i])
+            chains[f"{'ud'[k]}{j}"] = s
+            states.append(pltpu.make_async_copy(s.state(), state_refs[i], misc_sem.at[1 + i]))
     init = pltpu.make_async_copy(middle, acc, misc_sem.at[0])
-    states = [pltpu.make_async_copy(s.state(), (state_u, state_d)[k].at[j], misc_sem.at[1 + 2 * j + k])
-              for j in range(2) for k, s in ((0, groups[2 * j]), (1, groups[2 * j + 1]))]
+    mine = pl.ds(pl.multiple_of(p.x * (length // 2), length // 2), length // 2)
+    own = pltpu.make_async_copy(result.at[mine], outputs.at[p.x], misc_sem.at[9])
     outs = [pltpu.make_async_copy(g.at[k, j], (grad_u, grad_d)[k].at[j - 2], misc_sem.at[5 + 2 * (j - 2) + k])
             for j in (2, 3) for k in range(2)]
 
@@ -934,59 +979,16 @@
         start(*loads(0))
         start(*loads(1))
         init.start()
-        for w in (u2, d2, u3, d3):
-            w.go(1)
+        follow(chains, FEED_PLANS[0])
         second_t[...] = second[...].T
         cot_t[...] = cot[...].T
         grad_second[...] = jnp.zeros_like(grad_second)
 
-    def h1():
-        start(*loads(2))
-        for w in (u2, d2):
-            w.came(1)
-            w.go(2)
-
-    def h2():
-        start(*loads(3))
-        start(su0.core(), sd0.core())
-        for w in (u3, d3):
-            w.came(1)
-            w.go(2)
-
-    def h3():
-        su0.core_add()
-        sd0.core_add()
-        start(su0.first(), sd0.first())
-        for w in (u2, d2):
-            w.came(2)
-            w.go(3)
-
-    def h4():
-        for w in (u2, d2):
-            w.rest(0, 1, 2)
-        start(*loads(4))
-        start(*loads(5))
-        start(su1.core(), sd1.core())
-        for w in (u3, d3):
-            w.came(2)
-            w.go(3)
-
-    def h5():
-        for w in (u3, d3):
-            w.rest(0, 1, 2)
-        start(*loads(6))
-        su1.core_add()
-        sd1.core_add()
-        start(su1.first(), sd1.first())
-
-    def h6():
-        start(*loads(7))
-        su0.first_add()
-        sd0.first_add()
-        start(*states[:2])
-        start(*outs[:2])
-
-    on(step, {1: h1, 2: h2, 3: h3, 4: h4, 5: h5, 6: h6})
+    at_steps(step, chains, ((),) + FEED_PLANS[2::2])
+    for s in range(2, 8):
+        here = first_after(FEED_PLANS, f"U{s // 2}"), first_after(FEED_PLANS, f"D{s // 2}")
+        on(step, {max(s - 1, (max(here) + 1) // 2): lambda s=s: start(*loads(s))})
+    on(step, {7: lambda: start(*outs[:2])})
     wait(*loads(step))
 
     @pl.when(step == 0)
@@ -1006,6 +1008,7 @@
         grad_hidden[at] = b
         acc[at] += nt(a, w_down)
         grad_second[at] += nt(b, w_up)
+    at_steps(step, chains, FEED_PLANS[1::2])
     j, t = lax.div(step, 2), lax.rem(step, 2)
     shape = g.shape[3:]
     g[0, j, t] = nn(second_t[...], grad_hidden[...]).astype(BF16).reshape(shape)
@@ -1015,11 +1018,12 @@
     def _():
         start(*outs[2:])
         result[...] = acc[...].astype(BF16)
-        su1.first_add()
-        sd1.first_add()
-        start(*states[2:])
+        own.start()
+        follow(chains, FEED_END)
+        start(*states)
         wait(*states)
         wait(*outs)
+        own.wait()
 
 
 def feed(second, cot, middle, whole_u, whole_d, zs):
@@ -1031,28 +1035,25 @@
     square = pltpu.VMEM((length, width), BF16)
     strip = pltpu.VMEM((length, n), BF16)
     scratch = [pltpu.VMEM((length, width), F32), square, square, strip, strip, pltpu.VMEM((2, 2) + tile[1:], BF16),
-               pltpu.VMEM((2, 4) + tile, BF16), DMA((2, 2)), DMA((9,)), DMA((8, gather_sems(zs))), DMA((8, gather_sems(zs)))]
+               pltpu.VMEM((2, 4) + tile, BF16), DMA((2, 2)), DMA((10,)), DMA((10, gather_sems(zs))), DMA((10, gather_sems(zs)))]
     for i in range(4):
-        scratch += landing(zs, rows, n, FEED_ORDERS[i % 2], "01")
+        scratch += landing(zs, rows, n, FEED_ORDERS[i])[:2]
     return pl.pallas_call(
         functools.partial(feed_body, zs),
         grid=(8,),
         in_specs=[full(second.shape), full(cot.shape), HBM, HBM, HBM],
-        out_specs=[full(second.shape), full(second.shape)] + [HBM] * 6,
+        out_specs=[full(second.shape), full(second.shape)] + [HBM] * 9,
         out_shape=[same(second), jax.ShapeDtypeStruct((length, width), F32), grads, grads]
-        + [jax.ShapeDtypeStruct((2,) + state_shape(zs, rows, n, o), BF16) for o in FEED_ORDERS]
-        + [same(whole_u), same(whole_d)],
+        + [jax.ShapeDtypeStruct(rest_shape(zs, rows, n, o[0]), BF16) for o in FEED_ORDERS]
+        + [jax.ShapeDtypeStruct((2, length // 2, width), BF16), same(whole_u), same(whole_d)],
         scratch_shapes=scratch,
-        input_output_aliases={3: 6, 4: 7},
-        compiler_params=params(2),
+        input_output_aliases={3: 9, 4: 10},
+        compiler_params=params(1),
         name="feed",
     )(second, cot, middle, whole_u, whole_d)
 
 
-LATE_ORDERS = ("x", "y", "y", "y")
-
-
-def attend_back_step(gains, go, inv, query, keys, values, q_raw, k_raw, mixed, grad_q, grad_k, grad_v, grad_gains):
+def attend_back_step(between, gains, go, inv, query, keys, values, q_raw, k_raw, mixed, grad_q, grad_k, grad_v, grad_gains):
     length = query.shape[0]
     lanes = lax.broadcasted_iota(jnp.int32, (1, PAIR), 1)
     first = lanes < HD
@@ -1073,6 +1074,8 @@
     dk = jnp.zeros((length, PAIR), F32)
     dv = jnp.zeros((length, PAIR), F32)
     for i in range(length // Q_TILE):
+        if 2 * i == length // Q_TILE:
+            between()
         at = slice(i * Q_TILE, (i + 1) * Q_TILE)
         part = jnp.zeros((Q_TILE, PAIR), F32)
         for qm, km, gm, ga, va in heads:
@@ -1097,9 +1100,9 @@
 
 def backward_body(
     zs, rows_steps, norms, gains, cot, grad_second, middle, mixed_rows, w, qn, kn, v, q_raw, k_raw, mixed, inverse,
-    grads_u, grads_d, state_u, state_d, result,
+    grads_u, grads_d, state_0, state_1, state_2, state_3, result, _outputs,
     grad_middle, grad_q, grad_k, grad_v, grad_gains, sums, shard_u, shard_d, shard_o, outputs,
-    grad_mixed, acc, g_o, own_early, own_late, load_sem, swap_sem, send, recv, *landings,
+    grad_mixed, acc, g_o, own_late, load_sem, swap_sem, send, recv, *landings,
 ):
     step = pl.program_id(0)
     p = Place(zs)
@@ -1107,85 +1110,43 @@
     half = w.shape[2]
     at = iter(landings)
     take = lambda count: [next(at) for _ in range(count)]
-    early, late, loads = [], [], []
-    for i in range(4):
+    chains, loads = {}, []
+
+    def out(k, j):
+        return (shard_u, shard_d)[k].at[:, pl.ds(j * n, n)]
+
+    for i, state in enumerate((state_0, state_1, state_2, state_3)):
         j, k = divmod(i, 2)
-        order = FEED_ORDERS[k]
-        state = (state_u, state_d)[k].at[j]
-        if order == "x":
-            far, near = state.at[:, 1 - p.y], state.at[:, p.y]
-        else:
-            far, near = state.at[1 - p.x], state.at[p.x]
-        b2, b3 = take(2)
-        s = Scatter(p, order, lambda x, z, y, i=i: own_early.at[i, z], None, None, None, b2, b3, send.at[i], recv.at[i])
-        s.second = lambda s=s, far=far, order=order: s.copy(2, far, s.b2, p.dev(y=1 - p.y) if order == "x" else p.dev(x=1 - p.x))
-        early.append(s)
-        loads.append(pltpu.make_async_copy(near, own_early.at[i], load_sem.at[i]))
+        order = FEED_ORDERS[i]
+        own = next(at)
+
+        def held(x, z, y, own=own, order=order):
+            return own.at[tuple(index for e, index in zip("xzy", (x, z, y)) if e != order[0])]
+        chains[f"{'ud'[k]}{j}"] = Scatter(p, order, held, None, [None, None] + take(2), send.at[i], recv.at[i], out(k, j))
+        loads.append(pltpu.make_async_copy(state, own, load_sem.at[i]))
     for i in range(4):
         j, k = divmod(i, 2)
         grad = (grads_u, grads_d)[k].at[j]
-        s = Scatter(p, LATE_ORDERS[i], lambda x, z, y, i=i: own_late.at[i, x, z, y], grad.at[:, :, :, 1 - p.c],
-                    *take(4), send.at[4 + i], recv.at[4 + i])
-        late.append(s)
+        chains[f"{'ud'[k]}{2 + j}"] = Scatter(
+            p, LATE_ORDERS[i], lambda x, z, y, i=i: own_late.at[i, x, z, y], grad.at[:, :, :, 1 - p.c], take(4),
+            send.at[4 + i], recv.at[4 + i], out(k, 2 + j))
         loads.append(pltpu.make_async_copy(grad.at[:, :, :, p.c], own_late.at[i], load_sem.at[4 + i]))
-    so = Scatter(p, "y", lambda x, z, y: g_o.at[x, z, y, p.c], g_o.at[:, :, :, 1 - p.c], *take(4), send.at[8], recv.at[8])
-    swap = SwapBack(p, result, outputs, swap_sem)
-
-    def out(k, j):
-        return (shard_u, shard_d)[k].at[:, pl.ds(j * n, n)]
-
-    def h0():
+    chains["o"] = Scatter(p, O_BACK_ORDER, lambda x, z, y: g_o.at[x, z, y, p.c], g_o.at[:, :, :, 1 - p.c], take(4),
+                          send.at[8], recv.at[8], shard_o)
+    half_length = result.shape[0] // 2
+    chains["R"] = Swap(p, half_rows(result, 1 - p.x, half_length), outputs.at[p.x], swap_sem)
+
+    @pl.when(step == 0)
+    def _():
+        start(*loads)
         meet(p)
-        start(*loads)
-        start(*[s.second() for s in early])
-        start(*[s.core() for s in late[:2]])
-
-    def h2():
         wait(*loads)
-        for s in late[:2]:
-            s.core_add()
-            s.first().start()
-        start(*[s.core() for s in late[2:]])
-
-    def h4():
-        so.core().start()
-        for s in early:
-            s.second_add()
-            start(*s.last())
-        for s in late[2:]:
-            s.core_add()
-            s.first().start()
-
-    def h5():
-        so.core_add()
-        so.first().start()
-
-    def h6():
-        for s in late[:2]:
-            s.first_add()
-            s.second().start()
-        start(swap.copy, swap.mine)
-
-    def h9():
-        for s in late[2:]:
-            s.first_add()
-            s.second().start()
-        for s in late[:2]:
-            s.second_add()
-            start(*s.last())
-
-    def h10():
-        so.first_add()
-        so.second().start()
-        for i, s in enumerate(early):
-            s.finish(out(i % 2, i // 2))
-
-    def h11():
-        for s in late[2:]:
-            s.second_add()
-            start(*s.last())
-
-    on(step, {0: h0, 2: h2, 4: h4, 5: h5, 6: h6, 9: h9, 10: h10, 11: h11})
+        follow(chains, BACKWARD_PLANS[0])
+
+    at_steps(step, chains, ((),) + BACKWARD_PLANS[1:rows_steps] + BACKWARD_PLANS[rows_steps::2])
+
+    def between():
+        at_steps(step, chains, ((),) * rows_steps + BACKWARD_PLANS[rows_steps + 1::2])
 
     @pl.when(step == 0)
     def _():
@@ -1216,20 +1177,15 @@
     @pl.when(step >= rows_steps)
     def _():
         cols = pl.ds(pl.multiple_of((step - rows_steps) * PAIR, PAIR), PAIR)
-        attend_back_step(gains, grad_mixed[:, cols], inverse[...], qn[...], kn[...], v[...], q_raw[...], k_raw[...], mixed[...],
+        attend_back_step(between, gains, grad_mixed[:, cols], inverse[...], qn[...], kn[...], v[...], q_raw[...], k_raw[...], mixed[...],
                          grad_q, grad_k, grad_v, grad_gains)
 
     @pl.when(step == pl.num_programs(0) - 1)
     def _():
-        so.second_add()
-        start(*so.last())
-        for i, s in enumerate(late):
-            s.finish(out(i % 2, 2 + i // 2))
-        so.finish(shard_o)
-        wait(swap.copy, swap.mine)
-
-
-def backward(norms, gains, cot, grad_second, middle, mixed, w, kept, inverse, grads_u, grads_d, state_u, state_d, result, zs):
+        follow(chains, BACKWARD_END)
+
+
+def backward(norms, gains, cot, grad_second, middle, mixed, w, kept, inverse, grads_u, grads_d, states, result, outputs, zs):
     length, width = middle.shape
     half = w.shape[2]
     rows, n = grads_u.shape[5], FF_GROUP
@@ -1240,30 +1196,30 @@
     f32 = lambda *shape: jax.ShapeDtypeStruct(shape, F32)
     scratch = [
         pltpu.VMEM((length, 2 * half), BF16), pltpu.VMEM(w.shape, F32), pltpu.VMEM((2, zs, 2, 2, rows, half), BF16),
-        pltpu.VMEM((4, zs, rows, n), BF16), pltpu.VMEM((4, 2, zs, 2, rows, n), BF16), DMA((8,)), DMA((3,)),
+        pltpu.VMEM((4, 2, zs, 2, rows, n), BF16), DMA((8,)), DMA((2, CHUNKS)),
         DMA((9, scatter_sems(zs))), DMA((9, scatter_sems(zs))),
     ]
     for i in range(4):
-        scratch += landing(zs, rows, n, FEED_ORDERS[i % 2], "23")
+        scratch += [pltpu.VMEM(rest_shape(zs, rows, n, FEED_ORDERS[i][0]), BF16)] + landing(zs, rows, n, FEED_ORDERS[i], 2)
     for i in range(4):
         scratch += landing(zs, rows, n, LATE_ORDERS[i])
-    scratch += landing(zs, rows, half, "y")
+    scratch += landing(zs, rows, half, O_BACK_ORDER)
     return pl.pallas_call(
         functools.partial(backward_body, zs, row_steps),
         grid=(row_steps + pairs,),
-        in_specs=[full(norms.shape), full(gains.shape), row, row, row, row, full(w.shape)] + [head] * 7 + [HBM] * 5,
+        in_specs=[full(norms.shape), full(gains.shape), row, row, row, row, full(w.shape)] + [head] * 7 + [HBM] * 8,
         out_specs=[row, head, head, head, full((2, PAIR)), full((2, width)), full((rows, 4 * n)), full((rows, 4 * n)),
                    full((rows, half)), HBM],
         out_shape=[f32(length, width), heads, heads, heads, f32(2, PAIR), f32(2, width), f32(rows, 4 * n), f32(rows, 4 * n),
                    f32(rows, half), jax.ShapeDtypeStruct((2, length // 2, width), BF16)],
         scratch_shapes=scratch,
-        compiler_params=params(3),
+        input_output_aliases={21: 9},
+        compiler_params=params(2),
         name="backward",
-    )(norms, gains, cot, grad_second, middle, mixed, w, *kept, mixed, inverse, grads_u, grads_d, state_u, state_d, result)
+    )(norms, gains, cot, grad_second, middle, mixed, w, *kept, mixed, inverse, grads_u, grads_d, *states, result, outputs)
 
 
 PART_GROUP = 256
-CLOSING = ((0, 0, 768, "y"), (1, 0, 384, "y"), (1, 384, 384, "x"))
 
 
 def closing_body(
@@ -1281,14 +1237,17 @@
     load_image = pltpu.make_async_copy(image_in, image, load_sem.at[5])
     load_middle = pltpu.make_async_copy(grad_middle_in, grad_middle, load_sem.at[6])
     start(load_first, *load_grads, load_w, load_image, load_middle)
-    groups = []
+    chains = {}
+    at = iter(landings)
     for i, (k, lo, m, order) in enumerate(CLOSING):
-        at = pl.ds(lo, m)
-        held = lambda x, z, y, k=k, at=at: g.at[k, x, z, y, p.c, :, at]
-        groups.append(Scatter(p, order, held, g.at[k, :, :, :, 1 - p.c, :, at], *landings[4 * i:4 * i + 4], send.at[i], recv.at[i]))
-    a, b, c = groups
-    swap = SwapBack(p, grad_image, grad_tokens, swap_sem)
-    small = Sum(p, total, got, sum_send, sum_recv)
+        cols = pl.ds(lo, m)
+        held = lambda x, z, y, k=k, cols=cols: g.at[k, x, z, y, p.c, :, cols]
+        chains[i] = Scatter(p, order, held, g.at[k, :, :, :, 1 - p.c, :, cols], [next(at) for _ in range(4)], send.at[i], recv.at[i],
+                            shard_q.at[k, :, cols])
+    half_length = length // 2
+    chains["G"] = Swap(p, half_rows(grad_image, 1 - p.x, half_length), grad_tokens.at[p.x], swap_sem)
+    chains["S"] = Sum(p, total, got, sum_send, sum_recv)
+    own = pltpu.make_async_copy(half_rows(grad_image, p.x, half_length), grad_tokens.at[p.x], load_sem.at[7])
 
     load_first.wait()
     first_t[...] = first[...].T
@@ -1305,15 +1264,9 @@
         lax.fori_loop(0, 6, one, 0)
 
     weight_grad(0)
-    a.core().start()
+    follow(chains, CLOSING_PLANS[0])
     weight_grad(1)
-    start(b.core(), c.core())
-    a.core_add()
-    a.first().start()
-    b.core_add()
-    b.first().start()
-    c.core_add()
-    c.first().start()
+    follow(chains, CLOSING_PLANS[1])
     load_w.wait()
     acc[...] = jnp.zeros_like(acc)
 
@@ -1322,8 +1275,11 @@
         cols = pl.ds(pl.multiple_of(t * half, half), half)
         acc[...] += nt(grads[part, :, cols], w[t, :, pl.ds(pl.multiple_of(part * half, half), half)])
         return 0
-    lax.fori_loop(0, 6, to_first, 0)
+    lax.fori_loop(0, 3, to_first, 0)
+    follow(chains, CLOSING_PLANS[2])
+    lax.fori_loop(3, 6, to_first, 0)
     wait(load_image, load_middle)
+    follow(chains, CLOSING_PLANS[3])
 
     def norm_back(i, carry):
         at = pl.ds(pl.multiple_of(i * ROWS, ROWS), ROWS)
@@ -1333,35 +1289,14 @@
         return carry[0] + jnp.sum(gf * hat, 0, keepdims=True), carry[1] + jnp.sum(gf, 0, keepdims=True)
     zero = jnp.zeros((1, width), F32)
     sum_hat, sum_all = lax.fori_loop(0, length // ROWS, norm_back, (zero, zero))
-    start(swap.copy, swap.mine)
+    own.start()
     total[...] = jnp.zeros_like(total)
     total[0:1] = sum_hat
     total[1:2] = sum_all
     total[2:4] = sums_second[...]
     total[4:6, 0:PAIR] = sums_qk[...]
-    small.go(0)
-    a.first_add()
-    a.second().start()
-    small.add(0)
-    small.go(1)
-    c.first_add()
-    c.second().start()
-    small.add(1)
-    small.go(2)
-    b.first_add()
-    b.second().start()
-    small.add(2)
-    small.go(3)
-    a.second_add()
-    start(*a.last())
-    small.add(3)
-    c.second_add()
-    start(*c.last())
-    b.second_add()
-    start(*b.last())
-    for s, (k, lo, m, order) in zip(groups, CLOSING):
-        s.finish(shard_q.at[k, :, pl.ds(lo, m)])
-    wait(swap.copy, swap.mine)
+    follow(chains, CLOSING_END)
+    own.wait()
 
 
 def closing(norms, sums_second, sums_qk, image, first, grad_middle, gq, gk, gv, w, zs):
@@ -1371,9 +1306,9 @@
     square = pltpu.VMEM((length, width), BF16)
     scratch = [
         square, square, pltpu.VMEM((length, width), F32), pltpu.VMEM((3,) + gq.shape, BF16), pltpu.VMEM(w.shape, BF16), square,
-        pltpu.VMEM((length, width), F32), square, pltpu.VMEM((2, 2, zs, 2, 2, rows, wide), BF16), DMA((7,)), DMA((3,)),
+        pltpu.VMEM((length, width), F32), square, pltpu.VMEM((2, 2, zs, 2, 2, rows, wide), BF16), DMA((8,)), DMA((2, CHUNKS)),
         pltpu.VMEM((zs + 2, 8, width), F32), DMA((zs + 2,)), DMA((zs + 2,)),
-        DMA((3, scatter_sems(zs))), DMA((3, scatter_sems(zs))),
+        DMA((len(CLOSING), scatter_sems(zs))), DMA((len(CLOSING), scatter_sems(zs))),
     ]
     for k, lo, m, order in CLOSING:
         scratch += landing(zs, rows, m, order)
@@ -1384,7 +1319,7 @@
         out_shape=[jax.ShapeDtypeStruct((2, rows, wide), F32), jax.ShapeDtypeStruct((8, width), F32),
                    jax.ShapeDtypeStruct((2, length // 2, width), BF16)],
         scratch_shapes=scratch,
-        compiler_params=params(4),
+        compiler_params=params(3),
         name="closing",
     )(norms, sums_second, sums_qk, image, first, grad_middle, gq, gk, gv, w)
 
@@ -1397,17 +1332,16 @@
     cols = 3 * half
     side = jnp.concatenate([norm_gains, norm_shifts, jnp.zeros((rows, 124), BF16)], axis=1)
     shard_q = jnp.concatenate([w_qkv.reshape(rows, cols), side], axis=1)
-    whole_q, whole_o, whole_u, whole_d, image = opening(shard_q, wo_t, w_up, w_down_t, tokens, zs)
+    first, qn, kn, v, q_raw, k_raw, mixed, inverse, middle, second, norms, image, cot, whole_q, whole_o, whole_u, whole_d = attention(
+        qk_gains, shard_q, wo_t, w_up, w_down_t, tokens, cotangent, zs
+    )
+    result, grad_second, grads_u, grads_d, *states, outputs, whole_u, whole_d = feed(
+        second, cot, middle, whole_u, whole_d, zs
+    )
     qkv = whole_q.reshape(2, width, cols + 128)
-    norms = qkv[0, :, cols:cols + 4].T.astype(F32)
-    gains = qk_gains.astype(F32)
-    first, qn, kn, v, q_raw, k_raw, mixed, inverse, middle, second, cot, whole_o, whole_u, whole_d = attention(
-        image, norms, jnp.tile(gains, (1, QKV_TILE // HD)), qkv, cols, cotangent, w_up, w_down_t, whole_o, whole_u, whole_d, zs
-    )
-    result, grad_second, grads_u, grads_d, state_u, state_d, whole_u, whole_d = feed(second, cot, middle, whole_u, whole_d, zs)
     grad_middle, gq, gk, gv, sums_qk, sums_second, shard_u, shard_d, shard_o, outputs = backward(
-        norms, jnp.tile(gains, (1, 2)), cot, grad_second, middle, mixed, whole_o.reshape(2, width, half),
-        (qn, kn, v, q_raw, k_raw), inverse, grads_u, grads_d, state_u, state_d, result, zs
+        norms, jnp.tile(qk_gains.astype(F32), (1, 2)), cot, grad_second, middle, mixed, whole_o.reshape(2, width, half),
+        (qn, kn, v, q_raw, k_raw), inverse, grads_u, grads_d, states, result, outputs, zs
     )
     grad_q, small, grad_tokens = closing(norms, sums_second, sums_qk, image, first, grad_middle, gq, gk, gv, qkv, zs)
     grad_q = grad_q.reshape(2, rows, 3, PART_GROUP).transpose(1, 2, 0, 3).reshape(w_qkv.shape)

time: 459 us -> 393 us (0.86); the launches traced: 459 us -> 386 us
  Pallas kernels: 439 us -> 368 us
    pallas_call x2 -> x1, Pallas kernels: 169 us -> 115 us  [attention(): pl.pallas_call(functools.partial(attention_body, zs, pairs), grid=(row0 +...]
    pallas_call x1, Pallas kernels: 89.9 us -> 65.7 us  [closing(): pl.pallas_call(functools.partial(closing_body, zs), in_specs=[WHOLE_VMEM]...]
    pallas_call x1, Pallas kernels: 79.8 us -> 93.9 us  [feed(): pl.pallas_call(functools.partial(feed_body, zs), grid=(8,), in_specs=[ful...]
    pallas_call x1, Pallas kernels: 101 us -> 94.3 us  [backward(): pl.pallas_call(functools.partial(backward_body, zs, row_steps), grid=(row...]
where the time goes in v4:
time: 393 us; the launch traced here: 386 us
  Pallas kernels  368 us (94%)
  local copies, waits for them, and re-layouts  9.82 us (2%)
  other arithmetic  6.08 us (2%)
    pallas_call x1, Pallas kernels, attention(): pl.pallas_call(functools.partial(attention_body, zs, pairs), grid=(row0 +...  115 us
    pallas_call x1, Pallas kernels, backward(): pl.pallas_call(functools.partial(backward_body, zs, row_steps), grid=(row...  94.3 us
    pallas_call x1, Pallas kernels, feed(): pl.pallas_call(functools.partial(feed_body, zs), grid=(8,), in_specs=[ful...  93.9 us
    pallas_call x1, Pallas kernels, closing(): pl.pallas_call(functools.partial(closing_body, zs), in_specs=[WHOLE_VMEM]...  65.7 us

profile of v4, /device:TPU:0, one launch (start us, length us, event | category | flops | bytes accessed | tf_op | source)
XLA Modules:
  0.0 385.6 jit_solution(11583461440831685263)
XLA Ops:
  0.6 0.9 copy.32
  1.6 0.8 copy.29
  2.3 0.8 copy.30
  3.1 0.8 concatenate.3.q_in
  3.9 114.6 %attention.1 = (bf16[1024,1024]{1,0:T(8,128)(2,1)}, bf16[1024,1024]{1,0:T(8,128)(2,1)}, bf16[1024,1024]{1,0:T(8,128)(2,1)}, bf16[1024,1024]{1,0:T(8,128)(2,1)}, ...) custom-call(bf16[2,64]{1,0:T(2,128)(2,1)} %qk_gains.1, ...), custom_call_target="tpu_custom_call" | custom-call | tf_op jit(solution)/shard_map/attention/pallas_call | solution.py:915
  118.5 0.0 copy-start.5
  118.5 93.9 %feed.1 = (bf16[1024,1024]{1,0:T(8,128)(2,1)}, f32[1024,1024]{1,0:T(8,128)}, bf16[2,2,4,2,2,64,512]{6,5,4,3,2,1,0:T(8,128)(2,1)}, bf16[2,2,4,2,2,64,512]{6,5,4,3...) custom-call(bf16[1024,1024]{1,0:T(8,128)(2,1)} %get-tuple-element.50, ...), custom_call_target="tpu_custom_call", output_to_operand_aliasing={{9}: (3, {}), {10}: (4, {})} | custom-call | tf_op jit(solution)/shard_map/feed/pallas_call | solution.py:1041
  212.4 0.0 copy-done.5
  212.4 0.6 tile.10.gains
  213.1 94.3 %backward.1 = (f32[1024,1024]{1,0:T(8,128)}, bf16[1024,1024]{1,0:T(8,128)(2,1)}, bf16[1024,1024]{1,0:T(8,128)(2,1)}, bf16[1024,1024]{1,0:T(8,128)(2,1)}, f32[2,1...) custom-call(f32[8,1024]{1,0:T(8,128)} %get-tuple-element.48.norms, ...), custom_call_target="tpu_custom_call", output_to_operand_aliasing={{9}: (21, {})} | custom-call | tf_op jit(solution)/shard_map/backward/pallas_call | solution.py:1207
  307.4 65.7 %closing.1 = (f32[2,64,768]{2,1,0:T(8,128)}, f32[8,1024]{1,0:T(8,128)}, bf16[2,512,1024]{2,1,0:T(8,128)(2,1)}) custom-call(f32[8,1024]{1,0:T(8,128)} %get-tuple-element.48.norms, f32[2,1024]{1,0:T(2,128)} %get-tuple-element.72.sums_second, f32[2,128]{1,0:T(2,128)} %get-tuple-element.73.sums_qk, bf16[1024,1024]{1,0:T(8,128)(2,1)} %get-tuple-element.74.image_in, ...), custom_call_target="tpu_custom_call" | custom-call | tf_op jit(solution)/shard_map/closing/pallas_call | solution.py:1315
  373.1 0.8 constant_dynamic-slice_fusion
  373.9 0.6 pad_maximum_fusion
  374.4 0.0 copy-start.3
  374.5 4.1 %convert_element_type.7 = f32[2,512,1024]{2,1,0:T(8,128)} convert(bf16[2,512,1024]{2,1,0:T(8,128)(2,1)} %get-tuple-element.81) | non-fusion elementwise | flops 1048576 | bytes 6291456 | tf_op jit(solution)/shard_map/convert_element_type | solution.py:1351
  378.6 0.0 copy-start
  378.6 0.0 copy-done.3
  378.6 0.2 reshape.40
  378.8 0.3 copy.31
  379.1 1.1 reshape.41
  380.2 1.4 slice_add_fusion
  381.6 0.0 copy-done
  381.6 0.0 copy-start.4
  381.6 0.0 copy-start.2
  381.6 0.0 copy-start.1
  381.6 1.3 copy.40
  382.9 0.0 copy-done.4
  382.9 0.7 copy.41
  383.5 0.0 copy-done.2
  383.5 0.8 copy.42
  384.3 0.0 copy-done.1
  384.3 0.8 copy.43
  (3 shorter events, 0.0 us)
Async XLA Ops:
  118.5 93.9 %copy-start.5 = (bf16[2,64]{1,0:T(2,128)(2,1)S(1)}, bf16[2,64]{1,0:T(2,128)(2,1)}, u32[]{:S(2)}) copy-start(bf16[2,64]{1,0:T(2,128)(2,1)} %qk_gains.1) | copy-start | bytes 772
  374.4 4.1 %copy-start.3 = (f32[2,64,768]{2,1,0:T(8,128)S(1)}, f32[2,64,768]{2,1,0:T(8,128)}, u32[]{:S(2)}) copy-start(f32[2,64,768]{2,1,0:T(8,128)} %get-tuple-element.82) | copy-start | bytes 1179652
  378.6 3.0 copy-start
  381.6 1.3 copy-start.4
  381.6 2.0 copy-start.2
  381.6 2.8 copy-start.1

commit v5 on v4

--- a/solution.py
+++ b/solution.py
@@ -424,7 +424,7 @@
     def stage(self, i):
         d = self.order[i]
         held = self.at({e: ALL for e in self.order[:i]})
-        src = self.shard if i == 0 else held
+        src = self.shard if i == 0 and self.shard is not None else held
         return self.copies(0, i, [(src, held, self.p.dev(**{d: to})) for to in self.others(d)])
 
     def core_parts(self, i):
@@ -438,7 +438,7 @@
         return self.copies(self.p.zs + 1, i, [(ref, ref, peer) for ref in refs])
 
     def start(self, i):
-        if i == 0:
+        if i == 0 and self.shard is not None:
             self.own.start()
         if i < 3:
             start(*self.stage(i))
@@ -446,7 +446,7 @@
             start(*self.core_parts(i - 1))
 
     def done(self, i):
-        if i == 0:
+        if i == 0 and self.shard is not None:
             self.own.wait()
         if i < 3:
             wait(*self.stage(i))
@@ -552,24 +552,23 @@
             value = self.part(2, getattr(p, self.order[2]))[...].astype(F32)
             for k in range(len(self.others(self.order[2]))):
                 value = value + self.landings[3][k].astype(F32)
-            self.out[...] = value
+            for ref, lo, size in self.out:
+                ref[...] = value[:, lo:lo + size]
             return
         dims = [e for e in "xzy" if e not in self.order[:i]]
-        count = 1
-        for e in dims:
-            count *= self.size(e)
+        walked = [e for e in dims if e != "z"]
 
         def body(j, _):
-            at, left = {}, j
-            for e in reversed(dims):
-                at[e] = lax.rem(left, self.size(e))
-                left = lax.div(left, self.size(e))
+            at, left = {"z": ALL}, j
+            for e in reversed(walked):
+                at[e] = lax.rem(left, 2)
+                left = lax.div(left, 2)
             index = tuple(at[e] for e in dims)
             if i == 0:
                 into, froms = self.held(at["x"], at["z"], at["y"]), [self.landings[0].at[index]]
             else:
                 d = self.order[i - 1]
-                into = self.part(i - 1, getattr(p, d), at)
+                into = self.part(i - 1, getattr(p, d), {e: at[e] for e in dims})
                 froms = [self.landings[i].at[(k,) + index] for k in range(len(self.others(d)))]
             value = into[...]
             if len(froms) == 1:
@@ -581,10 +580,10 @@
                 value = value.astype(BF16)
             into[...] = value
             return 0
-        lax.fori_loop(0, count, body, 0)
-
-    def state(self):
-        return self.part(0, getattr(self.p, self.order[0]))
+        lax.fori_loop(0, 2 ** len(walked), body, 0)
+
+    def state(self, stages):
+        return self.part(stages - 2, getattr(self.p, self.order[stages - 2]))
 
 
 def scatter_sems(zs):
@@ -631,96 +630,102 @@
     return pltpu.CompilerParams(collective_id=collective_id, has_side_effects=True, vmem_limit_bytes=LIMIT)
 
 
-Q_ORDERS = ('zxy', 'xyz', 'zxy', 'yzx', 'zyx', 'yzx')
-O_ORDER = 'xzy'
-U_ORDERS = ('xzy', 'zxy', 'xzy', 'yzx')
-D_ORDERS = ('yzx', 'yzx', 'zyx', 'xyz')
-FEED_SINCE = (2, 1, 1)
-FEED_ORDERS = ('xyz', 'xzy', 'yxz', 'xyz')
-LATE_ORDERS = ('yxz', 'yxz', 'xzy', 'xyz')
+Q_ORDERS = ('zxy', 'zxy', 'xzy', 'zyx', 'xyz', 'xzy', 'zxy')
+O_ORDER = 'zxy'
+U_ORDERS = ('zxy', 'xzy', 'yzx', 'yzx')
+D_ORDERS = ('yzx', 'yxz', 'zxy', 'xyz')
+FEED_SINCE = (3, 1, 0)
+FEED_ORDERS = ('xzy', 'yzx', 'yxz', 'xyz')
+FEED_DONE = (3, 3)
+LATE_ORDERS = ('yxz', 'yzx', 'xzy', 'zxy')
 O_BACK_ORDER = 'yxz'
-CLOSING = ((0, 0, 384, 'yxz'), (0, 384, 384, 'xyz'), (1, 0, 384, 'yzx'), (1, 384, 384, 'zxy'))
-ATTENTION_LEAVES = (('U1', 2), ('D1', 2), ('U2', 1), ('D2', 1), ('U3', 1), ('D3', 1))
-OPENING_PLAN = (('T', -1), (0, -1), (1, -1), (2, -1), (3, -1), (5, -1), (1, 0), ('O', -1), (3, 0), (1, -2), (5, 0), ('D0', -1), (2, 0), (3, -2), (1, 1), ('D1', -1), ('O', 0), (2, -2), ('D0', 0), ('U3', -1), (0, 0), (1, -3), ('T', 0), ('T', -2), ('D1', 0), ('U3', 0), (2, 1), (0, -2), (2, -3), (3, 1), (4, -1), ('T', 1), ('T', -3), (2, 2), (2, -4), (0, 1), (0, -3), (3, -3), (2, 3), (4, 0), (4, -2), (5, -2), (1, 2), (1, -4), ('O', -2), ('T', 2), ('T', -4), (1, 3), (3, 2), (3, -4), ('U0', -1), (4, 1), (0, 2), (0, -4), (3, 3), (5, 1), ('D0', -2), ('U0', 0), (4, -3), (0, 3), ('T', 3), (5, -3),)
+CLOSING = ((0, 0, 256, 'zyx'), (0, 256, 256, 'yxz'), (0, 512, 256, 'xyz'), (1, 0, 256, 'yxz'), (1, 256, 256, 'zyx'), (1, 512, 256, 'yxz'))
+ATTENTION_LEAVES = (('U1', 3), ('D1', 3), ('U2', 1), ('D2', 1), ('U3', 0), ('D3', 0))
+OPENING_PLANS = (
+    ((6, -1), ('T', -1), (0, -1), (2, -1), ('D0', -1), ('D1', -1), (2, 0), (4, -1), (6, 0), (1, -1), ('D0', 0), ('U2', -1), ('D1', 0), (0, 0), (2, -2), (4, 0), (6, -2), (4, -2), ('U2', 0), ('T', 0), ('T', -2), (6, 1), (6, -3), (0, -2), (4, 1), (1, 0), (3, -1), (6, 2), (6, -4), (2, 1), (2, -3), (4, -3), (6, 3), (3, 0), (3, -2), ('O', -1), (0, 1), (1, -2),),
+    (('T', 1), ('T', -3), (1, 1), (5, -1), (3, 1), (0, -3), (5, 0), (3, -3), (2, 2), (1, -3), (2, -4), ('T', 2), ('T', -4), (2, 3), ('O', 0), (5, -2), (0, 2), (0, -4), (3, 2), (3, -4), ('O', -2), (4, 2), (4, -4), ('U0', -1), (1, 2), (1, -4), (0, 3), (3, 3), ('T', 3), ('U1', -1),),
+)
 ATTENTION_PLANS = (
-    (),
-    (),
-    (),
-    (),
-    (),
-    ((4, 2), (4, -4), ('C', -1),),
-    (('O', 1), ('O', -3), ('U0', -2), (5, 2), (5, -4), ('U2', -1),),
-    ((4, 3),),
-    ((5, 3), ('D0', 1), ('U1', -1), ('U2', 0), ('D0', -3),),
+    ((5, 1), (5, -3), ('D0', -2), (1, 3), (4, 3),),
+    (),
+    (),
+    (('U1', 0), ('C', -1),),
+    (('O', 1), ('O', -3), ('D1', -2),),
+    (('U0', 0), ('U1', -2), (5, 2), (5, -4),),
+    (),
+    ((5, 3), ('D1', 1), ('U0', -2),),
     (('C', 0), ('C', -2),),
     (),
-    (),
-    (('O', 2), ('O', -4),),
-    (),
-    (('U1', 0), ('D1', -2), ('O', 3), ('U0', 1), ('U0', -3), ('D2', -1),),
+    (('O', 2), ('O', -4), ('D0', 1), ('D1', -3),),
+    (),
+    (('U0', 1), ('U0', -3), ('D0', -3), ('O', 3),),
     (('C', 1), ('C', -3),),
-    (('D0', 2), ('D0', -4), ('U1', -2),),
-    (),
-    (('D0', 3),),
-    (('U0', 2), ('U0', -4), ('D2', 0), ('C', 2), ('C', -4),),
-    (),
-    (('U1', 1), ('D3', -1), ('U0', 3),),
-    (('D1', 1),),
-    (),
+    (('U1', 1), ('U1', -3), ('D2', -1),),
+    (),
+    (),
+    (),
+    (),
+    (('C', 2), ('C', -4),),
+    (('D2', 0), ('D0', 2), ('D0', -4), ('U0', 2), ('U0', -4),),
+    (),
+    (),
+    (('U1', 2), ('C', 3), ('D0', 3), ('U0', 3),),
 )
-ATTENTION_END = (('D3', 0), ('C', 3),)
+ATTENTION_END = (('D1', 2),)
 FEED_PLANS = (
-    (('U1', -3), ('D1', -3), ('U2', -2), ('D2', -2), ('U3', -2),),
-    (),
-    (),
-    (('D1', 2), ('D1', -4), ('D2', 1), ('D2', -3), ('D3', -2),),
-    (('u0', -1), ('d0', -1), ('U1', 2), ('U1', -4), ('D1', 3), ('D3', 1), ('U2', 1), ('U2', -3), ('D3', -3), ('U3', 1), ('U3', -3), ('U1', 3),),
-    (('u0', 0), ('d0', 0),),
-    (('D2', 2), ('D2', -4), ('u0', -2),),
-    (('U2', 2), ('U2', -4), ('D2', 3),),
-    (('u1', -1), ('d1', -1), ('U3', 2), ('d0', -2), ('U3', -4), ('U2', 3),),
-    (('D3', 2), ('D3', -4),),
-    (('U3', 3),),
-    (('u1', 0), ('u1', -2), ('d1', 0), ('D3', 3), ('u0', 1), ('d1', -2),),
-    (),
-    (('d0', 1),),
-    (),
-    (('u1', 1), ('d1', 1),),
+    (('U1', -4), ('D1', -4), ('U2', -2), ('D2', -2), ('U3', -1), ('D3', -1),),
+    (('U3', 0), ('U3', -2), ('U1', 3), ('D3', 0), ('D3', -2), ('D1', 3), ('D2', 1), ('D2', -3),),
+    (),
+    (('U2', 1), ('U2', -3), ('D3', 1), ('D3', -3),),
+    (('u0', -1), ('d0', -1),),
+    (('D2', 2), ('D2', -4),),
+    (('U3', 1), ('U3', -3),),
+    (('u0', 0), ('u0', -2), ('d0', 0), ('d0', -2), ('U2', 2), ('U2', -4), ('D2', 3),),
+    (('u1', -1), ('d1', -1), ('U2', 3),),
+    (),
+    (('D3', 2), ('D3', -4), ('u1', 0), ('u1', -2), ('d1', 0), ('d1', -2), ('U3', 2), ('U3', -4), ('d0', 1), ('d0', -3),),
+    (('D3', 3), ('U3', 3),),
+    (('u0', 1), ('u0', -3),),
+    (('u1', 1), ('u1', -3),),
+    (('d0', 2), ('d1', 1), ('d1', -3),),
+    (('u1', 2),),
 )
-FEED_END = ()
+FEED_END = (('u0', 2), ('d1', 2),)
 BACKWARD_PLANS = (
-    (('u0', -3), ('d0', -3), ('u1', -3), ('d1', -3), ('u2', -1), ('d2', -1), ('u3', -1), ('d3', -1), ('R', -1),),
-    (),
-    (),
-    (),
-    (),
-    (('u0', 2), ('u0', -4), ('d0', 2), ('d0', -4), ('u1', 2), ('u1', -4), ('d1', 2), ('d1', -4), ('R', 0), ('R', -2), ('u2', 0), ('o', -1), ('u2', -2), ('d2', 0), ('u3', 0), ('u3', -2), ('d3', 0),),
-    (('d0', 3), ('d2', -2),),
-    (('o', 0),),
-    (('R', 1), ('d3', -2),),
-    (),
-    (('u0', 3), ('u1', 3), ('d1', 3), ('u2', 1), ('o', -2),),
-    (('u3', 1), ('u2', -3), ('u3', -3),),
-    (('d2', 1),),
-    (('d3', 1), ('d2', -3), ('d3', -3),),
-    (('u2', 2), ('u2', -4), ('R', -3),),
-    (('o', 1), ('u3', 2), ('u3', -4),),
-    (('d3', 2), ('d3', -4), ('d2', 2), ('o', -3), ('d2', -4), ('u3', 3), ('u2', 3),),
+    (('u0', -4), ('d0', -4), ('u1', -4), ('d1', -4), ('u2', -1), ('d2', -1), ('u3', -1), ('d3', -1), ('R', -1),),
+    (('u0', 3), ('d0', 3),),
+    (),
+    (('R', 0), ('R', -2),),
+    (('u1', 3), ('d1', 3), ('u2', 0), ('o', -1), ('u2', -2), ('d2', 0), ('d2', -2), ('u3', 0), ('u3', -2), ('d3', 0), ('d3', -2),),
+    (('R', 1), ('R', -3), ('o', 0), ('o', -2),),
+    (),
+    (),
+    (),
     (('R', 2), ('R', -4),),
-    (),
-    (('o', 2), ('o', -4),),
+    (('u3', 1), ('u3', -3),),
+    (),
+    (('R', 3), ('d3', 1), ('d3', -3),),
+    (('u2', 1), ('u2', -3), ('d2', 1), ('d2', -3),),
+    (('d3', 2), ('d3', -4), ('o', 1), ('o', -3), ('u3', 2), ('u3', -4),),
+    (('d3', 3),),
+    (('u2', 2), ('u2', -4), ('u3', 3),),
+    (('o', 2), ('o', -4), ('d2', 2), ('d2', -4),),
+    (('d2', 3),),
+    (('u2', 3),),
 )
-BACKWARD_END = (('d3', 3), ('d2', 3), ('R', 3), ('o', 3),)
+BACKWARD_END = (('o', 3),)
 CLOSING_PLANS = (
-    ((0, -1), (1, -1),),
-    ((2, -1), (3, -1),),
-    ((0, 0), (0, -2), (1, 0), (1, -2),),
-    ((2, 0), (2, -2), (3, 0), (3, -2),),
+    ((0, -1), (1, -1), (2, -1),),
+    (),
+    (('G', -1),),
+    ((3, -1), (0, 0), (0, -2), (4, -1), (1, 0), (1, -2), (5, -1), (2, 0), (2, -2),),
+    (('G', 0), ('G', -2),),
 )
-CLOSING_END = (('S', -1), ('G', -1), (1, 1), ('S', 0), ('S', -2), (0, 1), (1, -3), ('S', 1), (0, -3), ('G', 0), ('G', -2), (2, 1), ('S', -3), (2, -3), (1, 2), (0, 2), (3, 1), (0, -4), (3, -3), ('S', 2), ('G', 1), ('G', -3), (3, 2), (3, -4), (3, 3), (0, 3), ('S', -4), ('G', 2), ('G', -4), (2, 2), (1, -4), (2, -4), (2, 3), ('S', 3), (1, 3), ('G', 3),)
+CLOSING_END = (('S', -1), (3, 0), (3, -2), (4, 0), (4, -2), (5, 0), (1, 1), (5, -2), ('S', 0), (2, 1), ('S', -2), ('S', 1), (1, -3), ('G', 1), ('G', -3), (0, 1), (3, 1), ('S', -3), (5, 1), (0, -3), (1, 2), (1, -4), (3, -3), ('S', 2), ('S', -4), (2, -3), (0, 2), (4, 1), (4, -3), ('G', 2), (0, -4), (3, 2), (3, -4), (5, -3), (2, 2), (1, 3), (2, -4), (0, 3), ('G', -4), (4, 2), ('S', 3), (5, 2), (4, -4), (5, -4), (3, 3), (2, 3), (4, 3), (5, 3), ('G', 3),)
 
 
 Q_TILE = 256
+ATTEND_TILE = 512
 ROWS = 256
 FF_GROUP = 512
 
@@ -777,20 +782,24 @@
 def attend_step(query_all, keys, values, mixed_s, cols, mixed, inverse):
     length = keys.shape[0]
     lane = lax.broadcasted_iota(jnp.int32, (1, PAIR), 1) < HD
-    values = jnp.concatenate([values, jnp.ones((length, PAIR), BF16)], axis=1)
     zero = jnp.zeros((), BF16)
-    for i in range(length // Q_TILE):
-        at = slice(i * Q_TILE, (i + 1) * Q_TILE)
+    values_t = values.astype(F32).T.astype(BF16)
+    ones = jnp.ones((16, length), BF16)
+    heads = [(jnp.where(mask, keys, zero), jnp.concatenate([values_t[h * HD:(h + 1) * HD], ones], axis=0))
+             for h, mask in ((0, lane), (1, ~lane))]
+    for i in range(length // ATTEND_TILE):
+        at = slice(i * ATTEND_TILE, (i + 1) * ATTEND_TILE)
         query = query_all[at]
-        got = []
-        for mask in (lane, ~lane):
-            scores = nt(jnp.where(mask, query, zero), keys)
-            got.append(nn(jnp.exp(scores).astype(BF16), values))
-        inv = 1.0 / jnp.where(lane, got[0][:, PAIR:], got[1][:, PAIR:])
-        value = (jnp.where(lane, got[0][:, :PAIR], got[1][:, :PAIR]) * inv).astype(BF16)
+        got, inv = [], []
+        for keys_h, values_h in heads:
+            both = nn(values_h, jnp.exp(nt(keys_h, query)).astype(BF16))
+            one_over = 1.0 / both[HD:HD + 1]
+            got.append(both[:HD] * one_over)
+            inv.append(jnp.broadcast_to(one_over, (HD, ATTEND_TILE)))
+        value = jnp.concatenate(got, axis=0).T.astype(BF16)
         mixed[at] = value
         mixed_s[at, cols] = value
-        inverse[at] = inv
+        inverse[at] = jnp.concatenate(inv, axis=0).T
 
 
 PROJECT_STEPS = 12
@@ -801,14 +810,14 @@
 
 
 def attention_body(
-    zs, pairs, qk_gains, q_in, o_in, u_in, d_in, tokens, cot_in,
+    zs, pairs, qk_gains, norm_gains, norm_shifts, q_in, o_in, u_in, d_in, tokens, cot_in,
     first, qn, kn, v, q_raw, k_raw, mixed, inverse, middle, second, norms, image, cot, whole_q, whole_o, whole_u, whole_d,
-    image_v, qn_s, kn_s, v_s, mixed_s, out_w, tiles, q_v, o_v, u_v, d_v, cot_v, side_v, local_sem, send, recv, swap_sem,
+    image_v, qn_s, kn_s, v_s, mixed_s, out_w, tiles, q_v, o_v, u_v, d_v, cot_v, side_v, turn, local_sem, send, recv, swap_sem,
 ):
     step = pl.program_id(0)
     p = Place(zs)
     length = image_v.shape[0]
-    half = whole_o.shape[5]
+    half, rows = whole_o.shape[5], whole_o.shape[4]
     tile = half // 2
     head0, row0 = PROJECT_STEPS, PROJECT_STEPS + pairs
     n = FF_GROUP
@@ -818,7 +827,8 @@
         "C": Swap(p, cot_in.at[1 - p.x], half_rows(cot, p.x, length // 2), swap_sem.at[1]),
     }
     local = lambda i, src, dst: pltpu.make_async_copy(src, dst, local_sem.at[i])
-    own_shards = [local(i, a, b) for i, (a, b) in enumerate(((q_in, q_v), (o_in, o_v), (u_in, u_v), (d_in, d_v)))]
+    own_shards = [local(i, a, b) for i, (a, b) in enumerate(((o_in, o_v), (u_in, u_v), (d_in, d_v)))]
+    own_shards += [local(i, q_in.at[k], q_v.at[:, pl.ds(k * half, half)]) for i, k in ((3, 0), (12, 1), (13, 2))]
     own_tokens = local(4, tokens.at[p.x], image_v.at[mine])
     own_cot = [local(5, cot_in.at[p.x], cot_v), local(6, cot_v, cot.at[mine])]
     keep_image = local(7, image_v, image)
@@ -826,7 +836,8 @@
     load_out = local(9, whole_o, out_w)
     starts = (2 * half + tile, 2 * half, half, half + tile, 0, tile)
     for i, lo in enumerate(starts):
-        chains[i] = Gather(p, q_v, whole_q, lo, tile + PAIR if i == 0 else tile, Q_ORDERS[i], send.at[i], recv.at[i])
+        chains[i] = Gather(p, q_v, whole_q, lo, tile, Q_ORDERS[i], send.at[i], recv.at[i])
+    chains[6] = Gather(p, q_v, whole_q, 3 * half, PAIR, Q_ORDERS[6], send.at[15], recv.at[15])
 
     def load_tile(i):
         return local(10 + i % 2, whole_q.at[:, :, :, :, :, pl.ds(starts[i], tile)], tiles.at[i % 2])
@@ -839,24 +850,36 @@
     @pl.when(step == 0)
     def _():
         start(*own_shards, own_tokens, own_cot[0])
+        turn[...] = jnp.zeros_like(turn)
+        turn[0:2, 0:rows] = norm_gains[...].astype(F32)
+        turn[2:4, 0:rows] = norm_shifts[...].astype(F32)
+        q_v[:, 3 * half:] = turn[...].T[:rows].astype(BF16)
         meet(p)
         wait(*own_shards)
-        follow(chains, OPENING_PLAN)
-        load_tile(0).start()
+        for name, stages in ATTENTION_LEAVES:
+            if stages == 0:
+                chains[name].own.start()
+
+        def norm(which):
+            def rows_norm(i, _):
+                at = pl.ds(pl.multiple_of(which * (length // 2) + i * ROWS, ROWS), ROWS)
+                hat, _f = stats(image_v[at].astype(F32))
+                first[at] = (hat * norms[0:1] + norms[2:3]).astype(BF16)
+                return 0
+            lax.fori_loop(0, length // 2 // ROWS, rows_norm, 0)
+
+        follow(chains, OPENING_PLANS[0])
         side.start()
         own_cot[0].wait()
         own_cot[1].start()
         side.wait()
         norms[...] = side_v[...].reshape(-1, PAIR).astype(F32).T[:8]
         own_tokens.wait()
+        norm(p.x)
+        follow(chains, OPENING_PLANS[1])
+        load_tile(0).start()
         keep_image.start()
-
-        def norm(i, _):
-            at = pl.ds(pl.multiple_of(i * ROWS, ROWS), ROWS)
-            hat, _f = stats(image_v[at].astype(F32))
-            first[at] = (hat * norms[0:1] + norms[2:3]).astype(BF16)
-            return 0
-        lax.fori_loop(0, length // ROWS, norm, 0)
+        norm(1 - p.x)
 
     at_steps(step, chains, ATTENTION_PLANS)
 
@@ -893,11 +916,13 @@
         follow(chains, ATTENTION_END)
         for name, stages in ATTENTION_LEAVES:
             chains[name].rest(0, stages - 1)
+            if stages == 0:
+                chains[name].own.wait()
         wait(own_cot[1], keep_image)
 
 
-def attention(qk_gains, q, o, u, d, tokens, cot, zs):
-    rows = q.shape[0]
+def attention(qk_gains, norm_gains, norm_shifts, q, o, u, d, tokens, cot, zs):
+    rows = o.shape[0]
     length, width = 2 * tokens.shape[1], tokens.shape[2]
     half = o.shape[1]
     pairs = 2 * half // PAIR
@@ -909,24 +934,24 @@
     bf = jax.ShapeDtypeStruct((length, 2 * half), BF16)
     square = jax.ShapeDtypeStruct((length, width), BF16)
     f32 = lambda *shape: jax.ShapeDtypeStruct(shape, F32)
-    whole = lambda s: jax.ShapeDtypeStruct((2, zs, 2, 2) + s.shape, BF16)
+    whole = lambda n: jax.ShapeDtypeStruct((2, zs, 2, 2, rows, n), BF16)
     store = pltpu.VMEM((length, 2 * half), BF16)
-    same = lambda s: pltpu.VMEM(s.shape, BF16)
+    wide = lambda n: pltpu.VMEM((rows, n), BF16)
     return pl.pallas_call(
         functools.partial(attention_body, zs, pairs),
         grid=(row0 + length // ROWS,),
-        in_specs=[full(qk_gains.shape)] + [HBM] * 6,
+        in_specs=[full(qk_gains.shape), full(norm_gains.shape), full(norm_shifts.shape)] + [HBM] * 6,
         out_specs=[full((length, width)), tiles(2), tiles(1), tiles(0), tiles(2), tiles(1), heads, heads, by_rows, by_rows,
                    full((8, width))] + [HBM] * 6,
         out_shape=[square, bf, bf, bf, bf, bf, bf, f32(length, 2 * half), f32(length, width), square, f32(8, width),
-                   square, square, whole(q), whole(o), whole(u), whole(d)],
+                   square, square, whole(3 * half + PAIR), whole(half), whole(u.shape[1]), whole(d.shape[1])],
         scratch_shapes=[pltpu.VMEM((length, width), BF16), store, store, store, store, pltpu.VMEM((2, zs, 2, 2, rows, half), BF16),
-                        pltpu.VMEM((2, 2, zs, 2, 2, rows, tile), BF16), same(q), same(o), same(u), same(d),
+                        pltpu.VMEM((2, 2, zs, 2, 2, rows, tile), BF16), wide(3 * half + PAIR), wide(half), wide(u.shape[1]), wide(d.shape[1]),
                         pltpu.VMEM((length // 2, width), BF16), pltpu.VMEM((zs, 2, 2, rows, PAIR), BF16),
-                        DMA((12,)), DMA((15, gather_sems(zs))), DMA((15, gather_sems(zs))), DMA((2, 2, CHUNKS))],
+                        pltpu.VMEM((PAIR, PAIR), F32), DMA((14,)), DMA((16, gather_sems(zs))), DMA((16, gather_sems(zs))), DMA((2, 2, CHUNKS))],
         compiler_params=params(0),
         name="attention",
-    )(qk_gains, q, o, u, d, tokens, cot)
+    )(qk_gains, norm_gains, norm_shifts, q, o, u, d, tokens, cot)
 
 
 def gelu_parts(v):
@@ -957,9 +982,9 @@
         for k in range(2):
             i = 2 * j + k
             held = lambda x, z, y, j=j, k=k: g.at[k, j, x, z, y, p.c]
-            s = Scatter(p, FEED_ORDERS[i], held, g.at[k, j, :, :, :, 1 - p.c], [next(at), next(at)], send.at[6 + i], recv.at[6 + i])
+            s = Scatter(p, FEED_ORDERS[i], held, g.at[k, j, :, :, :, 1 - p.c], [next(at) for _ in range(FEED_DONE[j])], send.at[6 + i], recv.at[6 + i])
             chains[f"{'ud'[k]}{j}"] = s
-            states.append(pltpu.make_async_copy(s.state(), state_refs[i], misc_sem.at[1 + i]))
+            states.append(pltpu.make_async_copy(s.state(FEED_DONE[j]), state_refs[i], misc_sem.at[1 + i]))
     init = pltpu.make_async_copy(middle, acc, misc_sem.at[0])
     mine = pl.ds(pl.multiple_of(p.x * (length // 2), length // 2), length // 2)
     own = pltpu.make_async_copy(result.at[mine], outputs.at[p.x], misc_sem.at[9])
@@ -1037,14 +1062,14 @@
     scratch = [pltpu.VMEM((length, width), F32), square, square, strip, strip, pltpu.VMEM((2, 2) + tile[1:], BF16),
                pltpu.VMEM((2, 4) + tile, BF16), DMA((2, 2)), DMA((10,)), DMA((10, gather_sems(zs))), DMA((10, gather_sems(zs)))]
     for i in range(4):
-        scratch += landing(zs, rows, n, FEED_ORDERS[i])[:2]
+        scratch += landing(zs, rows, n, FEED_ORDERS[i])[:FEED_DONE[i // 2]]
     return pl.pallas_call(
         functools.partial(feed_body, zs),
         grid=(8,),
         in_specs=[full(second.shape), full(cot.shape), HBM, HBM, HBM],
         out_specs=[full(second.shape), full(second.shape)] + [HBM] * 9,
         out_shape=[same(second), jax.ShapeDtypeStruct((length, width), F32), grads, grads]
-        + [jax.ShapeDtypeStruct(rest_shape(zs, rows, n, o[0]), BF16) for o in FEED_ORDERS]
+        + [jax.ShapeDtypeStruct(rest_shape(zs, rows, n, o[:FEED_DONE[i // 2] - 1]), BF16) for i, o in enumerate(FEED_ORDERS)]
         + [jax.ShapeDtypeStruct((2, length // 2, width), BF16), same(whole_u), same(whole_d)],
         scratch_shapes=scratch,
         input_output_aliases={3: 9, 4: 10},
@@ -1060,7 +1085,10 @@
     zero = jnp.zeros((), BF16)
     go = go.astype(F32)
     product = go * mixed.astype(F32) * inv
-    go_inv = (go * inv).astype(BF16)
+    go_inv = go * inv
+    go_t = go_inv.T.astype(BF16)
+    go_inv = go_inv.astype(BF16)
+    query_t = query.astype(F32).T.astype(BF16)
     heads = []
     for h, mask in ((0, first), (1, ~first)):
         delta = -jnp.sum(jnp.where(mask, product, 0.0), -1, keepdims=True)
@@ -1069,23 +1097,26 @@
         spare = (1 - h) * HD
         grad_aug = jnp.where(mask, go_inv, jnp.where(lanes == spare, high, jnp.where(lanes == spare + 1, low, zero)))
         values_aug = jnp.where(mask, values, jnp.where((lanes == spare) | (lanes == spare + 1), jnp.ones((), BF16), zero))
-        heads.append((jnp.where(mask, query, zero), jnp.where(mask, keys, zero), jnp.where(mask, go_inv, zero), grad_aug, values_aug))
+        mine = slice(h * HD, (h + 1) * HD)
+        heads.append((jnp.where(mask, keys, zero), grad_aug, values_aug, go_t[mine], query_t[mine]))
     dq = []
-    dk = jnp.zeros((length, PAIR), F32)
-    dv = jnp.zeros((length, PAIR), F32)
+    dk = [jnp.zeros((HD, length), F32)] * 2
+    dv = [jnp.zeros((HD, length), F32)] * 2
     for i in range(length // Q_TILE):
         if 2 * i == length // Q_TILE:
             between()
         at = slice(i * Q_TILE, (i + 1) * Q_TILE)
-        part = jnp.zeros((Q_TILE, PAIR), F32)
-        for qm, km, gm, ga, va in heads:
-            exponent = jnp.exp(nt(km, qm[at]))
-            grad_scores = (exponent * nt(va, ga[at])).astype(BF16)
-            dv = dv + nn(exponent.astype(BF16), gm[at])
-            dk = dk + nn(grad_scores, qm[at])
-            part = part + lax.dot_general(grad_scores, km, (((0,), (0,)), ((), ())), preferred_element_type=F32)
-        dq.append(part)
+        parts = []
+        for h, (km, ga, va, gt, qt) in enumerate(heads):
+            exponent = jnp.exp(nt(query[at], km))
+            grad_scores = (exponent * nt(ga[at], va)).astype(BF16)
+            dv[h] = dv[h] + nn(gt[:, at], exponent.astype(BF16))
+            dk[h] = dk[h] + nn(qt[:, at], grad_scores)
+            parts.append(nn(grad_scores, km))
+        dq.append(parts[0] + parts[1])
     dq = jnp.concatenate(dq, axis=0)
+    dk = jnp.concatenate(dk, axis=0).T
+    dv = jnp.concatenate(dv, axis=0).T
     grad_v[...] = dv.astype(BF16)
     matrix = head_mean_matrix(PAIR)
     hat, factor = head_stats(q_raw.astype(F32), matrix)
@@ -1113,16 +1144,17 @@
     chains, loads = {}, []
 
     def out(k, j):
-        return (shard_u, shard_d)[k].at[:, pl.ds(j * n, n)]
+        return [((shard_u, shard_d)[k].at[:, pl.ds(j * n, n)], 0, n)]
 
     for i, state in enumerate((state_0, state_1, state_2, state_3)):
         j, k = divmod(i, 2)
         order = FEED_ORDERS[i]
         own = next(at)
 
-        def held(x, z, y, own=own, order=order):
-            return own.at[tuple(index for e, index in zip("xzy", (x, z, y)) if e != order[0])]
-        chains[f"{'ud'[k]}{j}"] = Scatter(p, order, held, None, [None, None] + take(2), send.at[i], recv.at[i], out(k, j))
+        def held(x, z, y, own=own, gone=order[:FEED_DONE[j] - 1]):
+            return own.at[tuple(index for e, index in zip("xzy", (x, z, y)) if e not in gone)]
+        skip = FEED_DONE[j]
+        chains[f"{'ud'[k]}{j}"] = Scatter(p, order, held, None, [None] * skip + take(4 - skip), send.at[i], recv.at[i], out(k, j))
         loads.append(pltpu.make_async_copy(state, own, load_sem.at[i]))
     for i in range(4):
         j, k = divmod(i, 2)
@@ -1132,7 +1164,7 @@
             send.at[4 + i], recv.at[4 + i], out(k, 2 + j))
         loads.append(pltpu.make_async_copy(grad.at[:, :, :, p.c], own_late.at[i], load_sem.at[4 + i]))
     chains["o"] = Scatter(p, O_BACK_ORDER, lambda x, z, y: g_o.at[x, z, y, p.c], g_o.at[:, :, :, 1 - p.c], take(4),
-                          send.at[8], recv.at[8], shard_o)
+                          send.at[8], recv.at[8], [(shard_o, 0, half)])
     half_length = result.shape[0] // 2
     chains["R"] = Swap(p, half_rows(result, 1 - p.x, half_length), outputs.at[p.x], swap_sem)
 
@@ -1200,7 +1232,8 @@
         DMA((9, scatter_sems(zs))), DMA((9, scatter_sems(zs))),
     ]
     for i in range(4):
-        scratch += [pltpu.VMEM(rest_shape(zs, rows, n, FEED_ORDERS[i][0]), BF16)] + landing(zs, rows, n, FEED_ORDERS[i], 2)
+        skip = FEED_DONE[i // 2]
+        scratch += [pltpu.VMEM(rest_shape(zs, rows, n, FEED_ORDERS[i][:skip - 1]), BF16)] + landing(zs, rows, n, FEED_ORDERS[i], skip)
     for i in range(4):
         scratch += landing(zs, rows, n, LATE_ORDERS[i])
     scratch += landing(zs, rows, half, O_BACK_ORDER)
@@ -1220,6 +1253,15 @@
 
 
 PART_GROUP = 256
+
+
+def pieces(lo, size):
+    out = []
+    for part in range(3):
+        first, last = max(lo, part * PART_GROUP), min(lo + size, (part + 1) * PART_GROUP)
+        if first < last:
+            out.append((part, first - lo, last - first))
+    return out
 
 
 def closing_body(
@@ -1243,7 +1285,8 @@
         cols = pl.ds(lo, m)
         held = lambda x, z, y, k=k, cols=cols: g.at[k, x, z, y, p.c, :, cols]
         chains[i] = Scatter(p, order, held, g.at[k, :, :, :, 1 - p.c, :, cols], [next(at) for _ in range(4)], send.at[i], recv.at[i],
-                            shard_q.at[k, :, cols])
+                            [(shard_q.at[part, :, pl.ds(k * PART_GROUP + max(lo - part * PART_GROUP, 0), n)], at0, n)
+                             for part, at0, n in pieces(lo, m)])
     half_length = length // 2
     chains["G"] = Swap(p, half_rows(grad_image, 1 - p.x, half_length), grad_tokens.at[p.x], swap_sem)
     chains["S"] = Sum(p, total, got, sum_send, sum_recv)
@@ -1263,38 +1306,42 @@
             return 0
         lax.fori_loop(0, 6, one, 0)
 
+    def first_norm_back(which, carry, plan):
+        here = pl.ds(pl.multiple_of(which * half_length, half_length), half_length)
+        acc[...] = jnp.zeros_like(acc)
+
+        def to_first(i, _):
+            t, part = lax.div(i, 3), lax.rem(i, 3)
+            cols = pl.ds(pl.multiple_of(t * half, half), half)
+            acc[...] += nt(grads[part, here, cols], w[t, :, pl.ds(pl.multiple_of(part * half, half), half)])
+            return 0
+        lax.fori_loop(0, 6, to_first, 0)
+        follow(chains, plan)
+
+        def norm_back(i, carry):
+            at = pl.ds(pl.multiple_of(which * half_length + i * ROWS, ROWS), ROWS)
+            hat, factor = stats(image[at].astype(F32))
+            gf = acc[pl.ds(pl.multiple_of(i * ROWS, ROWS), ROWS)]
+            grad_image[at] = (grad_middle[at] + back(gf * norms[0:1], hat, factor)).astype(BF16)
+            return carry[0] + jnp.sum(gf * hat, 0, keepdims=True), carry[1] + jnp.sum(gf, 0, keepdims=True)
+        return lax.fori_loop(0, half_length // ROWS, norm_back, carry)
+
+    zero = jnp.zeros((1, width), F32)
     weight_grad(0)
     follow(chains, CLOSING_PLANS[0])
+    load_w.wait()
+    wait(load_image, load_middle)
+    sums = first_norm_back(1 - p.x, (zero, zero), CLOSING_PLANS[1])
+    follow(chains, CLOSING_PLANS[2])
     weight_grad(1)
-    follow(chains, CLOSING_PLANS[1])
-    load_w.wait()
-    acc[...] = jnp.zeros_like(acc)
-
-    def to_first(i, _):
-        t, part = lax.div(i, 3), lax.rem(i, 3)
-        cols = pl.ds(pl.multiple_of(t * half, half), half)
-        acc[...] += nt(grads[part, :, cols], w[t, :, pl.ds(pl.multiple_of(part * half, half), half)])
-        return 0
-    lax.fori_loop(0, 3, to_first, 0)
-    follow(chains, CLOSING_PLANS[2])
-    lax.fori_loop(3, 6, to_first, 0)
-    wait(load_image, load_middle)
     follow(chains, CLOSING_PLANS[3])
-
-    def norm_back(i, carry):
-        at = pl.ds(pl.multiple_of(i * ROWS, ROWS), ROWS)
-        hat, factor = stats(image[at].astype(F32))
-        gf = acc[at]
-        grad_image[at] = (grad_middle[at] + back(gf * norms[0:1], hat, factor)).astype(BF16)
-        return carry[0] + jnp.sum(gf * hat, 0, keepdims=True), carry[1] + jnp.sum(gf, 0, keepdims=True)
-    zero = jnp.zeros((1, width), F32)
-    sum_hat, sum_all = lax.fori_loop(0, length // ROWS, norm_back, (zero, zero))
+    sum_hat, sum_all = first_norm_back(p.x, sums, CLOSING_PLANS[4])
     own.start()
     total[...] = jnp.zeros_like(total)
     total[0:1] = sum_hat
     total[1:2] = sum_all
     total[2:4] = sums_second[...]
-    total[4:6, 0:PAIR] = sums_qk[...]
+    total[4:6, 0:HD] = sums_qk[:, :HD] + sums_qk[:, HD:]
     follow(chains, CLOSING_END)
     own.wait()
 
@@ -1306,7 +1353,7 @@
     square = pltpu.VMEM((length, width), BF16)
     scratch = [
         square, square, pltpu.VMEM((length, width), F32), pltpu.VMEM((3,) + gq.shape, BF16), pltpu.VMEM(w.shape, BF16), square,
-        pltpu.VMEM((length, width), F32), square, pltpu.VMEM((2, 2, zs, 2, 2, rows, wide), BF16), DMA((8,)), DMA((2, CHUNKS)),
+        pltpu.VMEM((length // 2, width), F32), square, pltpu.VMEM((2, 2, zs, 2, 2, rows, wide), BF16), DMA((8,)), DMA((2, CHUNKS)),
         pltpu.VMEM((zs + 2, 8, width), F32), DMA((zs + 2,)), DMA((zs + 2,)),
         DMA((len(CLOSING), scatter_sems(zs))), DMA((len(CLOSING), scatter_sems(zs))),
     ]
@@ -1316,7 +1363,7 @@
         functools.partial(closing_body, zs),
         in_specs=[WHOLE_VMEM] * 3 + [HBM] * 7,
         out_specs=[WHOLE_VMEM, WHOLE_VMEM, HBM],
-        out_shape=[jax.ShapeDtypeStruct((2, rows, wide), F32), jax.ShapeDtypeStruct((8, width), F32),
+        out_shape=[jax.ShapeDtypeStruct((3, rows, gq.shape[1] // 2), F32), jax.ShapeDtypeStruct((8, width), F32),
                    jax.ShapeDtypeStruct((2, length // 2, width), BF16)],
         scratch_shapes=scratch,
         compiler_params=params(3),
@@ -1330,10 +1377,8 @@
     width = tokens.shape[2]
     half = w_qkv.shape[2]
     cols = 3 * half
-    side = jnp.concatenate([norm_gains, norm_shifts, jnp.zeros((rows, 124), BF16)], axis=1)
-    shard_q = jnp.concatenate([w_qkv.reshape(rows, cols), side], axis=1)
     first, qn, kn, v, q_raw, k_raw, mixed, inverse, middle, second, norms, image, cot, whole_q, whole_o, whole_u, whole_d = attention(
-        qk_gains, shard_q, wo_t, w_up, w_down_t, tokens, cotangent, zs
+        qk_gains, norm_gains.T, norm_shifts.T, w_qkv.transpose(1, 0, 2), wo_t, w_up, w_down_t, tokens, cotangent, zs
     )
     result, grad_second, grads_u, grads_d, *states, outputs, whole_u, whole_d = feed(
         second, cot, middle, whole_u, whole_d, zs
@@ -1344,18 +1389,17 @@
         (qn, kn, v, q_raw, k_raw), inverse, grads_u, grads_d, states, result, outputs, zs
     )
     grad_q, small, grad_tokens = closing(norms, sums_second, sums_qk, image, first, grad_middle, gq, gk, gv, qkv, zs)
-    grad_q = grad_q.reshape(2, rows, 3, PART_GROUP).transpose(1, 2, 0, 3).reshape(w_qkv.shape)
     mine = lax.dynamic_slice_in_dim(small, lax.axis_index("fsdp") * rows, rows, 1)
     return (
         outputs,
         grad_tokens.astype(F32),
-        grad_q,
+        grad_q.transpose(1, 0, 2),
         shard_o,
         shard_u,
         shard_d,
         jnp.stack([mine[0], mine[2]], 1),
         jnp.stack([mine[1], mine[3]], 1),
-        small[4:6, :HD] + small[4:6, HD:2 * HD],
+        small[4:6, :HD],
     )
 
 

time: 393 us -> 371 us (0.944); the launches traced: 386 us -> 370 us
  Pallas kernels: 368 us -> 358 us
    pallas_call x1, Pallas kernels: 94.3 us -> 86.8 us  [backward(): pl.pallas_call(functools.partial(backward_body, zs, row_steps), grid=(row...]
    pallas_call x1, Pallas kernels: 115 us -> 119 us  [attention(): pl.pallas_call(functools.partial(attention_body, zs, pairs), grid=(row0 +...]
    pallas_call x1, Pallas kernels: 93.9 us -> 89.5 us  [feed(): pl.pallas_call(functools.partial(feed_body, zs), grid=(8,), in_specs=[ful...]
where the time goes in v5:
time: 371 us; the launch traced here: 370 us
  Pallas kernels  358 us (96%)
  local copies, waits for them, and re-layouts  6.99 us (2%)
  other arithmetic  4.79 us (1%)
    pallas_call x1, Pallas kernels, attention(): pl.pallas_call(functools.partial(attention_body, zs, pairs), grid=(row0 +...  119 us
    pallas_call x1, Pallas kernels, feed(): pl.pallas_call(functools.partial(feed_body, zs), grid=(8,), in_specs=[ful...  89.5 us
    pallas_call x1, Pallas kernels, backward(): pl.pallas_call(functools.partial(backward_body, zs, row_steps), grid=(row...  86.8 us
    pallas_call x1, Pallas kernels, closing(): pl.pallas_call(functools.partial(closing_body, zs), in_specs=[WHOLE_VMEM]...  62.3 us

profile of v5, /device:TPU:0, one launch (start us, length us, event | category | flops | bytes accessed | tf_op | source)
XLA Modules:
  0.0 370.3 jit_solution(11458167209891265570)
XLA Ops:
  0.6 119.3 %attention.1 = (bf16[1024,1024]{1,0:T(8,128)(2,1)}, bf16[1024,1024]{1,0:T(8,128)(2,1)}, bf16[1024,1024]{1,0:T(8,128)(2,1)}, bf16[1024,1024]{1,0:T(8,128)(2,1)}, ...) custom-call(bf16[2,64]{1,0:T(2,128)(2,1)} %qk_gains.1, ...), custom_call_target="tpu_custom_call" | custom-call | tf_op jit(solution)/shard_map/attention/pallas_call | solution.py:940
  119.9 0.0 copy-start.5
  119.9 89.5 %feed.1 = (bf16[1024,1024]{1,0:T(8,128)(2,1)}, f32[1024,1024]{1,0:T(8,128)}, bf16[2,2,4,2,2,64,512]{6,5,4,3,2,1,0:T(8,128)(2,1)}, bf16[2,2,4,2,2,64,512]{6,5,4,3...) custom-call(bf16[1024,1024]{1,0:T(8,128)(2,1)} %get-tuple-element.50, ...), custom_call_target="tpu_custom_call", output_to_operand_aliasing={{9}: (3, {}), {10}: (4, {})} | custom-call | tf_op jit(solution)/shard_map/feed/pallas_call | solution.py:1066
  209.4 0.0 copy-done.5
  209.4 0.6 tile.10.gains
  210.1 86.8 %backward.1 = (f32[1024,1024]{1,0:T(8,128)}, bf16[1024,1024]{1,0:T(8,128)(2,1)}, bf16[1024,1024]{1,0:T(8,128)(2,1)}, bf16[1024,1024]{1,0:T(8,128)(2,1)}, f32[2,1...) custom-call(f32[8,1024]{1,0:T(8,128)} %get-tuple-element.48.norms, ...), custom_call_target="tpu_custom_call", output_to_operand_aliasing={{9}: (21, {})} | custom-call | tf_op jit(solution)/shard_map/backward/pallas_call | solution.py:1240
  296.9 62.3 %closing.1 = (f32[3,64,512]{2,1,0:T(8,128)}, f32[8,1024]{1,0:T(8,128)}, bf16[2,512,1024]{2,1,0:T(8,128)(2,1)}) custom-call(f32[8,1024]{1,0:T(8,128)} %get-tuple-element.48.norms, f32[2,1024]{1,0:T(2,128)} %get-tuple-element.72.sums_second, f32[2,128]{1,0:T(2,128)} %get-tuple-element.73.sums_qk, bf16[1024,1024]{1,0:T(8,128)(2,1)} %get-tuple-element.74.image_in, ...), custom_call_target="tpu_custom_call" | custom-call | tf_op jit(solution)/shard_map/closing/pallas_call | solution.py:1362
  359.2 0.8 constant_dynamic-slice_fusion
  359.9 0.6 pad_maximum_fusion
  360.5 0.0 copy-start
  360.5 4.2 %convert_element_type.7 = f32[2,512,1024]{2,1,0:T(8,128)} convert(bf16[2,512,1024]{2,1,0:T(8,128)(2,1)} %get-tuple-element.81) | non-fusion elementwise | flops 1048576 | bytes 6291456 | tf_op jit(solution)/shard_map/convert_element_type | solution.py:1395
  364.7 1.2 slice.19
  366.0 0.0 copy-done
  366.0 0.0 copy-start.3
  366.0 0.0 copy-start.4
  366.0 0.0 copy-start.2
  366.0 1.3 copy.29
  367.3 0.0 copy-done.3
  367.3 0.0 copy-start.1
  367.3 0.7 copy.30
  368.1 0.0 copy-done.4
  368.1 0.7 copy.31
  368.7 0.0 copy-done.2
  368.7 0.8 copy.32
  369.5 0.0 copy-done.1
  369.5 0.8 copy.33
  (2 shorter events, 0.0 us)
Async XLA Ops:
  119.9 89.5 %copy-start.5 = (bf16[2,64]{1,0:T(2,128)(2,1)S(1)}, bf16[2,64]{1,0:T(2,128)(2,1)}, u32[]{:S(2)}) copy-start(bf16[2,64]{1,0:T(2,128)(2,1)} %qk_gains.1) | copy-start | bytes 772
  360.5 5.5 %copy-start = (bf16[2,512,1024]{2,1,0:T(8,128)(2,1)S(1)}, bf16[2,512,1024]{2,1,0:T(8,128)(2,1)}, u32[]{:S(2)}) copy-start(bf16[2,512,1024]{2,1,0:T(8,128)(2,1)} %get-tuple-element.102) | copy-start | bytes 6291460
  366.0 1.3 copy-start.3
  366.0 2.1 copy-start.4
  366.0 2.7 copy-start.2
  367.3 2.2 copy-start.1

commit v6 on v5

--- a/solution.py
+++ b/solution.py
@@ -630,90 +630,90 @@
     return pltpu.CompilerParams(collective_id=collective_id, has_side_effects=True, vmem_limit_bytes=LIMIT)
 
 
-Q_ORDERS = ('zxy', 'zxy', 'xzy', 'zyx', 'xyz', 'xzy', 'zxy')
+Q_ORDERS = ('zyx', 'xzy', 'zxy', 'xzy', 'zyx', 'zxy', 'xzy')
 O_ORDER = 'zxy'
-U_ORDERS = ('zxy', 'xzy', 'yzx', 'yzx')
-D_ORDERS = ('yzx', 'yxz', 'zxy', 'xyz')
+U_ORDERS = ('xyz', 'zyx', 'zxy', 'xzy')
+D_ORDERS = ('xzy', 'xzy', 'yzx', 'yzx')
 FEED_SINCE = (3, 1, 0)
-FEED_ORDERS = ('xzy', 'yzx', 'yxz', 'xyz')
-FEED_DONE = (3, 3)
-LATE_ORDERS = ('yxz', 'yzx', 'xzy', 'zxy')
-O_BACK_ORDER = 'yxz'
+FEED_ORDERS = ('zyx', 'xyz', 'yzx', 'xyz')
+FEED_DONE = (2, 2)
+LATE_ORDERS = ('xzy', 'xyz', 'yxz', 'yxz')
+O_BACK_ORDER = 'zxy'
 CLOSING = ((0, 0, 256, 'zyx'), (0, 256, 256, 'yxz'), (0, 512, 256, 'xyz'), (1, 0, 256, 'yxz'), (1, 256, 256, 'zyx'), (1, 512, 256, 'yxz'))
 ATTENTION_LEAVES = (('U1', 3), ('D1', 3), ('U2', 1), ('D2', 1), ('U3', 0), ('D3', 0))
 OPENING_PLANS = (
-    ((6, -1), ('T', -1), (0, -1), (2, -1), ('D0', -1), ('D1', -1), (2, 0), (4, -1), (6, 0), (1, -1), ('D0', 0), ('U2', -1), ('D1', 0), (0, 0), (2, -2), (4, 0), (6, -2), (4, -2), ('U2', 0), ('T', 0), ('T', -2), (6, 1), (6, -3), (0, -2), (4, 1), (1, 0), (3, -1), (6, 2), (6, -4), (2, 1), (2, -3), (4, -3), (6, 3), (3, 0), (3, -2), ('O', -1), (0, 1), (1, -2),),
-    (('T', 1), ('T', -3), (1, 1), (5, -1), (3, 1), (0, -3), (5, 0), (3, -3), (2, 2), (1, -3), (2, -4), ('T', 2), ('T', -4), (2, 3), ('O', 0), (5, -2), (0, 2), (0, -4), (3, 2), (3, -4), ('O', -2), (4, 2), (4, -4), ('U0', -1), (1, 2), (1, -4), (0, 3), (3, 3), ('T', 3), ('U1', -1),),
+    ((6, -1), ('T', -1), (0, -1), (2, -1), ('D2', -1), (6, 0), (1, -1), ('D2', 0), (1, 0), (3, -1), (0, 0), (6, -2), (0, -2), (2, 0), (1, -2), ('T', 0), ('T', -2), (3, 0), (2, -2), (0, 1), (6, 1), (6, -3), (3, -2), (2, 1), (0, -3), (2, -3), (1, 1), (4, -1), ('T', 1), ('T', -3), (6, 2), (6, -4), (1, -3), (6, 3),),
+    ((3, 1), (5, -1), (4, 0), ('O', -1), (2, 2), (2, -4), (3, -3), (0, 2), (0, -4), ('U0', -1), ('T', 2), ('T', -4), (2, 3), (1, 2), (1, -4), (4, -2), (0, 3), ('U0', 0), ('D0', -1), (5, 0), ('U1', -1), (1, 3), ('D0', 0), (5, -2), ('O', 0), ('D0', -2), (3, 2), (3, -4), ('U0', -2), (4, 1), ('T', 3), (4, -3),),
 )
 ATTENTION_PLANS = (
-    ((5, 1), (5, -3), ('D0', -2), (1, 3), (4, 3),),
-    (),
-    (),
-    (('U1', 0), ('C', -1),),
-    (('O', 1), ('O', -3), ('D1', -2),),
-    (('U0', 0), ('U1', -2), (5, 2), (5, -4),),
-    (),
-    ((5, 3), ('D1', 1), ('U0', -2),),
+    ((3, 3), (5, 1), (5, -3), ('O', -2),),
+    (('U0', 1),),
+    (('U1', 0), ('U0', -3), ('U1', -2),),
+    (),
+    (),
+    (),
+    ((4, 2), (4, -4), ('D1', -1), (5, 2), (5, -4),),
+    (('O', 1), ('O', -3), ('C', -1), ('U1', 1), (4, 3), ('D1', 0), ('U1', -3), (5, 3),),
+    (('D0', 1), ('D0', -3), ('D1', -2),),
+    (),
+    (),
+    (),
     (('C', 0), ('C', -2),),
     (),
-    (('O', 2), ('O', -4), ('D0', 1), ('D1', -3),),
-    (),
-    (('U0', 1), ('U0', -3), ('D0', -3), ('O', 3),),
-    (('C', 1), ('C', -3),),
-    (('U1', 1), ('U1', -3), ('D2', -1),),
-    (),
-    (),
-    (),
-    (),
-    (('C', 2), ('C', -4),),
-    (('D2', 0), ('D0', 2), ('D0', -4), ('U0', 2), ('U0', -4),),
-    (),
-    (),
-    (('U1', 2), ('C', 3), ('D0', 3), ('U0', 3),),
+    (),
+    (),
+    (('O', 2), ('O', -4), ('U1', 2),),
+    (('D0', 2), ('D0', -4), ('C', 1), ('C', -3),),
+    (('O', 3), ('D1', 1), ('D1', -3), ('U2', -1),),
+    (('D0', 3),),
+    (('U0', 2), ('U0', -4), ('C', 2), ('C', -4),),
+    (),
+    (('U2', 0),),
+    (('U0', 3),),
 )
-ATTENTION_END = (('D1', 2),)
+ATTENTION_END = (('C', 3), ('D1', 2),)
 FEED_PLANS = (
     (('U1', -4), ('D1', -4), ('U2', -2), ('D2', -2), ('U3', -1), ('D3', -1),),
-    (('U3', 0), ('U3', -2), ('U1', 3), ('D3', 0), ('D3', -2), ('D1', 3), ('D2', 1), ('D2', -3),),
-    (),
-    (('U2', 1), ('U2', -3), ('D3', 1), ('D3', -3),),
+    (('D3', 0), ('D3', -2), ('U3', 0), ('U1', 3), ('D1', 3), ('U2', 1), ('U2', -3),),
+    (),
+    (('D2', 1), ('D2', -3), ('U3', -2),),
     (('u0', -1), ('d0', -1),),
-    (('D2', 2), ('D2', -4),),
-    (('U3', 1), ('U3', -3),),
-    (('u0', 0), ('u0', -2), ('d0', 0), ('d0', -2), ('U2', 2), ('U2', -4), ('D2', 3),),
-    (('u1', -1), ('d1', -1), ('U2', 3),),
-    (),
-    (('D3', 2), ('D3', -4), ('u1', 0), ('u1', -2), ('d1', 0), ('d1', -2), ('U3', 2), ('U3', -4), ('d0', 1), ('d0', -3),),
-    (('D3', 3), ('U3', 3),),
-    (('u0', 1), ('u0', -3),),
-    (('u1', 1), ('u1', -3),),
-    (('d0', 2), ('d1', 1), ('d1', -3),),
+    (('U2', 2), ('U2', -4),),
+    (('D3', 1), ('D3', -3),),
+    (('u0', 0), ('u0', -2), ('d0', 0), ('D2', 2), ('D2', -4), ('d0', -2), ('U2', 3), ('U3', 1), ('U3', -3),),
+    (('u1', -1), ('d1', -1), ('D2', 3),),
+    (),
+    (('D3', 2), ('D3', -4), ('u1', 0), ('u1', -2), ('d1', 0), ('d1', -2),),
+    (('U3', 2), ('U3', -4), ('D3', 3),),
+    (('d0', 1), ('U3', 3),),
+    (('u0', 1), ('u1', 1),),
+    (('d1', 1),),
+    (),
+)
+FEED_END = ()
+BACKWARD_PLANS = (
+    (('u0', -3), ('d0', -3), ('u1', -3), ('u2', -1), ('d2', -1), ('u3', -1), ('d3', -1), ('R', -1),),
+    (),
+    (),
+    (('u0', 2), ('u0', -4), ('d1', -3), ('R', 0), ('R', -2), ('d0', 2), ('d0', -4),),
     (('u1', 2),),
+    (('u0', 3), ('u1', -4), ('u2', 0), ('o', -1), ('d2', 0), ('u3', 0), ('u3', -2), ('d3', 0), ('d1', 2), ('d1', -4), ('d3', -2), ('d0', 3), ('R', 1), ('u2', -2),),
+    (('u1', 3), ('d2', -2), ('o', 0), ('o', -2),),
+    (('d1', 3),),
+    (),
+    (),
+    (),
+    (('u2', 1), ('u2', -3), ('R', -3),),
+    (('u3', 1), ('d3', 1), ('d2', 1), ('d2', -3), ('u3', -3),),
+    (),
+    (('R', 2), ('d3', -3),),
+    (('d2', 2), ('d2', -4), ('o', 1), ('u3', 2), ('o', -3), ('u3', -4),),
+    (),
+    (('d3', 2), ('R', -4), ('u2', 2), ('u2', -4), ('d3', -4), ('o', 2), ('o', -4),),
+    (),
+    (('u2', 3), ('o', 3), ('R', 3),),
 )
-FEED_END = (('u0', 2), ('d1', 2),)
-BACKWARD_PLANS = (
-    (('u0', -4), ('d0', -4), ('u1', -4), ('d1', -4), ('u2', -1), ('d2', -1), ('u3', -1), ('d3', -1), ('R', -1),),
-    (('u0', 3), ('d0', 3),),
-    (),
-    (('R', 0), ('R', -2),),
-    (('u1', 3), ('d1', 3), ('u2', 0), ('o', -1), ('u2', -2), ('d2', 0), ('d2', -2), ('u3', 0), ('u3', -2), ('d3', 0), ('d3', -2),),
-    (('R', 1), ('R', -3), ('o', 0), ('o', -2),),
-    (),
-    (),
-    (),
-    (('R', 2), ('R', -4),),
-    (('u3', 1), ('u3', -3),),
-    (),
-    (('R', 3), ('d3', 1), ('d3', -3),),
-    (('u2', 1), ('u2', -3), ('d2', 1), ('d2', -3),),
-    (('d3', 2), ('d3', -4), ('o', 1), ('o', -3), ('u3', 2), ('u3', -4),),
-    (('d3', 3),),
-    (('u2', 2), ('u2', -4), ('u3', 3),),
-    (('o', 2), ('o', -4), ('d2', 2), ('d2', -4),),
-    (('d2', 3),),
-    (('u2', 3),),
-)
-BACKWARD_END = (('o', 3),)
+BACKWARD_END = (('d2', 3), ('u3', 3), ('d3', 3),)
 CLOSING_PLANS = (
     ((0, -1), (1, -1), (2, -1),),
     (),

time: 371 us -> 364 us (0.981)
  Pallas kernels: 358 us -> 351 us
    pallas_call x1, Pallas kernels: 119 us -> 111 us  [attention(): pl.pallas_call(functools.partial(attention_body, zs, pairs), grid=(row0 +...]
    pallas_call x1, Pallas kernels: 62.3 us -> 66.7 us  [closing(): pl.pallas_call(functools.partial(closing_body, zs), in_specs=[WHOLE_VMEM]...]
where the time goes in v6:
time: 364 us
  Pallas kernels  351 us (96%)
  local copies, waits for them, and re-layouts  6.99 us (2%)
  other arithmetic  4.79 us (1%)
    pallas_call x1, Pallas kernels, attention(): pl.pallas_call(functools.partial(attention_body, zs, pairs), grid=(row0 +...  111 us
    pallas_call x1, Pallas kernels, feed(): pl.pallas_call(functools.partial(feed_body, zs), grid=(8,), in_specs=[ful...  88.6 us
    pallas_call x1, Pallas kernels, backward(): pl.pallas_call(functools.partial(backward_body, zs, row_steps), grid=(row...  84.5 us
    pallas_call x1, Pallas kernels, closing(): pl.pallas_call(functools.partial(closing_body, zs), in_specs=[WHOLE_VMEM]...  66.7 us

profile of v6, /device:TPU:0, one launch (start us, length us, event | category | flops | bytes accessed | tf_op | source)
XLA Modules:
  0.0 363.7 jit_solution(6744003491493216929)
XLA Ops:
  0.6 111.4 %attention.1 = (bf16[1024,1024]{1,0:T(8,128)(2,1)}, bf16[1024,1024]{1,0:T(8,128)(2,1)}, bf16[1024,1024]{1,0:T(8,128)(2,1)}, bf16[1024,1024]{1,0:T(8,128)(2,1)}, ...) custom-call(bf16[2,64]{1,0:T(2,128)(2,1)} %qk_gains.1, ...), custom_call_target="tpu_custom_call" | custom-call | tf_op jit(solution)/shard_map/attention/pallas_call | solution.py:940
  112.0 0.0 copy-start.5
  112.0 88.6 %feed.1 = (bf16[1024,1024]{1,0:T(8,128)(2,1)}, f32[1024,1024]{1,0:T(8,128)}, bf16[2,2,4,2,2,64,512]{6,5,4,3,2,1,0:T(8,128)(2,1)}, bf16[2,2,4,2,2,64,512]{6,5,4,3...) custom-call(bf16[1024,1024]{1,0:T(8,128)(2,1)} %get-tuple-element.50, ...), custom_call_target="tpu_custom_call", output_to_operand_aliasing={{9}: (3, {}), {10}: (4, {})} | custom-call | tf_op jit(solution)/shard_map/feed/pallas_call | solution.py:1066
  200.6 0.0 copy-done.5
  200.7 0.6 tile.10.gains
  201.3 84.5 %backward.1 = (f32[1024,1024]{1,0:T(8,128)}, bf16[1024,1024]{1,0:T(8,128)(2,1)}, bf16[1024,1024]{1,0:T(8,128)(2,1)}, bf16[1024,1024]{1,0:T(8,128)(2,1)}, f32[2,1...) custom-call(f32[8,1024]{1,0:T(8,128)} %get-tuple-element.48.norms, ...), custom_call_target="tpu_custom_call", output_to_operand_aliasing={{9}: (21, {})} | custom-call | tf_op jit(solution)/shard_map/backward/pallas_call | solution.py:1240
  285.9 66.7 %closing.1 = (f32[3,64,512]{2,1,0:T(8,128)}, f32[8,1024]{1,0:T(8,128)}, bf16[2,512,1024]{2,1,0:T(8,128)(2,1)}) custom-call(f32[8,1024]{1,0:T(8,128)} %get-tuple-element.48.norms, f32[2,1024]{1,0:T(2,128)} %get-tuple-element.72.sums_second, f32[2,128]{1,0:T(2,128)} %get-tuple-element.73.sums_qk, bf16[1024,1024]{1,0:T(8,128)(2,1)} %get-tuple-element.74.image_in, ...), custom_call_target="tpu_custom_call" | custom-call | tf_op jit(solution)/shard_map/closing/pallas_call | solution.py:1362
  352.5 0.8 constant_dynamic-slice_fusion
  353.3 0.6 pad_maximum_fusion
  353.9 0.0 copy-start
  353.9 4.2 %convert_element_type.7 = f32[2,512,1024]{2,1,0:T(8,128)} convert(bf16[2,512,1024]{2,1,0:T(8,128)(2,1)} %get-tuple-element.81) | non-fusion elementwise | flops 1048576 | bytes 6291456 | tf_op jit(solution)/shard_map/convert_element_type | solution.py:1395
  358.1 1.2 slice.19
  359.3 0.0 copy-done
  359.3 0.0 copy-start.3
  359.3 0.0 copy-start.4
  359.3 0.0 copy-start.2
  359.3 1.3 copy.29
  360.7 0.0 copy-done.3
  360.7 0.0 copy-start.1
  360.7 0.7 copy.30
  361.4 0.0 copy-done.4
  361.4 0.7 copy.31
  362.1 0.0 copy-done.2
  362.1 0.8 copy.32
  362.9 0.0 copy-done.1
  362.9 0.8 copy.33
  (2 shorter events, 0.0 us)
Async XLA Ops:
  112.0 88.6 %copy-start.5 = (bf16[2,64]{1,0:T(2,128)(2,1)S(1)}, bf16[2,64]{1,0:T(2,128)(2,1)}, u32[]{:S(2)}) copy-start(bf16[2,64]{1,0:T(2,128)(2,1)} %qk_gains.1) | copy-start | bytes 772
  353.9 5.5 %copy-start = (bf16[2,512,1024]{2,1,0:T(8,128)(2,1)S(1)}, bf16[2,512,1024]{2,1,0:T(8,128)(2,1)}, u32[]{:S(2)}) copy-start(bf16[2,512,1024]{2,1,0:T(8,128)(2,1)} %get-tuple-element.102) | copy-start | bytes 6291460
  359.3 1.3 copy-start.3
  359.3 2.1 copy-start.4
  359.3 2.7 copy-start.2
  360.7 2.2 copy-start.1

commit v7 on v6

--- a/solution.py
+++ b/solution.py
@@ -637,9 +637,9 @@
 FEED_SINCE = (3, 1, 0)
 FEED_ORDERS = ('zyx', 'xyz', 'yzx', 'xyz')
 FEED_DONE = (2, 2)
-LATE_ORDERS = ('xzy', 'xyz', 'yxz', 'yxz')
-O_BACK_ORDER = 'zxy'
-CLOSING = ((0, 0, 256, 'zyx'), (0, 256, 256, 'yxz'), (0, 512, 256, 'xyz'), (1, 0, 256, 'yxz'), (1, 256, 256, 'zyx'), (1, 512, 256, 'yxz'))
+LATE_ORDERS = ('zyx', 'yxz', 'xyz', 'xyz')
+O_BACK_ORDER = 'yzx'
+CLOSING = ((0, 0, 256, 'zyx'), (0, 256, 256, 'xyz'), (0, 512, 256, 'yxz'), (1, 0, 256, 'yxz'), (1, 256, 256, 'yxz'), (1, 512, 256, 'zyx'))
 ATTENTION_LEAVES = (('U1', 3), ('D1', 3), ('U2', 1), ('D2', 1), ('U3', 0), ('D3', 0))
 OPENING_PLANS = (
     ((6, -1), ('T', -1), (0, -1), (2, -1), ('D2', -1), (6, 0), (1, -1), ('D2', 0), (1, 0), (3, -1), (0, 0), (6, -2), (0, -2), (2, 0), (1, -2), ('T', 0), ('T', -2), (3, 0), (2, -2), (0, 1), (6, 1), (6, -3), (3, -2), (2, 1), (0, -3), (2, -3), (1, 1), (4, -1), ('T', 1), ('T', -3), (6, 2), (6, -4), (1, -3), (6, 3),),
@@ -697,23 +697,23 @@
     (),
     (('u0', 2), ('u0', -4), ('d1', -3), ('R', 0), ('R', -2), ('d0', 2), ('d0', -4),),
     (('u1', 2),),
-    (('u0', 3), ('u1', -4), ('u2', 0), ('o', -1), ('d2', 0), ('u3', 0), ('u3', -2), ('d3', 0), ('d1', 2), ('d1', -4), ('d3', -2), ('d0', 3), ('R', 1), ('u2', -2),),
-    (('u1', 3), ('d2', -2), ('o', 0), ('o', -2),),
+    (('u0', 3), ('u1', -4), ('u2', 0), ('u2', -2), ('o', -1), ('d2', 0), ('d2', -2), ('u3', 0), ('d3', 0), ('d1', 2), ('d1', -4), ('d0', 3), ('R', 1), ('u3', -2),),
+    (('u1', 3), ('d3', -2), ('o', 0), ('o', -2),),
+    (),
+    (),
     (('d1', 3),),
-    (),
-    (),
-    (),
-    (('u2', 1), ('u2', -3), ('R', -3),),
-    (('u3', 1), ('d3', 1), ('d2', 1), ('d2', -3), ('u3', -3),),
-    (),
-    (('R', 2), ('d3', -3),),
-    (('d2', 2), ('d2', -4), ('o', 1), ('u3', 2), ('o', -3), ('u3', -4),),
-    (),
-    (('d3', 2), ('R', -4), ('u2', 2), ('u2', -4), ('d3', -4), ('o', 2), ('o', -4),),
-    (),
-    (('u2', 3), ('o', 3), ('R', 3),),
+    (('d2', 1),),
+    (('u3', 1), ('d2', -3), ('u3', -3),),
+    (('o', 1), ('o', -3), ('d3', 1), ('d3', -3), ('R', -3),),
+    (('u2', 1),),
+    (('u3', 2), ('u2', -3), ('u3', -4), ('d2', 2), ('d2', -4),),
+    (('d3', 2), ('R', 2), ('R', -4),),
+    (('u2', 2), ('u2', -4),),
+    (),
+    (('o', 2), ('d3', -4), ('u2', 3), ('o', -4), ('R', 3),),
+    (('u3', 3), ('d2', 3), ('o', 3),),
 )
-BACKWARD_END = (('d2', 3), ('u3', 3), ('d3', 3),)
+BACKWARD_END = (('d3', 3),)
 CLOSING_PLANS = (
     ((0, -1), (1, -1), (2, -1),),
     (),
@@ -721,7 +721,7 @@
     ((3, -1), (0, 0), (0, -2), (4, -1), (1, 0), (1, -2), (5, -1), (2, 0), (2, -2),),
     (('G', 0), ('G', -2),),
 )
-CLOSING_END = (('S', -1), (3, 0), (3, -2), (4, 0), (4, -2), (5, 0), (1, 1), (5, -2), ('S', 0), (2, 1), ('S', -2), ('S', 1), (1, -3), ('G', 1), ('G', -3), (0, 1), (3, 1), ('S', -3), (5, 1), (0, -3), (1, 2), (1, -4), (3, -3), ('S', 2), ('S', -4), (2, -3), (0, 2), (4, 1), (4, -3), ('G', 2), (0, -4), (3, 2), (3, -4), (5, -3), (2, 2), (1, 3), (2, -4), (0, 3), ('G', -4), (4, 2), ('S', 3), (5, 2), (4, -4), (5, -4), (3, 3), (2, 3), (4, 3), (5, 3), ('G', 3),)
+CLOSING_END = (('S', -1), (3, 0), (3, -2), (4, 0), (5, 0), (5, -2), (2, 1), (4, -2), ('S', 0), (1, 1), ('S', -2), ('S', 1), (2, -3), ('G', 1), ('G', -3), (0, 1), (3, 1), ('S', -3), (4, 1), (0, -3), (2, 2), (2, -4), (3, -3), ('S', 2), ('S', -4), (1, -3), (0, 2), (5, 1), (5, -3), ('G', 2), (0, -4), (3, 2), (3, -4), (4, -3), (1, 2), (2, 3), (1, -4), (0, 3), ('G', -4), (5, 2), ('S', 3), (4, 2), (4, -4), (5, -4), (3, 3), (1, 3), (5, 3), (4, 3), ('G', 3),)
 
 
 Q_TILE = 256

time: 364 us -> 372 us (1.022)
  Pallas kernels: 351 us -> 359 us
    pallas_call x1, Pallas kernels: 84.5 us -> 97.9 us  [backward(): pl.pallas_call(functools.partial(backward_body, zs, row_steps), grid=(row...]
    pallas_call x1, Pallas kernels: 66.7 us -> 61.6 us  [closing(): pl.pallas_call(functools.partial(closing_body, zs), in_specs=[WHOLE_VMEM]...]
where the time goes in v7:
time: 372 us
  Pallas kernels  359 us (97%)
  local copies, waits for them, and re-layouts  6.99 us (2%)
  other arithmetic  4.79 us (1%)
    pallas_call x1, Pallas kernels, attention(): pl.pallas_call(functools.partial(attention_body, zs, pairs), grid=(row0 +...  111 us
    pallas_call x1, Pallas kernels, backward(): pl.pallas_call(functools.partial(backward_body, zs, row_steps), grid=(row...  97.9 us
    pallas_call x1, Pallas kernels, feed(): pl.pallas_call(functools.partial(feed_body, zs), grid=(8,), in_specs=[ful...  88.6 us
    pallas_call x1, Pallas kernels, closing(): pl.pallas_call(functools.partial(closing_body, zs), in_specs=[WHOLE_VMEM]...  61.6 us

profile of v7, /device:TPU:0, one launch (start us, length us, event | category | flops | bytes accessed | tf_op | source)
XLA Modules:
  0.0 372.0 jit_solution(6784874283819404848)
XLA Ops:
  0.6 111.4 %attention.1 = (bf16[1024,1024]{1,0:T(8,128)(2,1)}, bf16[1024,1024]{1,0:T(8,128)(2,1)}, bf16[1024,1024]{1,0:T(8,128)(2,1)}, bf16[1024,1024]{1,0:T(8,128)(2,1)}, ...) custom-call(bf16[2,64]{1,0:T(2,128)(2,1)} %qk_gains.1, ...), custom_call_target="tpu_custom_call" | custom-call | tf_op jit(solution)/shard_map/attention/pallas_call | solution.py:940
  112.0 0.0 copy-start.5
  112.0 88.6 %feed.1 = (bf16[1024,1024]{1,0:T(8,128)(2,1)}, f32[1024,1024]{1,0:T(8,128)}, bf16[2,2,4,2,2,64,512]{6,5,4,3,2,1,0:T(8,128)(2,1)}, bf16[2,2,4,2,2,64,512]{6,5,4,3...) custom-call(bf16[1024,1024]{1,0:T(8,128)(2,1)} %get-tuple-element.50, ...), custom_call_target="tpu_custom_call", output_to_operand_aliasing={{9}: (3, {}), {10}: (4, {})} | custom-call | tf_op jit(solution)/shard_map/feed/pallas_call | solution.py:1066
  200.6 0.0 copy-done.5
  200.7 0.6 tile.10.gains
  201.3 97.9 %backward.1 = (f32[1024,1024]{1,0:T(8,128)}, bf16[1024,1024]{1,0:T(8,128)(2,1)}, bf16[1024,1024]{1,0:T(8,128)(2,1)}, bf16[1024,1024]{1,0:T(8,128)(2,1)}, f32[2,1...) custom-call(f32[8,1024]{1,0:T(8,128)} %get-tuple-element.48.norms, ...), custom_call_target="tpu_custom_call", output_to_operand_aliasing={{9}: (21, {})} | custom-call | tf_op jit(solution)/shard_map/backward/pallas_call | solution.py:1240
  299.2 61.6 %closing.1 = (f32[3,64,512]{2,1,0:T(8,128)}, f32[8,1024]{1,0:T(8,128)}, bf16[2,512,1024]{2,1,0:T(8,128)(2,1)}) custom-call(f32[8,1024]{1,0:T(8,128)} %get-tuple-element.48.norms, f32[2,1024]{1,0:T(2,128)} %get-tuple-element.72.sums_second, f32[2,128]{1,0:T(2,128)} %get-tuple-element.73.sums_qk, bf16[1024,1024]{1,0:T(8,128)(2,1)} %get-tuple-element.74.image_in, ...), custom_call_target="tpu_custom_call" | custom-call | tf_op jit(solution)/shard_map/closing/pallas_call | solution.py:1362
  360.8 0.8 constant_dynamic-slice_fusion
  361.6 0.6 pad_maximum_fusion
  362.2 0.0 copy-start
  362.2 4.2 %convert_element_type.7 = f32[2,512,1024]{2,1,0:T(8,128)} convert(bf16[2,512,1024]{2,1,0:T(8,128)(2,1)} %get-tuple-element.81) | non-fusion elementwise | flops 1048576 | bytes 6291456 | tf_op jit(solution)/shard_map/convert_element_type | solution.py:1395
  366.4 1.2 slice.19
  367.6 0.0 copy-done
  367.6 0.0 copy-start.3
  367.7 0.0 copy-start.4
  367.7 0.0 copy-start.2
  367.7 1.3 copy.29
  369.0 0.0 copy-done.3
  369.0 0.0 copy-start.1
  369.0 0.7 copy.30
  369.7 0.0 copy-done.4
  369.7 0.7 copy.31
  370.4 0.0 copy-done.2
  370.4 0.8 copy.32
  371.2 0.0 copy-done.1
  371.2 0.8 copy.33
  (2 shorter events, 0.0 us)
Async XLA Ops:
  112.0 88.6 %copy-start.5 = (bf16[2,64]{1,0:T(2,128)(2,1)S(1)}, bf16[2,64]{1,0:T(2,128)(2,1)}, u32[]{:S(2)}) copy-start(bf16[2,64]{1,0:T(2,128)(2,1)} %qk_gains.1) | copy-start | bytes 772
  362.2 5.5 %copy-start = (bf16[2,512,1024]{2,1,0:T(8,128)(2,1)S(1)}, bf16[2,512,1024]{2,1,0:T(8,128)(2,1)}, u32[]{:S(2)}) copy-start(bf16[2,512,1024]{2,1,0:T(8,128)(2,1)} %get-tuple-element.102) | copy-start | bytes 6291460
  367.6 1.3 copy-start.3
  367.7 2.1 copy-start.4
  367.7 2.7 copy-start.2
  369.0 2.2 copy-start.1
